TPU v7x, 32 devices: a whole 2x2x4 slice. The times are simulated.
32 devices in a mesh: fsdp: 2 (over x), ctx: 4 (over z), tp: 4 (over y, core).
Axes of the slice: x: 2, y: 2, z: 4, core: 2. Of those that a mesh axis runs over, the one named last changes fastest.
Arguments:
- layer_input: bfloat16 [4, 1024, 2048], P('fsdp', 'ctx'), may hold values from -6 to 6
- cotangent: bfloat16 [4, 1024, 2048], P('fsdp', 'ctx'), may hold values from -6 to 6
- lengths: int32 [4], P('fsdp'), may hold values from 256 to 1024, as said below
- w_query: bfloat16 [2048, 2048], P('fsdp', 'tp'), may hold values from -0.125 to 0.125
- w_key: bfloat16 [2048, 2048], P('fsdp', 'tp'), may hold values from -0.125 to 0.125
- w_value: bfloat16 [2048, 2048], P('fsdp', 'tp'), may hold values from -0.125 to 0.125
- w_attn_out: bfloat16 [2048, 2048], P('tp', 'fsdp'), may hold values from -0.5 to 0.5
- w_gate: bfloat16 [2048, 8192], P('fsdp', 'tp'), may hold values from -0.125 to 0.125
- w_up: bfloat16 [2048, 8192], P('fsdp', 'tp'), may hold values from -0.125 to 0.125
- w_down: bfloat16 [8192, 2048], P('tp', 'fsdp'), may hold values from -0.0625 to 0.0625
Outputs:
- out_block: bfloat16 [4, 1024, 2048], P('fsdp', 'ctx')
- grad_input: float32 [4, 1024, 2048], P('fsdp', 'ctx')
- grad_query: float32 [2048, 2048], P('fsdp', 'tp')
- grad_key: float32 [2048, 2048], P('fsdp', 'tp')
- grad_value: float32 [2048, 2048], P('fsdp', 'tp')
- grad_attn_out: float32 [2048, 2048], P('tp', 'fsdp')
- grad_gate: float32 [2048, 8192], P('fsdp', 'tp')
- grad_up: float32 [2048, 8192], P('fsdp', 'tp')
- grad_down: float32 [8192, 2048], P('tp', 'fsdp')
Inputs may be any that keep to these rules, and one draw needn't show every extreme that they name: Each sequence's used slots are its first lengths[s]; some sequence is full in every draw.
All inputs are finite; a program needn't handle non-finite values.
Results may differ from a plain program's by a relative error of at most 0.015.
Values may be sent and summed in bfloat16 or wider, within the bound.
No kernel may reach another device: no remote copies, remote signals or barrier semaphores. Data moves between devices by JAX's collectives and lax.ppermute only.
A program may use at most 256 MiB of HBM per device.

v0:
```python
import jax
import jax.numpy as jnp
from jax import lax
from jax.experimental import pallas as pl
from jax.experimental.pallas import tpu as pltpu
from jax.sharding import PartitionSpec as P

HD = 128
BF = jnp.bfloat16
F32 = jnp.float32


def layer_norm(v):
    centered = v - jnp.mean(v, axis=-1, keepdims=True)
    rstd = lax.rsqrt(jnp.mean(centered * centered, axis=-1, keepdims=True) + 1e-05)
    return (centered * rstd, rstd)


def norm_back(grad, normed, rstd):
    return rstd * (
        grad
        - jnp.mean(grad, axis=-1, keepdims=True)
        - normed * jnp.mean(grad * normed, axis=-1, keepdims=True)
    )


def dot(left, right):
    return jnp.dot(left, right, preferred_element_type=F32)


def tdot(left, right):
    return lax.dot_general(left, right, (((0,), (0,)), ((), ())), preferred_element_type=F32)


def ndot(left, right):
    return lax.dot_general(left, right, (((1,), (1,)), ((), ())), preferred_element_type=F32)


def after(v, *others):
    return lax.optimization_barrier((v,) + others)[0]


def mm(left, right, dims):
    return lax.dot_general(left, right, (dims, ((), ())), preferred_element_type=F32)


def block_probs(q, k, length, first):
    span = (q.shape[0], k.shape[0])
    scores = mm(q, k, ((1,), (1,))) * (1.0 / HD**0.5)
    query = first + lax.broadcasted_iota(jnp.int32, span, 0)
    key = lax.broadcasted_iota(jnp.int32, span, 1)
    visible = (key <= query) & (key < length)
    masked = jnp.where(visible, scores, -1e30)
    top = jnp.max(masked, axis=-1, keepdims=True)
    expo = jnp.where(visible, jnp.exp(masked - top), 0.0)
    return expo / jnp.sum(expo, axis=-1, keepdims=True)


def forward_body(block, lens, qraw, kraw, v, cosine, sine, qr, kr, ctx):
    length = lens[pl.program_id(0)]
    for raw, out in ((qraw, qr), (kraw, kr)):
        x = raw[...]
        out[...] = (x * cosine[...] + pltpu.roll(x, HD // 2, 1) * sine[...]).astype(BF)
    for first in range(0, qr.shape[0], block):
        last = first + block
        probs = block_probs(qr[first:last, :], kr[:last, :], length, first).astype(BF)
        ctx[first:last, :] = mm(probs, v[:last, :], ((1,), (0,))).astype(BF)


def backward_body(block, lens, qr, kr, v, dctx, cosine, sine, dq, dk, dv, dk_sum, dv_sum):
    length = lens[pl.program_id(0)]
    factor = 1.0 / HD**0.5
    dk_sum[...] = jnp.zeros_like(dk_sum)
    dv_sum[...] = jnp.zeros_like(dv_sum)

    def unturn(x, c, s):
        return (x * c - pltpu.roll(x, HD // 2, 1) * s).astype(BF)

    for first in range(0, qr.shape[0], block):
        last = first + block
        q = qr[first:last, :]
        dc = dctx[first:last, :]
        k = kr[:last, :]
        probs = block_probs(q, k, length, first)
        dprobs = mm(dc, v[:last, :], ((1,), (1,)))
        delta = jnp.sum(probs * dprobs, axis=-1, keepdims=True)
        dscores = (probs * (dprobs - delta)).astype(BF)
        dq[first:last, :] = unturn(
            mm(dscores, k, ((1,), (0,))) * factor, cosine[first:last, :], sine[first:last, :]
        )
        dk_sum[:last, :] += mm(dscores, q, ((0,), (0,)))
        dv_sum[:last, :] += mm(probs.astype(BF), dc, ((0,), (0,)))
    dk[...] = unturn(dk_sum[...] * factor, cosine[...], sine[...])
    dv[...] = dv_sum[...].astype(BF)


def attention_call(body, lengths, arrays, tables, outs, scratch):
    rows, width = arrays[0].shape
    nseq = lengths.shape[0]
    whole = rows // nseq
    tile = pl.BlockSpec((whole, HD), lambda s, h, lens: (s, h))
    table = pl.BlockSpec((whole, HD), lambda s, h, lens: (0, 0))
    block = whole // 4
    return pl.pallas_call(
        lambda *refs: body(block, *refs),
        grid_spec=pltpu.PrefetchScalarGridSpec(
            num_scalar_prefetch=1,
            grid=(nseq, width // HD),
            in_specs=[tile] * len(arrays) + [table] * len(tables),
            out_specs=[tile] * outs,
            scratch_shapes=[pltpu.VMEM((whole, HD), F32)] * scratch,
        ),
        out_shape=[jax.ShapeDtypeStruct((rows, width), BF)] * outs,
    )(lengths, *arrays, *tables)


def swap_fsdp(v):
    return lax.ppermute(v, "fsdp", [(0, 1), (1, 0)])


def tp_swap(v, bit):
    n = lax.axis_size("tp")
    return lax.ppermute(v, "tp", [(i, i ^ bit) for i in range(n)])


def tp_half(make, *parts):
    n = lax.axis_size("tp")
    mid = parts[0].shape[0] // 2
    got = tp_swap(make(*(p[mid:] for p in parts)).astype(BF), 1)
    total = make(*(p[:mid] for p in parts)) + got.astype(F32)
    bit = 2
    while bit < n:
        sent = total.astype(BF)
        total = sent.astype(F32) + tp_swap(sent, bit).astype(F32)
        bit *= 2
    return total.astype(BF)


def tp_join(kept):
    return jnp.concatenate([kept, tp_swap(kept, 1)], axis=0).astype(F32)


class LineGather:
    def __init__(self, piece):
        self.piece = piece
        self.me = lax.axis_index("ctx")
        self.up1 = lax.ppermute(piece, "ctx", [(0, 1), (1, 2), (2, 3)])
        self.down1 = lax.ppermute(piece, "ctx", [(1, 0), (2, 1), (3, 2)])
        self.up2 = lax.ppermute(piece, "ctx", [(0, 2), (1, 3)])
        self.down2 = lax.ppermute(piece, "ctx", [(2, 0), (3, 1)])

    def finish(self, store, *held):
        me = self.me
        relay = jnp.where(me == 2, self.up2, self.down2)
        if held:
            relay = after(relay, *held)
        far = lax.ppermute(relay, "ctx", [(2, 3), (1, 0)])
        store(me, self.piece)
        store((me - 1) % 4, jnp.where(me >= 1, self.up1, far))
        store((me - 2) % 4, jnp.where(me >= 2, self.up2, self.down2))
        store((me - 3) % 4, jnp.where(me == 3, far, self.down1))


class Box:
    def __init__(self, shape, dtype):
        self.v = jnp.zeros(shape, dtype)

    def put(self, piece, *at):
        at = [jnp.asarray(a, jnp.int32) for a in at]
        at += [jnp.int32(0)] * (self.v.ndim - len(at))
        self.v = lax.dynamic_update_slice(self.v, piece.astype(self.v.dtype), at)


def quarter(w):
    part = w.shape[0] // lax.axis_size("ctx")
    return lax.dynamic_slice_in_dim(w, lax.axis_index("ctx") * part, part, 0)


class Rows:
    def __init__(self, piece):
        self.gather = LineGather(piece)
        self.line = Box((4,) + piece.shape, piece.dtype)

    def finish(self):
        half = (lax.axis_index("tp") >> 1) & 1
        self.gather.finish(lambda which, got: self.line.put(got[None], which))
        line = self.line.v
        other = tp_swap(line, 2)
        pair = Box((4, 2) + line.shape[1:], line.dtype)
        pair.put(line[:, None], 0, half)
        pair.put(other[:, None], 0, 1 - half)
        mine = pair.v.reshape(-1, line.shape[-1])
        return jnp.concatenate([mine, tp_swap(mine, 1)], axis=0)


class Stream:
    def __init__(self):
        self.chunks, self.done, self.tick = [], [], 0
        self.stage1, self.stage2, self.stage3 = {}, {}, {}

    def step(self, *extra):
        t, place = self.tick, lax.axis_index("ctx")
        send = {}
        if t < len(self.chunks):
            send["x"] = self.chunks[t][1]
        for name, held, lag in (("a", self.stage1, 1), ("b", self.stage2, 2), ("c", self.stage3, 3)):
            if t - lag in held:
                send[name] = held[t - lag]
        send, extra = lax.optimization_barrier((send, extra))
        if "c" in send:
            back = lax.ppermute(send["c"], "ctx", [(1, 0), (2, 3)])
            self.done.append(jnp.where((place == 0) | (place == 3), back, send["c"]))
        if "b" in send:
            got = lax.ppermute(send["b"], "ctx", [(1, 2), (2, 1)])
            self.stage3[t - 2] = (send["b"].astype(F32) + got.astype(F32)).astype(BF)
        if "a" in send:
            got = lax.ppermute(send["a"], "ctx", [(0, 1), (3, 2)])
            self.stage2[t - 1] = (send["a"].astype(F32) + got.astype(F32)).astype(BF)
        if "x" in send:
            got = swap_fsdp(send["x"])
            self.stage1[t] = (self.chunks[t][0] + got.astype(F32)).astype(BF)
        self.tick += 1
        return extra


def per_device(
    layer_input, cotangent, lengths, w_query, w_key, w_value, w_attn_out, w_gate, w_up, w_down
):
    nseq, local, width = layer_input.shape
    dh = width // 2
    rows = nseq * local
    whole = local * lax.axis_size("ctx")
    pair = lax.axis_index("fsdp")
    me = lax.axis_index("ctx")
    t = lax.axis_index("tp")
    core = t & 1
    fourth = rows // 4
    at_fourth = ((t >> 1) & 1) * fourth
    places = me * local + jnp.arange(local, dtype=jnp.int32)
    freqs = 10000.0 ** (-(jnp.arange(HD // 2, dtype=F32) * 2.0) / HD)
    angles = jnp.arange(whole, dtype=F32)[:, None] * freqs[None, :]
    cosine = jnp.cos(angles)
    sine = jnp.sin(angles)
    tables = (
        jnp.concatenate([cosine, cosine], axis=-1),
        jnp.concatenate([-sine, sine], axis=-1),
    )
    lens = jnp.stack(
        [lax.dynamic_index_in_dim(lengths, core, 0, False), lax.dynamic_index_in_dim(lengths, 1 - core, 0, False)]
    )

    def block_of(v, seq, start, size):
        return jnp.concatenate(
            [
                lax.dynamic_slice(v, (seq, start, side * dh), (1, size, dh))
                for side in (pair, 1 - pair)
            ],
            axis=-1,
        )[0]

    def arranged(v):
        return jnp.concatenate([block_of(v, s, 0, local) for s in (core, 1 - core)], axis=0)

    def restored(v, dtype):
        box = Box((nseq, local, width), dtype)
        for i, seq in enumerate((core, 1 - core)):
            for j, side in enumerate((pair, 1 - pair)):
                part = v[i * local : (i + 1) * local, j * dh : (j + 1) * dh]
                box.put(part[None], seq, 0, side * dh)
        return box.v

    u1_rows = Rows(
        layer_norm(block_of(layer_input, core, at_fourth, fourth).astype(F32))[0].astype(BF)
    )
    gate_part = swap_fsdp(quarter(w_gate))
    key_other = swap_fsdp(w_key)
    value_other = swap_fsdp(w_value)
    query_other = swap_fsdp(w_query)
    up_part = swap_fsdp(quarter(w_up))
    out_other = swap_fsdp(w_attn_out)
    hf = w_down.shape[0] // 2
    down_part = swap_fsdp(quarter(w_down[hf:]))
    down_other = swap_fsdp(w_down[:hf])

    gate_line = LineGather(gate_part)
    u1 = u1_rows.finish()
    full_q = jnp.concatenate([w_query, query_other], axis=0)
    full_k = jnp.concatenate([w_key, key_other], axis=0)
    full_v = jnp.concatenate([w_value, value_other], axis=0)
    full_o = jnp.concatenate([w_attn_out, out_other], axis=1)
    up_line = LineGather(after(up_part, u1))
    qraw = dot(u1, full_q)
    kraw = dot(u1, full_k)
    values = dot(u1, full_v).astype(BF)
    full_g, full_u = Box((width, w_gate.shape[1]), BF), Box((width, w_up.shape[1]), BF)
    part = dh // 4
    full_g.put(w_gate, 0)
    gate_line.finish(lambda which, got: full_g.put(got, dh + which * part), qraw, kraw, values)
    down_line = LineGather(after(down_part, qraw, kraw, values))
    qr, kr, context = attention_call(forward_body, lens, (qraw, kraw, values), tables, 3, 0)

    def my_rows(v):
        picked = lax.dynamic_slice_in_dim(v.reshape(nseq, whole, -1), me * local, local, 1)
        return picked.reshape(rows, -1)

    keep = jnp.concatenate([(places < lens[i]).astype(F32) for i in range(nseq)]).reshape(rows, 1)
    dy = arranged(cotangent).astype(F32) * keep
    dy_low = dy.astype(BF)
    xf = arranged(layer_input).astype(F32)
    attn_half = tp_half(lambda u: dot(u, full_o), my_rows(context))
    full_u.put(w_up, 0)
    up_line.finish(lambda which, got: full_u.put(got, dh + which * part), attn_half)
    full_d = Box((w_down.shape[0], width), BF)
    full_d.put(w_down, 0)
    full_d.put(down_other, 0, dh)
    down_line.finish(
        lambda which, got: full_d.put(got, hf + which * (hf // 4), dh), attn_half
    )
    h1 = xf + tp_join(attn_half)
    n2, rstd2 = layer_norm(h1)
    u2 = n2.astype(BF)
    gate = dot(u2, full_g.v)
    upper = dot(u2, full_u.v)
    sigma = jax.nn.sigmoid(gate)
    hidden = (gate * sigma * upper).astype(BF)

    def grads_into(u, g, parts):
        step = dh // parts
        return [
            (
                tdot(u[:, j * step : (j + 1) * step], g),
                tdot(u[:, dh + j * step : dh + (j + 1) * step], g).astype(BF),
            )
            for j in range(parts)
        ]

    def grads_out(u, g, parts):
        step = u.shape[1] // parts
        return [
            (
                tdot(u[:, j * step : (j + 1) * step], g[:, :dh]),
                tdot(u[:, j * step : (j + 1) * step], g[:, dh:]).astype(BF),
            )
            for j in range(parts)
        ]

    even, uneven = Stream(), Stream()

    def enqueue(chunks):
        even.chunks += chunks[0::2]
        uneven.chunks += chunks[1::2]

    enqueue(grads_out(hidden, dy_low, 4))
    (dy_next,) = even.step(dy_low)
    (dy_next,) = uneven.step(dy_next)
    dhidden = ndot(dy_next, full_d.v)
    dgate = (dhidden * upper * sigma * (1.0 + gate * (1.0 - sigma))).astype(BF)
    dupper = (dhidden * gate * sigma).astype(BF)
    enqueue(grads_into(u2, dgate, 4))
    enqueue(grads_into(u2, dupper, 4))
    du2_half = tp_half(
        lambda dg, du: ndot(dg, full_g.v) + ndot(du, full_u.v), dgate, dupper
    )
    even.step()
    uneven.step()

    def fourth_at(v):
        return lax.dynamic_slice_in_dim(v, at_fourth, fourth, 0)

    da_part = fourth_at(dy) + norm_back(
        fourth_at(du2_half).astype(F32), fourth_at(n2), fourth_at(rstd2)
    )
    (da_part,) = even.step(da_part.astype(BF))
    da_rows = Rows(da_part)
    uneven.step()
    even.step()
    uneven.step()
    da = da_rows.finish()
    (da,) = even.step(da)
    uneven.step()
    dcontext = ndot(da, full_o).astype(BF)
    dq, dk, dv = attention_call(backward_body, lens, (qr, kr, values, dcontext), tables, 3, 2)
    dq, dk, dv, hidden_late = even.step(dq, dk, dv, hidden)
    uneven.step()
    n1, rstd1 = layer_norm(xf)
    pairs = grads_out(context, da, 1) + [grads_into(u1, g, 1)[0] for g in (dv, dk, dq)]
    sent = even.step(*(p[1] for p in pairs))
    g_attn, g_value, g_key, g_query = [
        p[0] + swap_fsdp(s).astype(F32) for p, s in zip(pairs, sent)
    ]
    uneven.step()
    du1 = tp_join(
        tp_half(
            lambda q, k, v: ndot(q, full_q) + ndot(k, full_k) + ndot(v, full_v),
            my_rows(dq),
            my_rows(dk),
            my_rows(dv),
        )
    )
    h2 = h1 + tp_join(tp_half(lambda u: dot(u, full_d.v), hidden_late))
    even.step()
    uneven.step()
    even.step()
    uneven.step()
    dh1 = dy + norm_back(tp_join(du2_half), n2, rstd2)
    grad_input = restored(dh1 + norm_back(du1, n1, rstd1), F32)
    out_block = restored(h2 * keep, BF)
    totals = [None] * 12
    totals[0::2] = even.done
    totals[1::2] = uneven.done

    def lay(parts):
        box = Box((parts[0].shape[0] * len(parts), parts[0].shape[1]), F32)
        for j, p in enumerate(parts):
            box.put(p, j * p.shape[0])
        return box.v

    return (
        out_block,
        grad_input,
        g_query,
        g_key,
        g_value,
        g_attn,
        lay(totals[4:8]),
        lay(totals[8:12]),
        lay(totals[0:4]),
    )


def solution(mesh):
    return jax.shard_map(
        per_device,
        mesh=mesh,
        in_specs=(
            P("fsdp", "ctx", None),
            P("fsdp", "ctx", None),
            P("fsdp"),
            P("fsdp", "tp"),
            P("fsdp", "tp"),
            P("fsdp", "tp"),
            P("tp", "fsdp"),
            P("fsdp", "tp"),
            P("fsdp", "tp"),
            P("tp", "fsdp"),
        ),
        out_specs=(
            P("fsdp", "ctx", None),
            P("fsdp", "ctx", None),
            P("fsdp", "tp"),
            P("fsdp", "tp"),
            P("fsdp", "tp"),
            P("tp", "fsdp"),
            P("fsdp", "tp"),
            P("fsdp", "tp"),
            P("tp", "fsdp"),
        ),
        check_vma=False,
    )
```

profile of v0, /device:TPU:0, one launch (start us, length us, event | category | flops | bytes accessed | tf_op | source)
XLA Modules:
  0.0 1180.2 jit_solution(13093698343974785136)
XLA Ops:
  3.3 6.0 collective-permute-start.1
  14.9 7.0 collective-permute-done.1
  21.9 15.0 %collective-permute-done.2 = bf16[128,2048]{1,0:T(8,128)(2,1)S(1)} collective-permute-done((bf16[128,2048]{1,0:T(8,128)(2,1)}, bf16[128,2048]{1,0:T(8,128)(2,1)S(1)}, u32[]{:S(2)}, u32[]{:S(2)}) %collective-permute-start.2) | collective-permute-done | bytes 524320 | tf_op jit(solution)/shard_map/ppermute | solution.py:150
  41.1 13.7 %collective-permute-done.3 = bf16[128,2048]{1,0:T(8,128)(2,1)} collective-permute-done((bf16[128,2048]{1,0:T(8,128)(2,1)}, bf16[128,2048]{1,0:T(8,128)(2,1)}, u32[]{:S(2)}, u32[]{:S(2)}) %collective-permute-start.3) | collective-permute-done | bytes 524320 | tf_op jit(solution)/shard_map/ppermute | solution.py:157
  56.2 7.9 collective-permute-done.4
  88.3 22.9 %collective-permute-done.5 = bf16[4,128,2048]{2,1,0:T(8,128)(2,1)} collective-permute-done((bf16[4,128,2048]{2,1,0:T(8,128)(2,1)S(1)}, bf16[4,128,2048]{2,1,0:T(8,128)(2,1)}, u32[]{:S(2)}, u32[]{:S(2)}) %collective-permute-start.5) | collective-permute-done | bytes 2097184 | tf_op jit(solution)/shard_map/ppermute | solution.py:123
  127.3 10.8 collective-permute-done.20
  141.6 6.6 dynamic_update_slice.166
  148.3 6.9 dynamic_update_slice.161
  170.1 13.0 %collective-permute-done.7 = bf16[1024,512]{1,0:T(8,128)(2,1)} collective-permute-done((bf16[1024,512]{1,0:T(8,128)(2,1)}, bf16[1024,512]{1,0:T(8,128)(2,1)}, u32[]{:S(2)}, u32[]{:S(2)}) %collective-permute-start.7) | collective-permute-done | bytes 1048608 | tf_op jit(solution)/shard_map/ppermute | solution.py:118
  185.9 19.7 %collective-permute-done.10 = bf16[512,1024]{1,0:T(8,128)(2,1)} collective-permute-done((bf16[512,1024]{1,0:T(8,128)(2,1)}, bf16[512,1024]{1,0:T(8,128)(2,1)}, u32[]{:S(2)}, u32[]{:S(2)}) %collective-permute-start.10) | collective-permute-done | bytes 1048608 | tf_op jit(solution)/shard_map/ppermute | solution.py:118
  220.2 9.3 convolution_convert_fusion.1.refs_3_
  229.5 10.0 fusion.151.refs_2_
  239.5 10.1 fusion.152.refs_1_
  249.6 7.1 collective-permute-start.29
  256.6 22.5 %shard_map.169 = (bf16[2048,512]{1,0:T(8,128)(2,1)}, bf16[2048,512]{1,0:T(8,128)(2,1)}, bf16[2048,512]{1,0:T(8,128)(2,1)}) custom-call(s32[2]{0:T(128)} %pad_add_fusion.refs_0_, f32[2048,512]{1,0:T(8,128)} %fusion.152.refs_1_, f32[2048,512]{1,0:T(8,128)} %fusion.151.refs_2_, bf16[2048,512]{1,0:T(8,128)(2,1)} %convolution_convert_fusion.1.refs_3_, ...), custom_call_target="tpu_custom_call" | custom-call | tf_op jit(solution)/shard_map/pallas_call | solution.py:104
  290.8 10.0 collective-permute-start.21
  312.1 7.8 collective-permute-done.18
  323.2 20.9 %collective-permute-done.12 = bf16[256,2048]{1,0:T(8,128)(2,1)S(1)} collective-permute-done((bf16[256,2048]{1,0:T(8,128)(2,1)S(1)}, bf16[256,2048]{1,0:T(8,128)(2,1)S(1)}, u32[]{:S(2)}, u32[]{:S(2)}) %collective-permute-start.12) | collective-permute-done | bytes 1048608 | tf_op jit(solution)/shard_map/ppermute | solution.py:123
  344.5 19.8 %collective-permute-done.19 = bf16[256,2048]{1,0:T(8,128)(2,1)S(1)} collective-permute-done((bf16[256,2048]{1,0:T(8,128)(2,1)}, bf16[256,2048]{1,0:T(8,128)(2,1)S(1)}, u32[]{:S(2)}, u32[]{:S(2)}) %collective-permute-start.19) | collective-permute-done | bytes 1048608 | tf_op jit(solution)/shard_map/ppermute | solution.py:148
  368.4 12.6 %collective-permute-done.31 = bf16[256,1024]{1,0:T(8,128)(2,1)S(1)} collective-permute-done((bf16[256,1024]{1,0:T(8,128)(2,1)S(1)}, bf16[256,1024]{1,0:T(8,128)(2,1)S(1)}, u32[]{:S(2)}, u32[]{:S(2)}) %collective-permute-start.31) | collective-permute-done | bytes 524320 | tf_op jit(solution)/shard_map/ppermute | solution.py:157
  384.4 7.8 collective-permute-done.32
  397.4 16.0 %collective-permute-done.24 = bf16[256,2048]{1,0:T(8,128)(2,1)S(1)} collective-permute-done((bf16[256,2048]{1,0:T(8,128)(2,1)S(1)}, bf16[256,2048]{1,0:T(8,128)(2,1)S(1)}, u32[]{:S(2)}, u32[]{:S(2)}) %collective-permute-start.24) | collective-permute-done | bytes 1048608 | tf_op jit(solution)/shard_map/ppermute | solution.py:157
  419.0 6.1 fusion.157
  425.6 9.8 multiply_convert_fusion.3
  436.9 11.9 %multiply_convert_fusion.2 = (bf16[512,2048]{1,0:T(8,128)(2,1)S(1)}, bf16[512,2048]{1,0:T(8,128)(2,1)S(1)}) fusion(f32[512,2048]{1,0:T(8,128)} %fusion.157, f32[512,2048]{1,0:T(8,128)} %get-tuple-element.182, bf16[512,2048]{1,0:T(8,128)(2,1)} %get-tuple-element.83, bf16[2048,2048]{1,0:T(8,128)(2,1)} %select_dynamic-update-slice_fusion.6), kind=kOutput, calls=%fused_computation.38 | convolution fusion | flops 4308598784 | bytes 23068672 | tf_op jit(solution)/shard_map/dot_general | solution.py:36
  480.4 7.0 fusion.53
  487.4 6.6 fusion.28
  496.4 7.2 collective-permute-done.33
  506.5 19.7 %collective-permute-done.69 = bf16[512,1024]{1,0:T(8,128)(2,1)} collective-permute-done((bf16[512,1024]{1,0:T(8,128)(2,1)S(1)}, bf16[512,1024]{1,0:T(8,128)(2,1)}, u32[]{:S(2)}, u32[]{:S(2)}) %collective-permute-start.69) | collective-permute-done | bytes 1048608 | tf_op jit(solution)/shard_map/ppermute | solution.py:118
  531.2 17.3 %collective-permute-done.34 = bf16[512,1024]{1,0:T(8,128)(2,1)S(1)} collective-permute-done((bf16[512,1024]{1,0:T(8,128)(2,1)}, bf16[512,1024]{1,0:T(8,128)(2,1)S(1)}, u32[]{:S(2)}, u32[]{:S(2)}) %collective-permute-start.34) | collective-permute-done | bytes 1048608 | tf_op jit(solution)/shard_map/ppermute | solution.py:118
  554.0 16.5 %collective-permute-done.70 = bf16[512,1024]{1,0:T(8,128)(2,1)S(1)} collective-permute-done((bf16[512,1024]{1,0:T(8,128)(2,1)S(1)}, bf16[512,1024]{1,0:T(8,128)(2,1)S(1)}, u32[]{:S(2)}, u32[]{:S(2)}) %collective-permute-start.70) | collective-permute-done | bytes 1048608 | tf_op jit(solution)/shard_map/ppermute | solution.py:118
  582.1 25.8 %collective-permute-done.73 = bf16[512,1024]{1,0:T(8,128)(2,1)S(1)} collective-permute-done((bf16[512,1024]{1,0:T(8,128)(2,1)S(1)}, bf16[512,1024]{1,0:T(8,128)(2,1)S(1)}, u32[]{:S(2)}, u32[]{:S(2)}) %collective-permute-start.73) | collective-permute-done | bytes 1048608 | tf_op jit(solution)/shard_map/ppermute | solution.py:217
  612.8 12.4 %collective-permute-done.72 = bf16[256,2048]{1,0:T(8,128)(2,1)S(1)} collective-permute-done((bf16[256,2048]{1,0:T(8,128)(2,1)S(1)}, bf16[256,2048]{1,0:T(8,128)(2,1)S(1)}, u32[]{:S(2)}, u32[]{:S(2)}) %collective-permute-start.72) | collective-permute-done | bytes 1048608 | tf_op jit(solution)/shard_map/ppermute | solution.py:118
  635.3 14.8 %collective-permute-done.47 = bf16[128,2048]{1,0:T(8,128)(2,1)S(1)} collective-permute-done((bf16[128,2048]{1,0:T(8,128)(2,1)S(1)}, bf16[128,2048]{1,0:T(8,128)(2,1)S(1)}, u32[]{:S(2)}, u32[]{:S(2)}) %collective-permute-start.47) | collective-permute-done | bytes 524320 | tf_op jit(solution)/shard_map/ppermute | solution.py:157
  660.1 11.2 collective-permute-done.76
  680.4 12.7 %collective-permute-done.78 = bf16[256,2048]{1,0:T(8,128)(2,1)S(1)} collective-permute-done((bf16[256,2048]{1,0:T(8,128)(2,1)S(1)}, bf16[256,2048]{1,0:T(8,128)(2,1)S(1)}, u32[]{:S(2)}, u32[]{:S(2)}) %collective-permute-start.78) | collective-permute-done | bytes 1048608 | tf_op jit(solution)/shard_map/ppermute | solution.py:118
  700.7 15.4 %collective-permute-done.49 = bf16[4,128,2048]{2,1,0:T(8,128)(2,1)S(1)} collective-permute-done((bf16[4,128,2048]{2,1,0:T(8,128)(2,1)S(1)}, bf16[4,128,2048]{2,1,0:T(8,128)(2,1)S(1)}, u32[]{:S(2)}, u32[]{:S(2)}) %collective-permute-start.49) | collective-permute-done | bytes 2097184 | tf_op jit(solution)/shard_map/ppermute | solution.py:123
  723.8 14.4 %collective-permute-done.84 = bf16[256,2048]{1,0:T(8,128)(2,1)S(1)} collective-permute-done((bf16[256,2048]{1,0:T(8,128)(2,1)S(1)}, bf16[256,2048]{1,0:T(8,128)(2,1)S(1)}, u32[]{:S(2)}, u32[]{:S(2)}) %collective-permute-start.84) | collective-permute-done | bytes 1048608 | tf_op jit(solution)/shard_map/ppermute | solution.py:217
  742.5 25.0 %collective-permute-start.90 = (bf16[256,2048]{1,0:T(8,128)(2,1)S(1)}, bf16[256,2048]{1,0:T(8,128)(2,1)S(1)}, u32[]{:S(2)}, u32[]{:S(2)}) collective-permute-start(bf16[256,2048]{1,0:T(8,128)(2,1)S(1)} %add_convert_fusion.8), channel_id=1, source_target_pairs={{0,4},{12,8},{1,5},{13,9},{2,6},{14,10},{3,7},{15,11},{16,20},{28,... | collective-permute-start | bytes 3145736 | tf_op jit(solution)/shard_map/ppermute | solution.py:217
  773.9 17.1 %collective-permute-done.90 = bf16[256,2048]{1,0:T(8,128)(2,1)S(1)} collective-permute-done((bf16[256,2048]{1,0:T(8,128)(2,1)S(1)}, bf16[256,2048]{1,0:T(8,128)(2,1)S(1)}, u32[]{:S(2)}, u32[]{:S(2)}) %collective-permute-start.90) | collective-permute-done | bytes 1048608 | tf_op jit(solution)/shard_map/ppermute | solution.py:217
  796.6 9.0 collective-permute-done.42
  811.0 8.5 pad_maximum_fusion.1
  821.5 9.8 convolution_convert_fusion.refs_4_
  831.4 9.4 collective-permute-start.52
  840.7 32.4 %shard_map.170 = (bf16[2048,512]{1,0:T(8,128)(2,1)}, bf16[2048,512]{1,0:T(8,128)(2,1)}, bf16[2048,512]{1,0:T(8,128)(2,1)}) custom-call(s32[2]{0:T(128)} %pad_add_fusion.refs_0_, bf16[2048,512]{1,0:T(8,128)(2,1)} %get-tuple-element.99.refs_1_, bf16[2048,512]{1,0:T(8,128)(2,1)} %get-tuple-element.100.refs_2_, ...), custom_call_target="tpu_custom_call" | custom-call | tf_op jit(solution)/shard_map/pallas_call | solution.py:104
  873.1 6.3 fusion.31
  886.2 9.9 collective-permute-done.51
  925.7 6.7 collective-permute-start.62
  936.5 8.2 collective-permute-done.62
  949.8 12.4 %collective-permute-done.61 = bf16[256,2048]{1,0:T(8,128)(2,1)S(1)} collective-permute-done((bf16[256,2048]{1,0:T(8,128)(2,1)S(1)}, bf16[256,2048]{1,0:T(8,128)(2,1)S(1)}, u32[]{:S(2)}, u32[]{:S(2)}) %collective-permute-start.61) | collective-permute-done | bytes 1048608 | tf_op jit(solution)/shard_map/ppermute | solution.py:118
  963.9 6.7 collective-permute-done.68
  977.9 19.0 %collective-permute-done.66 = bf16[1024,512]{1,0:T(8,128)(2,1)S(1)} collective-permute-done((bf16[1024,512]{1,0:T(8,128)(2,1)}, bf16[1024,512]{1,0:T(8,128)(2,1)S(1)}, u32[]{:S(2)}, u32[]{:S(2)}) %collective-permute-start.66) | collective-permute-done | bytes 1048608 | tf_op jit(solution)/shard_map/ppermute | solution.py:118
  1003.8 15.5 %collective-permute-done.65 = bf16[1024,512]{1,0:T(8,128)(2,1)S(1)} collective-permute-done((bf16[1024,512]{1,0:T(8,128)(2,1)S(1)}, bf16[1024,512]{1,0:T(8,128)(2,1)S(1)}, u32[]{:S(2)}, u32[]{:S(2)}) %collective-permute-start.65) | collective-permute-done | bytes 1048608 | tf_op jit(solution)/shard_map/ppermute | solution.py:118
  1020.0 6.1 convert_add_fusion.3
  1026.1 11.3 collective-permute-done.64
  1037.4 6.5 collective-permute-start.87
  1052.3 13.6 %collective-permute-done.87 = bf16[256,2048]{1,0:T(8,128)(2,1)S(1)} collective-permute-done((bf16[256,2048]{1,0:T(8,128)(2,1)S(1)}, bf16[256,2048]{1,0:T(8,128)(2,1)S(1)}, u32[]{:S(2)}, u32[]{:S(2)}) %collective-permute-start.87) | collective-permute-done | bytes 1048608 | tf_op jit(solution)/shard_map/ppermute | solution.py:217
  1067.5 6.8 collective-permute-done.67
  1079.1 12.6 %collective-permute-done.82 = bf16[256,2048]{1,0:T(8,128)(2,1)S(1)} collective-permute-done((bf16[256,2048]{1,0:T(8,128)(2,1)S(1)}, bf16[256,2048]{1,0:T(8,128)(2,1)S(1)}, u32[]{:S(2)}, u32[]{:S(2)}) %collective-permute-start.82) | collective-permute-done | bytes 1048608 | tf_op jit(solution)/shard_map/ppermute | solution.py:211
  1093.1 7.2 collective-permute-done.55
  1101.5 18.8 %collective-permute-done.59 = bf16[256,2048]{1,0:T(8,128)(2,1)S(1)} collective-permute-done((bf16[256,2048]{1,0:T(8,128)(2,1)S(1)}, bf16[256,2048]{1,0:T(8,128)(2,1)S(1)}, u32[]{:S(2)}, u32[]{:S(2)}) %collective-permute-start.59) | collective-permute-done | bytes 1048608 | tf_op jit(solution)/shard_map/ppermute | solution.py:123
  1140.2 11.3 collective-permute-done.89
  1157.4 15.7 %collective-permute-done.94 = bf16[256,2048]{1,0:T(8,128)(2,1)} collective-permute-done((bf16[256,2048]{1,0:T(8,128)(2,1)S(1)}, bf16[256,2048]{1,0:T(8,128)(2,1)}, u32[]{:S(2)}, u32[]{:S(2)}) %collective-permute-start.94) | collective-permute-done | bytes 1048608 | tf_op jit(solution)/shard_map/ppermute | solution.py:211
  (521 shorter events, 378.2 us)
Async XLA Ops:
  9.3 27.6 %collective-permute-start.2 = (bf16[128,2048]{1,0:T(8,128)(2,1)}, bf16[128,2048]{1,0:T(8,128)(2,1)S(1)}, u32[]{:S(2)}, u32[]{:S(2)}) collective-permute-start(bf16[128,2048]{1,0:T(8,128)(2,1)} %fusion.40), channel_id=1, source_target_pairs={{8,0},{12,4},{9,1},{13,5},{10,2},{14,6},{11,3},{15,7},{24,16},{28,... | collective-permute-start | bytes 1572872 | tf_op jit(solution)/shard_map/ppermute | solution.py:150
  10.6 30.5 %collective-permute-start = (bf16[128,2048]{1,0:T(8,128)(2,1)}, bf16[128,2048]{1,0:T(8,128)(2,1)}, u32[]{:S(2)}, u32[]{:S(2)}) collective-permute-start(bf16[128,2048]{1,0:T(8,128)(2,1)} %fusion.40), channel_id=1, source_target_pairs={{0,4},{4,8},{8,12},{1,5},{5,9},{9,13},{2,6},{6,10},{10,14},{3,7},{... | collective-permute-start | bytes 1572872 | tf_op jit(solution)/shard_map/ppermute | solution.py:147
  65.3 45.9 %collective-permute-start.5 = (bf16[4,128,2048]{2,1,0:T(8,128)(2,1)S(1)}, bf16[4,128,2048]{2,1,0:T(8,128)(2,1)}, u32[]{:S(2)}, u32[]{:S(2)}) collective-permute-start(bf16[4,128,2048]{2,1,0:T(8,128)(2,1)S(1)} %bitcast_dynamic-update-slice_fusion.8), channel_id=1, source_target_pairs={{0,2},{1,3},{2,0},{3,1},{4,6},{5,7},{6,4},{7,5},{8,10},{9,11},{10,... | collective-permute-start | bytes 6291464 | tf_op jit(solution)/shard_map/ppermute | solution.py:123
  66.9 59.0 %collective-permute-start.9 = (bf16[1024,512]{1,0:T(8,128)(2,1)}, bf16[1024,512]{1,0:T(8,128)(2,1)}, u32[]{:S(2)}, u32[]{:S(2)}) collective-permute-start(bf16[1024,512]{1,0:T(8,128)(2,1)} %param.15), channel_id=1, source_target_pairs={{0,16},{16,0},{1,17},{17,1},{2,18},{18,2},{3,19},{19,3},{4,20},{20... | collective-permute-start | bytes 3145736 | tf_op jit(solution)/shard_map/ppermute | solution.py:118
  68.4 97.0 %collective-permute-start.8 = (bf16[1024,512]{1,0:T(8,128)(2,1)}, bf16[1024,512]{1,0:T(8,128)(2,1)}, u32[]{:S(2)}, u32[]{:S(2)}) collective-permute-start(bf16[1024,512]{1,0:T(8,128)(2,1)} %param.14), channel_id=1, source_target_pairs={{0,16},{16,0},{1,17},{17,1},{2,18},{18,2},{3,19},{19,3},{4,20},{20... | collective-permute-start | bytes 3145736 | tf_op jit(solution)/shard_map/ppermute | solution.py:118
  71.2 67.0 %collective-permute-start.20 = (bf16[256,2048]{1,0:T(8,128)(2,1)}, bf16[256,2048]{1,0:T(8,128)(2,1)}, u32[]{:S(2)}, u32[]{:S(2)}) collective-permute-start(bf16[256,2048]{1,0:T(8,128)(2,1)} %constant_dynamic-slice_fusion.5), channel_id=1, source_target_pairs={{0,16},{16,0},{1,17},{17,1},{2,18},{18,2},{3,19},{19,3},{4,20},{20... | collective-permute-start | bytes 3145736 | tf_op jit(solution)/shard_map/ppermute | solution.py:118
  75.0 88.9 %collective-permute-start.14 = (bf16[256,2048]{1,0:T(8,128)(2,1)}, bf16[256,2048]{1,0:T(8,128)(2,1)}, u32[]{:S(2)}, u32[]{:S(2)}) collective-permute-start(bf16[256,2048]{1,0:T(8,128)(2,1)} %constant_dynamic-slice_fusion.6), channel_id=1, source_target_pairs={{0,16},{16,0},{1,17},{17,1},{2,18},{18,2},{3,19},{19,3},{4,20},{20... | collective-permute-start | bytes 3145736 | tf_op jit(solution)/shard_map/ppermute | solution.py:118
  114.3 103.3 %collective-permute-start.6 = (bf16[1024,2048]{1,0:T(8,128)(2,1)}, bf16[1024,2048]{1,0:T(8,128)(2,1)}, u32[]{:S(2)}, u32[]{:S(2)}) collective-permute-start(bf16[1024,2048]{1,0:T(8,128)(2,1)} %bitcast.9), channel_id=1, source_target_pairs={{0,1},{1,0},{2,3},{3,2},{4,5},{5,4},{6,7},{7,6},{8,9},{9,8},{10,11... | collective-permute-start | bytes 12582920 | tf_op jit(solution)/shard_map/ppermute | solution.py:123
  125.8 57.3 %collective-permute-start.7 = (bf16[1024,512]{1,0:T(8,128)(2,1)}, bf16[1024,512]{1,0:T(8,128)(2,1)}, u32[]{:S(2)}, u32[]{:S(2)}) collective-permute-start(bf16[1024,512]{1,0:T(8,128)(2,1)} %param.13), channel_id=1, source_target_pairs={{0,16},{16,0},{1,17},{17,1},{2,18},{18,2},{3,19},{19,3},{4,20},{20... | collective-permute-start | bytes 3145736 | tf_op jit(solution)/shard_map/ppermute | solution.py:118
  138.2 67.4 %collective-permute-start.10 = (bf16[512,1024]{1,0:T(8,128)(2,1)}, bf16[512,1024]{1,0:T(8,128)(2,1)}, u32[]{:S(2)}, u32[]{:S(2)}) collective-permute-start(bf16[512,1024]{1,0:T(8,128)(2,1)} %param.16), channel_id=1, source_target_pairs={{0,16},{16,0},{1,17},{17,1},{2,18},{18,2},{3,19},{19,3},{4,20},{20... | collective-permute-start | bytes 3145736 | tf_op jit(solution)/shard_map/ppermute | solution.py:118
  163.9 49.9 %collective-permute-start.16 = (bf16[256,2048]{1,0:T(8,128)(2,1)}, bf16[256,2048]{1,0:T(8,128)(2,1)S(1)}, u32[]{:S(2)}, u32[]{:S(2)}) collective-permute-start(bf16[256,2048]{1,0:T(8,128)(2,1)} %collective-permute-done.14), channel_id=1, source_target_pairs={{0,8},{4,12},{1,9},{5,13},{2,10},{6,14},{3,11},{7,15},{16,24},{20,... | collective-permute-start | bytes 3145736 | tf_op jit(solution)/shard_map/ppermute | solution.py:149
  165.4 49.7 %collective-permute-start.17 = (bf16[256,2048]{1,0:T(8,128)(2,1)}, bf16[256,2048]{1,0:T(8,128)(2,1)S(1)}, u32[]{:S(2)}, u32[]{:S(2)}) collective-permute-start(bf16[256,2048]{1,0:T(8,128)(2,1)} %collective-permute-done.14), channel_id=1, source_target_pairs={{8,0},{12,4},{9,1},{13,5},{10,2},{14,6},{11,3},{15,7},{24,16},{28,... | collective-permute-start | bytes 3145736 | tf_op jit(solution)/shard_map/ppermute | solution.py:150
  183.1 66.5 %collective-permute-start.27 = (bf16[256,1024]{1,0:T(8,128)(2,1)S(1)}, bf16[256,1024]{1,0:T(8,128)(2,1)}, u32[]{:S(2)}, u32[]{:S(2)}) collective-permute-start(bf16[256,1024]{1,0:T(8,128)(2,1)S(1)} %copy-done.65), channel_id=1, source_target_pairs={{0,16},{16,0},{1,17},{17,1},{2,18},{18,2},{3,19},{19,3},{4,20},{20... | collective-permute-start | bytes 1572872 | tf_op jit(solution)/shard_map/ppermute | solution.py:118
  205.6 76.1 %collective-permute-start.26 = (bf16[1024,1024]{1,0:T(8,128)(2,1)}, bf16[1024,1024]{1,0:T(8,128)(2,1)}, u32[]{:S(2)}, u32[]{:S(2)}) collective-permute-start(bf16[1024,1024]{1,0:T(8,128)(2,1)} %get-tuple-element.162), channel_id=1, source_target_pairs={{0,16},{16,0},{1,17},{17,1},{2,18},{18,2},{3,19},{19,3},{4,20},{20... | collective-permute-start | bytes 6291464 | tf_op jit(solution)/shard_map/ppermute | solution.py:118
  213.8 69.2 %collective-permute-start.22 = (bf16[256,2048]{1,0:T(8,128)(2,1)}, bf16[256,2048]{1,0:T(8,128)(2,1)S(1)}, u32[]{:S(2)}, u32[]{:S(2)}) collective-permute-start(bf16[256,2048]{1,0:T(8,128)(2,1)} %collective-permute-done.20), channel_id=1, source_target_pairs={{0,8},{4,12},{1,9},{5,13},{2,10},{6,14},{3,11},{7,15},{16,24},{20,... | collective-permute-start | bytes 3145736 | tf_op jit(solution)/shard_map/ppermute | solution.py:149
  215.1 67.9 %collective-permute-start.23 = (bf16[256,2048]{1,0:T(8,128)(2,1)}, bf16[256,2048]{1,0:T(8,128)(2,1)}, u32[]{:S(2)}, u32[]{:S(2)}) collective-permute-start(bf16[256,2048]{1,0:T(8,128)(2,1)} %collective-permute-done.20), channel_id=1, source_target_pairs={{8,0},{12,4},{9,1},{13,5},{10,2},{14,6},{11,3},{15,7},{24,16},{28,... | collective-permute-start | bytes 3145736 | tf_op jit(solution)/shard_map/ppermute | solution.py:150
  217.6 89.2 %collective-permute-start.15 = (bf16[256,2048]{1,0:T(8,128)(2,1)}, bf16[256,2048]{1,0:T(8,128)(2,1)}, u32[]{:S(2)}, u32[]{:S(2)}) collective-permute-start(bf16[256,2048]{1,0:T(8,128)(2,1)} %collective-permute-done.14), channel_id=1, source_target_pairs={{0,4},{4,8},{8,12},{1,5},{5,9},{9,13},{2,6},{6,10},{10,14},{3,7},{... | collective-permute-start | bytes 3145736 | tf_op jit(solution)/shard_map/ppermute | solution.py:147
  249.6 41.3 %collective-permute-start.29 = (bf16[256,1024]{1,0:T(8,128)(2,1)}, bf16[256,1024]{1,0:T(8,128)(2,1)}, u32[]{:S(2)}, u32[]{:S(2)}) collective-permute-start(bf16[256,1024]{1,0:T(8,128)(2,1)} %collective-permute-done.27), channel_id=1, source_target_pairs={{0,8},{4,12},{1,9},{5,13},{2,10},{6,14},{3,11},{7,15},{16,24},{20,... | collective-permute-start | bytes 1572872 | tf_op jit(solution)/shard_map/ppermute | solution.py:149
  283.1 36.8 %collective-permute-start.18 = (bf16[256,2048]{1,0:T(8,128)(2,1)S(1)}, bf16[256,2048]{1,0:T(8,128)(2,1)S(1)}, u32[]{:S(2)}, u32[]{:S(2)}) collective-permute-start(bf16[256,2048]{1,0:T(8,128)(2,1)S(1)} %copy-done.60), channel_id=1, source_target_pairs={{8,12},{4,0},{9,13},{5,1},{10,14},{6,2},{11,15},{7,3},{24,28},{20,... | collective-permute-start | bytes 3145736 | tf_op jit(solution)/shard_map/ppermute | solution.py:157
  290.8 106.5 %collective-permute-start.21 = (bf16[256,2048]{1,0:T(8,128)(2,1)}, bf16[256,2048]{1,0:T(8,128)(2,1)S(1)}, u32[]{:S(2)}, u32[]{:S(2)}) collective-permute-start(bf16[256,2048]{1,0:T(8,128)(2,1)} %collective-permute-done.20), channel_id=1, source_target_pairs={{0,4},{4,8},{8,12},{1,5},{5,9},{9,13},{2,6},{6,10},{10,14},{3,7},{... | collective-permute-start | bytes 3145736 | tf_op jit(solution)/shard_map/ppermute | solution.py:147
  302.3 122.8 %collective-permute-start.25 = (bf16[256,2048]{1,0:T(8,128)(2,1)}, bf16[256,2048]{1,0:T(8,128)(2,1)S(1)}, u32[]{:S(2)}, u32[]{:S(2)}) collective-permute-start(bf16[256,2048]{1,0:T(8,128)(2,1)} %collective-permute-done.20), channel_id=1, source_target_pairs={{4,0},{8,4},{12,8},{5,1},{9,5},{13,9},{6,2},{10,6},{14,10},{7,3},{... | collective-permute-start | bytes 3145736 | tf_op jit(solution)/shard_map/ppermute | solution.py:148
  303.7 60.6 %collective-permute-start.19 = (bf16[256,2048]{1,0:T(8,128)(2,1)}, bf16[256,2048]{1,0:T(8,128)(2,1)S(1)}, u32[]{:S(2)}, u32[]{:S(2)}) collective-permute-start(bf16[256,2048]{1,0:T(8,128)(2,1)} %collective-permute-done.14), channel_id=1, source_target_pairs={{4,0},{8,4},{12,8},{5,1},{9,5},{13,9},{6,2},{10,6},{14,10},{7,3},{... | collective-permute-start | bytes 3145736 | tf_op jit(solution)/shard_map/ppermute | solution.py:148
  306.7 60.3 %collective-permute-start.28 = (bf16[256,1024]{1,0:T(8,128)(2,1)}, bf16[256,1024]{1,0:T(8,128)(2,1)S(1)}, u32[]{:S(2)}, u32[]{:S(2)}) collective-permute-start(bf16[256,1024]{1,0:T(8,128)(2,1)} %collective-permute-done.27), channel_id=1, source_target_pairs={{0,4},{4,8},{8,12},{1,5},{5,9},{9,13},{2,6},{6,10},{10,14},{3,7},{... | collective-permute-start | bytes 1572872 | tf_op jit(solution)/shard_map/ppermute | solution.py:147
  344.5 48.8 %collective-permute-start.13 = (bf16[256,2048]{1,0:T(8,128)(2,1)S(1)}, bf16[256,2048]{1,0:T(8,128)(2,1)S(1)}, u32[]{:S(2)}, u32[]{:S(2)}) collective-permute-start(bf16[256,2048]{1,0:T(8,128)(2,1)S(1)} %add_convert_fusion.39), channel_id=1, source_target_pairs={{0,1},{1,0},{2,3},{3,2},{4,5},{5,4},{6,7},{7,6},{8,9},{9,8},{10,11... | collective-permute-start | bytes 3145736 | tf_op jit(solution)/shard_map/ppermute | solution.py:123
  381.0 32.4 %collective-permute-start.24 = (bf16[256,2048]{1,0:T(8,128)(2,1)S(1)}, bf16[256,2048]{1,0:T(8,128)(2,1)S(1)}, u32[]{:S(2)}, u32[]{:S(2)}) collective-permute-start(bf16[256,2048]{1,0:T(8,128)(2,1)S(1)} %broadcast_select_fusion.3), channel_id=1, source_target_pairs={{8,12},{4,0},{9,13},{5,1},{10,14},{6,2},{11,15},{7,3},{24,28},{20,... | collective-permute-start | bytes 3145736 | tf_op jit(solution)/shard_map/ppermute | solution.py:157
  477.6 26.0 %collective-permute-start.33 = (bf16[512,1024]{1,0:T(8,128)(2,1)S(1)}, bf16[512,1024]{1,0:T(8,128)(2,1)S(1)}, u32[]{:S(2)}, u32[]{:S(2)}) collective-permute-start(bf16[512,1024]{1,0:T(8,128)(2,1)S(1)} %convolution_convert_fusion.14), channel_id=1, source_target_pairs={{0,16},{16,0},{1,17},{17,1},{2,18},{18,2},{3,19},{19,3},{4,20},{20... | collective-permute-start | bytes 3145736 | tf_op jit(solution)/shard_map/ppermute | solution.py:118
  478.1 48.1 %collective-permute-start.69 = (bf16[512,1024]{1,0:T(8,128)(2,1)S(1)}, bf16[512,1024]{1,0:T(8,128)(2,1)}, u32[]{:S(2)}, u32[]{:S(2)}) collective-permute-start(bf16[512,1024]{1,0:T(8,128)(2,1)S(1)} %convolution_convert_fusion.15), channel_id=1, source_target_pairs={{0,16},{16,0},{1,17},{17,1},{2,18},{18,2},{3,19},{19,3},{4,20},{20... | collective-permute-start | bytes 3145736 | tf_op jit(solution)/shard_map/ppermute | solution.py:118
  494.1 36.5 %collective-permute-start.37 = (bf16[256,2048]{1,0:T(8,128)(2,1)S(1)}, bf16[256,2048]{1,0:T(8,128)(2,1)S(1)}, u32[]{:S(2)}, u32[]{:S(2)}) collective-permute-start(bf16[256,2048]{1,0:T(8,128)(2,1)S(1)} %fusion.28), channel_id=1, source_target_pairs={{0,2},{1,3},{2,0},{3,1},{4,6},{5,7},{6,4},{7,5},{8,10},{9,11},{10,... | collective-permute-start | bytes 3145736 | tf_op jit(solution)/shard_map/ppermute | solution.py:123
  504.4 44.6 %collective-permute-start.35 = (bf16[512,1024]{1,0:T(8,128)(2,1)S(1)}, bf16[512,1024]{1,0:T(8,128)(2,1)S(1)}, u32[]{:S(2)}, u32[]{:S(2)}) collective-permute-start(bf16[512,1024]{1,0:T(8,128)(2,1)S(1)} %add_convert_fusion.38), channel_id=1, source_target_pairs={{0,4},{12,8},{1,5},{13,9},{2,6},{14,10},{3,7},{15,11},{16,20},{28,... | collective-permute-start | bytes 3145736 | tf_op jit(solution)/shard_map/ppermute | solution.py:217
  505.9 42.7 %collective-permute-start.34 = (bf16[512,1024]{1,0:T(8,128)(2,1)}, bf16[512,1024]{1,0:T(8,128)(2,1)S(1)}, u32[]{:S(2)}, u32[]{:S(2)}) collective-permute-start(bf16[512,1024]{1,0:T(8,128)(2,1)} %convolution_convert_fusion.13), channel_id=1, source_target_pairs={{0,16},{16,0},{1,17},{17,1},{2,18},{18,2},{3,19},{19,3},{4,20},{20... | collective-permute-start | bytes 3145736 | tf_op jit(solution)/shard_map/ppermute | solution.py:118
  529.9 40.7 %collective-permute-start.70 = (bf16[512,1024]{1,0:T(8,128)(2,1)S(1)}, bf16[512,1024]{1,0:T(8,128)(2,1)S(1)}, u32[]{:S(2)}, u32[]{:S(2)}) collective-permute-start(bf16[512,1024]{1,0:T(8,128)(2,1)S(1)} %convolution_convert_fusion.12), channel_id=1, source_target_pairs={{0,16},{16,0},{1,17},{17,1},{2,18},{18,2},{3,19},{19,3},{4,20},{20... | collective-permute-start | bytes 3145736 | tf_op jit(solution)/shard_map/ppermute | solution.py:118
  551.0 27.8 %collective-permute-start.45 = (bf16[128,2048]{1,0:T(8,128)(2,1)S(1)}, bf16[128,2048]{1,0:T(8,128)(2,1)S(1)}, u32[]{:S(2)}, u32[]{:S(2)}) collective-permute-start(bf16[128,2048]{1,0:T(8,128)(2,1)S(1)} %fusion.44), channel_id=1, source_target_pairs={{0,8},{4,12},{1,9},{5,13},{2,10},{6,14},{3,11},{7,15},{16,24},{20,... | collective-permute-start | bytes 1572872 | tf_op jit(solution)/shard_map/ppermute | solution.py:149
  552.3 27.1 %collective-permute-start.46 = (bf16[128,2048]{1,0:T(8,128)(2,1)S(1)}, bf16[128,2048]{1,0:T(8,128)(2,1)S(1)}, u32[]{:S(2)}, u32[]{:S(2)}) collective-permute-start(bf16[128,2048]{1,0:T(8,128)(2,1)S(1)} %fusion.44), channel_id=1, source_target_pairs={{8,0},{12,4},{9,1},{13,5},{10,2},{14,6},{11,3},{15,7},{24,16},{28,... | collective-permute-start | bytes 1572872 | tf_op jit(solution)/shard_map/ppermute | solution.py:150
  571.8 62.7 %collective-permute-start.44 = (bf16[128,2048]{1,0:T(8,128)(2,1)S(1)}, bf16[128,2048]{1,0:T(8,128)(2,1)S(1)}, u32[]{:S(2)}, u32[]{:S(2)}) collective-permute-start(bf16[128,2048]{1,0:T(8,128)(2,1)S(1)} %fusion.44), channel_id=1, source_target_pairs={{0,4},{4,8},{8,12},{1,5},{5,9},{9,13},{2,6},{6,10},{10,14},{3,7},{... | collective-permute-start | bytes 1572872 | tf_op jit(solution)/shard_map/ppermute | solution.py:147
  574.5 33.4 %collective-permute-start.73 = (bf16[512,1024]{1,0:T(8,128)(2,1)S(1)}, bf16[512,1024]{1,0:T(8,128)(2,1)S(1)}, u32[]{:S(2)}, u32[]{:S(2)}) collective-permute-start(bf16[512,1024]{1,0:T(8,128)(2,1)S(1)} %add_convert_fusion.19), channel_id=1, source_target_pairs={{0,4},{12,8},{1,5},{13,9},{2,6},{14,10},{3,7},{15,11},{16,20},{28,... | collective-permute-start | bytes 3145736 | tf_op jit(solution)/shard_map/ppermute | solution.py:217
  578.8 48.4 %collective-permute-start.38 = (bf16[256,2048]{1,0:T(8,128)(2,1)S(1)}, bf16[256,2048]{1,0:T(8,128)(2,1)S(1)}, u32[]{:S(2)}, u32[]{:S(2)}) collective-permute-start(bf16[256,2048]{1,0:T(8,128)(2,1)S(1)} %copy-done.58), channel_id=1, source_target_pairs={{0,16},{16,0},{1,17},{17,1},{2,18},{18,2},{3,19},{19,3},{4,20},{20... | collective-permute-start | bytes 3145736 | tf_op jit(solution)/shard_map/ppermute | solution.py:118
  579.4 45.8 %collective-permute-start.72 = (bf16[256,2048]{1,0:T(8,128)(2,1)S(1)}, bf16[256,2048]{1,0:T(8,128)(2,1)S(1)}, u32[]{:S(2)}, u32[]{:S(2)}) collective-permute-start(bf16[256,2048]{1,0:T(8,128)(2,1)S(1)} %copy-done.59), channel_id=1, source_target_pairs={{0,16},{16,0},{1,17},{17,1},{2,18},{18,2},{3,19},{19,3},{4,20},{20... | collective-permute-start | bytes 3145736 | tf_op jit(solution)/shard_map/ppermute | solution.py:118
  581.0 47.1 %collective-permute-start.40 = (bf16[512,1024]{1,0:T(8,128)(2,1)S(1)}, bf16[512,1024]{1,0:T(8,128)(2,1)S(1)}, u32[]{:S(2)}, u32[]{:S(2)}) collective-permute-start(bf16[512,1024]{1,0:T(8,128)(2,1)S(1)} %add_convert_fusion.36), channel_id=1, source_target_pairs={{4,8},{8,4},{5,9},{9,5},{6,10},{10,6},{7,11},{11,7},{20,24},{24,20... | collective-permute-start | bytes 3145736 | tf_op jit(solution)/shard_map/ppermute | solution.py:214
  625.2 47.1 %collective-permute-start.48 = (bf16[128,2048]{1,0:T(8,128)(2,1)S(1)}, bf16[128,2048]{1,0:T(8,128)(2,1)S(1)}, u32[]{:S(2)}, u32[]{:S(2)}) collective-permute-start(bf16[128,2048]{1,0:T(8,128)(2,1)S(1)} %fusion.44), channel_id=1, source_target_pairs={{4,0},{8,4},{12,8},{5,1},{9,5},{13,9},{6,2},{10,6},{14,10},{7,3},{... | collective-permute-start | bytes 1572872 | tf_op jit(solution)/shard_map/ppermute | solution.py:148
  627.2 46.5 %collective-permute-start.57 = (bf16[256,2048]{1,0:T(8,128)(2,1)S(1)}, bf16[256,2048]{1,0:T(8,128)(2,1)S(1)}, u32[]{:S(2)}, u32[]{:S(2)}) collective-permute-start(bf16[256,2048]{1,0:T(8,128)(2,1)S(1)} %add_convert_fusion.35), channel_id=1, source_target_pairs={{0,1},{1,0},{2,3},{3,2},{4,5},{5,4},{6,7},{7,6},{8,9},{9,8},{10,11... | collective-permute-start | bytes 3145736 | tf_op jit(solution)/shard_map/ppermute | solution.py:123
  656.6 85.8 %collective-permute-start.97 = (bf16[512,1024]{1,0:T(8,128)(2,1)S(1)}, bf16[512,1024]{1,0:T(8,128)(2,1)S(1)}, u32[]{:S(2)}, u32[]{:S(2)}) collective-permute-start(bf16[512,1024]{1,0:T(8,128)(2,1)S(1)} %add_convert_fusion.32), channel_id=1, source_target_pairs={{4,0},{8,12},{5,1},{9,13},{6,2},{10,14},{7,3},{11,15},{20,16},{24,... | collective-permute-start | bytes 3145736 | tf_op jit(solution)/shard_map/ppermute | solution.py:211
  672.4 43.7 %collective-permute-start.49 = (bf16[4,128,2048]{2,1,0:T(8,128)(2,1)S(1)}, bf16[4,128,2048]{2,1,0:T(8,128)(2,1)S(1)}, u32[]{:S(2)}, u32[]{:S(2)}) collective-permute-start(bf16[4,128,2048]{2,1,0:T(8,128)(2,1)S(1)} %bitcast_dynamic-update-slice_fusion.4), channel_id=1, source_target_pairs={{0,2},{1,3},{2,0},{3,1},{4,6},{5,7},{6,4},{7,5},{8,10},{9,11},{10,... | collective-permute-start | bytes 6291464 | tf_op jit(solution)/shard_map/ppermute | solution.py:123
  693.1 75.4 %collective-permute-start.98 = (bf16[512,1024]{1,0:T(8,128)(2,1)S(1)}, bf16[512,1024]{1,0:T(8,128)(2,1)S(1)}, u32[]{:S(2)}, u32[]{:S(2)}) collective-permute-start(bf16[512,1024]{1,0:T(8,128)(2,1)S(1)} %add_convert_fusion.15), channel_id=1, source_target_pairs={{4,0},{8,12},{5,1},{9,13},{6,2},{10,14},{7,3},{11,15},{20,16},{24,... | collective-permute-start | bytes 3145736 | tf_op jit(solution)/shard_map/ppermute | solution.py:211
  695.2 97.5 %collective-permute-start.43 = (bf16[512,1024]{1,0:T(8,128)(2,1)S(1)}, bf16[512,1024]{1,0:T(8,128)(2,1)S(1)}, u32[]{:S(2)}, u32[]{:S(2)}) collective-permute-start(bf16[512,1024]{1,0:T(8,128)(2,1)S(1)} %add_convert_fusion.33), channel_id=1, source_target_pairs={{4,8},{8,4},{5,9},{9,5},{6,10},{10,6},{7,11},{11,7},{20,24},{24,20... | collective-permute-start | bytes 3145736 | tf_op jit(solution)/shard_map/ppermute | solution.py:214
  738.2 72.7 %collective-permute-start.50 = (bf16[1024,2048]{1,0:T(8,128)(2,1)S(1)}, bf16[1024,2048]{1,0:T(8,128)(2,1)}, u32[]{:S(2)}, u32[]{:S(2)}) collective-permute-start(bf16[1024,2048]{1,0:T(8,128)(2,1)S(1)} %bitcast.161), channel_id=1, source_target_pairs={{0,1},{1,0},{2,3},{3,2},{4,5},{5,4},{6,7},{7,6},{8,9},{9,8},{10,11... | collective-permute-start | bytes 12582920 | tf_op jit(solution)/shard_map/ppermute | solution.py:123
  741.7 28.9 %collective-permute-start.91 = (bf16[256,2048]{1,0:T(8,128)(2,1)S(1)}, bf16[256,2048]{1,0:T(8,128)(2,1)S(1)}, u32[]{:S(2)}, u32[]{:S(2)}) collective-permute-start(bf16[256,2048]{1,0:T(8,128)(2,1)S(1)} %add_convert_fusion.7), channel_id=1, source_target_pairs={{4,8},{8,4},{5,9},{9,5},{6,10},{10,6},{7,11},{11,7},{20,24},{24,20... | collective-permute-start | bytes 3145736 | tf_op jit(solution)/shard_map/ppermute | solution.py:214
  742.5 48.5 %collective-permute-start.90 = (bf16[256,2048]{1,0:T(8,128)(2,1)S(1)}, bf16[256,2048]{1,0:T(8,128)(2,1)S(1)}, u32[]{:S(2)}, u32[]{:S(2)}) collective-permute-start(bf16[256,2048]{1,0:T(8,128)(2,1)S(1)} %add_convert_fusion.8), channel_id=1, source_target_pairs={{0,4},{12,8},{1,5},{13,9},{2,6},{14,10},{3,7},{15,11},{16,20},{28,... | collective-permute-start | bytes 3145736 | tf_op jit(solution)/shard_map/ppermute | solution.py:217
  768.6 37.0 %collective-permute-start.42 = (bf16[256,2048]{1,0:T(8,128)(2,1)S(1)}, bf16[256,2048]{1,0:T(8,128)(2,1)S(1)}, u32[]{:S(2)}, u32[]{:S(2)}) collective-permute-start(bf16[256,2048]{1,0:T(8,128)(2,1)S(1)} %add_convert_fusion.34), channel_id=1, source_target_pairs={{0,4},{12,8},{1,5},{13,9},{2,6},{14,10},{3,7},{15,11},{16,20},{28,... | collective-permute-start | bytes 3145736 | tf_op jit(solution)/shard_map/ppermute | solution.py:217
  791.0 134.6 %collective-permute-start.100 = (bf16[512,1024]{1,0:T(8,128)(2,1)}, bf16[512,1024]{1,0:T(8,128)(2,1)}, u32[]{:S(2)}, u32[]{:S(2)}) collective-permute-start(bf16[512,1024]{1,0:T(8,128)(2,1)} %add_convert_fusion.12), channel_id=1, source_target_pairs={{4,0},{8,12},{5,1},{9,13},{6,2},{10,14},{7,3},{11,15},{20,16},{24,... | collective-permute-start | bytes 3145736 | tf_op jit(solution)/shard_map/ppermute | solution.py:211
  807.0 165.8 %collective-permute-start.81 = (bf16[256,2048]{1,0:T(8,128)(2,1)}, bf16[256,2048]{1,0:T(8,128)(2,1)}, u32[]{:S(2)}, u32[]{:S(2)}) collective-permute-start(bf16[256,2048]{1,0:T(8,128)(2,1)} %add_convert_fusion.9), channel_id=1, source_target_pairs={{4,0},{8,12},{5,1},{9,13},{6,2},{10,14},{7,3},{11,15},{20,16},{24,... | collective-permute-start | bytes 3145736 | tf_op jit(solution)/shard_map/ppermute | solution.py:211
  808.3 312.5 %collective-permute-start.86 = (bf16[256,2048]{1,0:T(8,128)(2,1)}, bf16[256,2048]{1,0:T(8,128)(2,1)}, u32[]{:S(2)}, u32[]{:S(2)}) collective-permute-start(bf16[256,2048]{1,0:T(8,128)(2,1)} %add_convert_fusion.6), channel_id=1, source_target_pairs={{4,0},{8,12},{5,1},{9,13},{6,2},{10,14},{7,3},{11,15},{20,16},{24,... | collective-permute-start | bytes 3145736 | tf_op jit(solution)/shard_map/ppermute | solution.py:211
  819.5 59.9 %collective-permute-start.53 = (bf16[256,2048]{1,0:T(8,128)(2,1)}, bf16[256,2048]{1,0:T(8,128)(2,1)}, u32[]{:S(2)}, u32[]{:S(2)}) collective-permute-start(bf16[256,2048]{1,0:T(8,128)(2,1)} %add_convert_fusion.30), channel_id=1, source_target_pairs={{4,8},{8,4},{5,9},{9,5},{6,10},{10,6},{7,11},{11,7},{20,24},{24,20... | collective-permute-start | bytes 3145736 | tf_op jit(solution)/shard_map/ppermute | solution.py:214
  831.4 51.2 %collective-permute-start.52 = (bf16[256,2048]{1,0:T(8,128)(2,1)}, bf16[256,2048]{1,0:T(8,128)(2,1)}, u32[]{:S(2)}, u32[]{:S(2)}) collective-permute-start(bf16[256,2048]{1,0:T(8,128)(2,1)} %add_convert_fusion.31), channel_id=1, source_target_pairs={{0,4},{12,8},{1,5},{13,9},{2,6},{14,10},{3,7},{15,11},{16,20},{28,... | collective-permute-start | bytes 3145736 | tf_op jit(solution)/shard_map/ppermute | solution.py:217
  882.5 273.3 %collective-permute-start.92 = (bf16[256,2048]{1,0:T(8,128)(2,1)S(1)}, bf16[256,2048]{1,0:T(8,128)(2,1)}, u32[]{:S(2)}, u32[]{:S(2)}) collective-permute-start(bf16[256,2048]{1,0:T(8,128)(2,1)S(1)} %copy-done.36), channel_id=1, source_target_pairs={{4,0},{8,12},{5,1},{9,13},{6,2},{10,14},{7,3},{11,15},{20,16},{24,... | collective-permute-start | bytes 3145736 | tf_op jit(solution)/shard_map/ppermute | solution.py:211
  896.0 27.2 %collective-permute-start.99 = (bf16[512,1024]{1,0:T(8,128)(2,1)S(1)}, bf16[512,1024]{1,0:T(8,128)(2,1)S(1)}, u32[]{:S(2)}, u32[]{:S(2)}) collective-permute-start(bf16[512,1024]{1,0:T(8,128)(2,1)S(1)} %copy-done.38), channel_id=1, source_target_pairs={{4,0},{8,12},{5,1},{9,13},{6,2},{10,14},{7,3},{11,15},{20,16},{24,... | collective-permute-start | bytes 3145736 | tf_op jit(solution)/shard_map/ppermute | solution.py:211
  970.6 26.2 %collective-permute-start.66 = (bf16[1024,512]{1,0:T(8,128)(2,1)}, bf16[1024,512]{1,0:T(8,128)(2,1)S(1)}, u32[]{:S(2)}, u32[]{:S(2)}) collective-permute-start(bf16[1024,512]{1,0:T(8,128)(2,1)} %convolution_convert_fusion.18), channel_id=1, source_target_pairs={{0,16},{16,0},{1,17},{17,1},{2,18},{18,2},{3,19},{19,3},{4,20},{20... | collective-permute-start | bytes 3145736 | tf_op jit(solution)/shard_map/ppermute | solution.py:118
  972.9 201.8 %collective-permute-start.96 = (bf16[256,2048]{1,0:T(8,128)(2,1)S(1)}, bf16[256,2048]{1,0:T(8,128)(2,1)}, u32[]{:S(2)}, u32[]{:S(2)}) collective-permute-start(bf16[256,2048]{1,0:T(8,128)(2,1)S(1)} %copy-done.37), channel_id=1, source_target_pairs={{4,0},{8,12},{5,1},{9,13},{6,2},{10,14},{7,3},{11,15},{20,16},{24,... | collective-permute-start | bytes 3145736 | tf_op jit(solution)/shard_map/ppermute | solution.py:211
  976.0 43.3 %collective-permute-start.65 = (bf16[1024,512]{1,0:T(8,128)(2,1)S(1)}, bf16[1024,512]{1,0:T(8,128)(2,1)S(1)}, u32[]{:S(2)}, u32[]{:S(2)}) collective-permute-start(bf16[1024,512]{1,0:T(8,128)(2,1)S(1)} %copy-done.82), channel_id=1, source_target_pairs={{0,16},{16,0},{1,17},{17,1},{2,18},{18,2},{3,19},{19,3},{4,20},{20... | collective-permute-start | bytes 3145736 | tf_op jit(solution)/shard_map/ppermute | solution.py:118
  996.8 40.6 %collective-permute-start.64 = (bf16[1024,512]{1,0:T(8,128)(2,1)S(1)}, bf16[1024,512]{1,0:T(8,128)(2,1)S(1)}, u32[]{:S(2)}, u32[]{:S(2)}) collective-permute-start(bf16[1024,512]{1,0:T(8,128)(2,1)S(1)} %copy-done.81), channel_id=1, source_target_pairs={{0,16},{16,0},{1,17},{17,1},{2,18},{18,2},{3,19},{19,3},{4,20},{20... | collective-permute-start | bytes 3145736 | tf_op jit(solution)/shard_map/ppermute | solution.py:118
  1019.3 30.6 %collective-permute-start.88 = (bf16[256,2048]{1,0:T(8,128)(2,1)S(1)}, bf16[256,2048]{1,0:T(8,128)(2,1)S(1)}, u32[]{:S(2)}, u32[]{:S(2)}) collective-permute-start(bf16[256,2048]{1,0:T(8,128)(2,1)S(1)} %add_convert_fusion.22), channel_id=1, source_target_pairs={{4,8},{8,4},{5,9},{9,5},{6,10},{10,6},{7,11},{11,7},{20,24},{24,20... | collective-permute-start | bytes 3145736 | tf_op jit(solution)/shard_map/ppermute | solution.py:214
  1037.4 28.4 %collective-permute-start.87 = (bf16[256,2048]{1,0:T(8,128)(2,1)S(1)}, bf16[256,2048]{1,0:T(8,128)(2,1)S(1)}, u32[]{:S(2)}, u32[]{:S(2)}) collective-permute-start(bf16[256,2048]{1,0:T(8,128)(2,1)S(1)} %add_convert_fusion.23), channel_id=1, source_target_pairs={{0,4},{12,8},{1,5},{13,9},{2,6},{14,10},{3,7},{15,11},{16,20},{28,... | collective-permute-start | bytes 3145736 | tf_op jit(solution)/shard_map/ppermute | solution.py:217
  1091.7 28.6 %collective-permute-start.59 = (bf16[256,2048]{1,0:T(8,128)(2,1)S(1)}, bf16[256,2048]{1,0:T(8,128)(2,1)S(1)}, u32[]{:S(2)}, u32[]{:S(2)}) collective-permute-start(bf16[256,2048]{1,0:T(8,128)(2,1)S(1)} %fusion.27), channel_id=1, source_target_pairs={{0,2},{1,3},{2,0},{3,1},{4,6},{5,7},{6,4},{7,5},{8,10},{9,11},{10,... | collective-permute-start | bytes 3145736 | tf_op jit(solution)/shard_map/ppermute | solution.py:123
  1123.1 28.5 %collective-permute-start.89 = (bf16[256,2048]{1,0:T(8,128)(2,1)}, bf16[256,2048]{1,0:T(8,128)(2,1)}, u32[]{:S(2)}, u32[]{:S(2)}) collective-permute-start(bf16[256,2048]{1,0:T(8,128)(2,1)} %add_convert_fusion.4), channel_id=1, source_target_pairs={{4,0},{8,12},{5,1},{9,13},{6,2},{10,14},{7,3},{11,15},{20,16},{24,... | collective-permute-start | bytes 3145736 | tf_op jit(solution)/shard_map/ppermute | solution.py:211
  1125.1 48.1 %collective-permute-start.94 = (bf16[256,2048]{1,0:T(8,128)(2,1)S(1)}, bf16[256,2048]{1,0:T(8,128)(2,1)}, u32[]{:S(2)}, u32[]{:S(2)}) collective-permute-start(bf16[256,2048]{1,0:T(8,128)(2,1)S(1)} %add_convert_fusion.1), channel_id=1, source_target_pairs={{4,0},{8,12},{5,1},{9,13},{6,2},{10,14},{7,3},{11,15},{20,16},{24,... | collective-permute-start | bytes 3145736 | tf_op jit(solution)/shard_map/ppermute | solution.py:211
  (128 other events, 2879.7 us)
where the time goes:
time: 1190 us; the launch traced here: 1180 us
  waiting for transfers between devices  571 us (48%)
  starting transfers between devices  193 us (16%)
  matrix products  183 us (15%)
  other arithmetic  101 us (8%)
  local copies, waits for them, and re-layouts  73.5 us (6%)
  Pallas kernels  54.9 us (5%)
    ppermute x24, waiting for transfers between devices, swap_fsdp(): return lax.ppermute(v, 'fsdp', [(0, 1), (1, 0)])  211 us
    ppermute x12, waiting for transfers between devices, step(): got = lax.ppermute(send['a'], 'ctx', [(0, 1), (3, 2)])  104 us
    ppermute x16, waiting for transfers between devices, tp_swap(): return lax.ppermute(v, 'tp', [(i, i ^ bit) for i in range(n)])  85.3 us
    dot_general x32, matrix products, tdot(): lax.dot_general(left, right, (((0,), (0,)), ((), ())), preferred_element_...  77.1 us
    ppermute x12, starting transfers between devices, step(): got = lax.ppermute(send['a'], 'ctx', [(0, 1), (3, 2)])  72.3 us
    ppermute x5, waiting for transfers between devices, finish(): far = lax.ppermute(relay, 'ctx', [(2, 3), (1, 0)])  64.8 us
    pallas_call x2, Pallas kernels, attention_call(): pl.pallas_call(lambda *refs: body(block, *refs), grid_spec=pltpu.Prefetch...  54.9 us
    dot_general x9, matrix products, dot(): return jnp.dot(left, right, preferred_element_type=F32)  54.1 us
  transfers between devices with their start and end apart: 101, of which 46 were waited for; matrix products, arithmetic and copies ran while one was open for 25% of the time, Pallas kernels for 5%

commit v1 on v0

--- a/solution.py
+++ b/solution.py
@@ -34,10 +34,6 @@
 
 def ndot(left, right):
     return lax.dot_general(left, right, (((1,), (1,)), ((), ())), preferred_element_type=F32)
-
-
-def after(v, *others):
-    return lax.optimization_barrier((v,) + others)[0]
 
 
 def mm(left, right, dims):
@@ -56,8 +52,9 @@
     return expo / jnp.sum(expo, axis=-1, keepdims=True)
 
 
-def forward_body(block, lens, qraw, kraw, v, cosine, sine, qr, kr, ctx):
+def forward_body(block, lens, qraw, kraw, vraw, cosine, sine, qr, kr, v, ctx):
     length = lens[pl.program_id(0)]
+    v[...] = vraw[...].astype(BF)
     for raw, out in ((qraw, qr), (kraw, kr)):
         x = raw[...]
         out[...] = (x * cosine[...] + pltpu.roll(x, HD // 2, 1) * sine[...]).astype(BF)
@@ -94,19 +91,27 @@
     dv[...] = dv_sum[...].astype(BF)
 
 
-def attention_call(body, lengths, arrays, tables, outs, scratch):
+def attention_call(body, lengths, arrays, tables, outs, scratch, thirds=False):
     rows, width = arrays[0].shape
+    if thirds:
+        width //= 3
     nseq = lengths.shape[0]
     whole = rows // nseq
+    heads = width // HD
     tile = pl.BlockSpec((whole, HD), lambda s, h, lens: (s, h))
+    tiles = [tile] * len(arrays)
+    if thirds:
+        tiles = [
+            pl.BlockSpec((whole, HD), lambda s, h, lens, i=i: (s, h + i * heads)) for i in range(3)
+        ]
     table = pl.BlockSpec((whole, HD), lambda s, h, lens: (0, 0))
     block = whole // 4
     return pl.pallas_call(
         lambda *refs: body(block, *refs),
         grid_spec=pltpu.PrefetchScalarGridSpec(
             num_scalar_prefetch=1,
-            grid=(nseq, width // HD),
-            in_specs=[tile] * len(arrays) + [table] * len(tables),
+            grid=(nseq, heads),
+            in_specs=tiles + [table] * len(tables),
             out_specs=[tile] * outs,
             scratch_shapes=[pltpu.VMEM((whole, HD), F32)] * scratch,
         ),
@@ -123,11 +128,11 @@
     return lax.ppermute(v, "tp", [(i, i ^ bit) for i in range(n)])
 
 
-def tp_half(make, *parts):
+def tp_half(term):
     n = lax.axis_size("tp")
-    mid = parts[0].shape[0] // 2
-    got = tp_swap(make(*(p[mid:] for p in parts)).astype(BF), 1)
-    total = make(*(p[:mid] for p in parts)) + got.astype(F32)
+    mid = term.shape[0] // 2
+    got = tp_swap(term[mid:].astype(BF), 1)
+    total = term[:mid] + got.astype(F32)
     bit = 2
     while bit < n:
         sent = total.astype(BF)
@@ -143,17 +148,14 @@
 class LineGather:
     def __init__(self, piece):
         self.piece = piece
-        self.me = lax.axis_index("ctx")
         self.up1 = lax.ppermute(piece, "ctx", [(0, 1), (1, 2), (2, 3)])
         self.down1 = lax.ppermute(piece, "ctx", [(1, 0), (2, 1), (3, 2)])
         self.up2 = lax.ppermute(piece, "ctx", [(0, 2), (1, 3)])
         self.down2 = lax.ppermute(piece, "ctx", [(2, 0), (3, 1)])
 
-    def finish(self, store, *held):
-        me = self.me
+    def finish(self, store):
+        me = lax.axis_index("ctx")
         relay = jnp.where(me == 2, self.up2, self.down2)
-        if held:
-            relay = after(relay, *held)
         far = lax.ppermute(relay, "ctx", [(2, 3), (1, 0)])
         store(me, self.piece)
         store((me - 1) % 4, jnp.where(me >= 1, self.up1, far))
@@ -190,44 +192,31 @@
         pair.put(line[:, None], 0, half)
         pair.put(other[:, None], 0, 1 - half)
         mine = pair.v.reshape(-1, line.shape[-1])
-        return jnp.concatenate([mine, tp_swap(mine, 1)], axis=0)
-
-
-class Stream:
-    def __init__(self):
-        self.chunks, self.done, self.tick = [], [], 0
-        self.stage1, self.stage2, self.stage3 = {}, {}, {}
-
-    def step(self, *extra):
-        t, place = self.tick, lax.axis_index("ctx")
-        send = {}
-        if t < len(self.chunks):
-            send["x"] = self.chunks[t][1]
-        for name, held, lag in (("a", self.stage1, 1), ("b", self.stage2, 2), ("c", self.stage3, 3)):
-            if t - lag in held:
-                send[name] = held[t - lag]
-        send, extra = lax.optimization_barrier((send, extra))
-        if "c" in send:
-            back = lax.ppermute(send["c"], "ctx", [(1, 0), (2, 3)])
-            self.done.append(jnp.where((place == 0) | (place == 3), back, send["c"]))
-        if "b" in send:
-            got = lax.ppermute(send["b"], "ctx", [(1, 2), (2, 1)])
-            self.stage3[t - 2] = (send["b"].astype(F32) + got.astype(F32)).astype(BF)
-        if "a" in send:
-            got = lax.ppermute(send["a"], "ctx", [(0, 1), (3, 2)])
-            self.stage2[t - 1] = (send["a"].astype(F32) + got.astype(F32)).astype(BF)
-        if "x" in send:
-            got = swap_fsdp(send["x"])
-            self.stage1[t] = (self.chunks[t][0] + got.astype(F32)).astype(BF)
-        self.tick += 1
-        return extra
-
-
-def per_device(
+        return mine, tp_swap(mine, 1)
+
+
+def reduce_chunks(chunks):
+    place = lax.axis_index("ctx")
+    edge = (place == 0) | (place == 3)
+    done = []
+    for own, other in chunks:
+        got = swap_fsdp(other)
+        v = (own() + got.astype(F32)).astype(BF)
+        got = lax.ppermute(v, "ctx", [(0, 1), (3, 2)])
+        v = (v.astype(F32) + got.astype(F32)).astype(BF)
+        got = lax.ppermute(v, "ctx", [(1, 2), (2, 1)])
+        v = (v.astype(F32) + got.astype(F32)).astype(BF)
+        got = lax.ppermute(v, "ctx", [(1, 0), (2, 3)])
+        done.append(jnp.where(edge, got, v))
+    return done
+
+
+def layer(
     layer_input, cotangent, lengths, w_query, w_key, w_value, w_attn_out, w_gate, w_up, w_down
 ):
     nseq, local, width = layer_input.shape
     dh = width // 2
+    ff = w_gate.shape[1]
     rows = nseq * local
     whole = local * lax.axis_size("ctx")
     pair = lax.axis_index("fsdp")
@@ -269,35 +258,38 @@
                 box.put(part[None], seq, 0, side * dh)
         return box.v
 
-    u1_rows = Rows(
-        layer_norm(block_of(layer_input, core, at_fourth, fourth).astype(F32))[0].astype(BF)
-    )
     gate_part = swap_fsdp(quarter(w_gate))
     key_other = swap_fsdp(w_key)
     value_other = swap_fsdp(w_value)
     query_other = swap_fsdp(w_query)
     up_part = swap_fsdp(quarter(w_up))
     out_other = swap_fsdp(w_attn_out)
-    hf = w_down.shape[0] // 2
-    down_part = swap_fsdp(quarter(w_down[hf:]))
-    down_other = swap_fsdp(w_down[:hf])
-
+    down_other = swap_fsdp(w_down)
+    u1 = jnp.concatenate(Rows(
+        layer_norm(block_of(layer_input, core, at_fourth, fourth).astype(F32))[0].astype(BF)
+    ).finish(), axis=0)
     gate_line = LineGather(gate_part)
-    u1 = u1_rows.finish()
-    full_q = jnp.concatenate([w_query, query_other], axis=0)
-    full_k = jnp.concatenate([w_key, key_other], axis=0)
-    full_v = jnp.concatenate([w_value, value_other], axis=0)
+    up_line = LineGather(up_part)
+    full_qkv = jnp.concatenate(
+        [
+            jnp.concatenate([w_query, query_other], axis=0),
+            jnp.concatenate([w_key, key_other], axis=0),
+            jnp.concatenate([w_value, value_other], axis=0),
+        ],
+        axis=1,
+    )
     full_o = jnp.concatenate([w_attn_out, out_other], axis=1)
-    up_line = LineGather(after(up_part, u1))
-    qraw = dot(u1, full_q)
-    kraw = dot(u1, full_k)
-    values = dot(u1, full_v).astype(BF)
-    full_g, full_u = Box((width, w_gate.shape[1]), BF), Box((width, w_up.shape[1]), BF)
+    raw = dot(u1, full_qkv)
+    full_gu = Box((width, 2 * ff), BF)
+    full_d = Box((ff, width), BF)
     part = dh // 4
-    full_g.put(w_gate, 0)
-    gate_line.finish(lambda which, got: full_g.put(got, dh + which * part), qraw, kraw, values)
-    down_line = LineGather(after(down_part, qraw, kraw, values))
-    qr, kr, context = attention_call(forward_body, lens, (qraw, kraw, values), tables, 3, 0)
+    full_gu.put(w_gate, 0)
+    full_gu.put(w_up, 0, ff)
+    full_d.put(w_down, 0)
+    gate_line.finish(lambda which, got: full_gu.put(got, dh + which * part))
+    qr, kr, values, context = attention_call(
+        forward_body, lens, (raw, raw, raw), tables, 4, 0, thirds=True
+    )
 
     def my_rows(v):
         picked = lax.dynamic_slice_in_dim(v.reshape(nseq, whole, -1), me * local, local, 1)
@@ -307,28 +299,20 @@
     dy = arranged(cotangent).astype(F32) * keep
     dy_low = dy.astype(BF)
     xf = arranged(layer_input).astype(F32)
-    attn_half = tp_half(lambda u: dot(u, full_o), my_rows(context))
-    full_u.put(w_up, 0)
-    up_line.finish(lambda which, got: full_u.put(got, dh + which * part), attn_half)
-    full_d = Box((w_down.shape[0], width), BF)
-    full_d.put(w_down, 0)
+    h1 = xf + tp_join(tp_half(dot(my_rows(context), full_o)))
+    up_line.finish(lambda which, got: full_gu.put(got, dh + which * part, ff))
     full_d.put(down_other, 0, dh)
-    down_line.finish(
-        lambda which, got: full_d.put(got, hf + which * (hf // 4), dh), attn_half
-    )
-    h1 = xf + tp_join(attn_half)
     n2, rstd2 = layer_norm(h1)
     u2 = n2.astype(BF)
-    gate = dot(u2, full_g.v)
-    upper = dot(u2, full_u.v)
-    sigma = jax.nn.sigmoid(gate)
-    hidden = (gate * sigma * upper).astype(BF)
+    both = dot(u2, full_gu.v)
+    gate, upper = both[:, :ff], both[:, ff:]
+    hidden = (gate * jax.nn.sigmoid(gate) * upper).astype(BF)
 
     def grads_into(u, g, parts):
         step = dh // parts
         return [
             (
-                tdot(u[:, j * step : (j + 1) * step], g),
+                lambda j=j: tdot(u[:, j * step : (j + 1) * step], g),
                 tdot(u[:, dh + j * step : dh + (j + 1) * step], g).astype(BF),
             )
             for j in range(parts)
@@ -338,31 +322,22 @@
         step = u.shape[1] // parts
         return [
             (
-                tdot(u[:, j * step : (j + 1) * step], g[:, :dh]),
+                lambda j=j: tdot(u[:, j * step : (j + 1) * step], g[:, :dh]),
                 tdot(u[:, j * step : (j + 1) * step], g[:, dh:]).astype(BF),
             )
             for j in range(parts)
         ]
 
-    even, uneven = Stream(), Stream()
-
-    def enqueue(chunks):
-        even.chunks += chunks[0::2]
-        uneven.chunks += chunks[1::2]
-
-    enqueue(grads_out(hidden, dy_low, 4))
-    (dy_next,) = even.step(dy_low)
-    (dy_next,) = uneven.step(dy_next)
-    dhidden = ndot(dy_next, full_d.v)
+    hidden, gate, upper = lax.optimization_barrier((hidden, gate, upper))
+    sigma = jax.nn.sigmoid(gate)
+    dhidden = ndot(dy_low, full_d.v)
     dgate = (dhidden * upper * sigma * (1.0 + gate * (1.0 - sigma))).astype(BF)
     dupper = (dhidden * gate * sigma).astype(BF)
-    enqueue(grads_into(u2, dgate, 4))
-    enqueue(grads_into(u2, dupper, 4))
-    du2_half = tp_half(
-        lambda dg, du: ndot(dg, full_g.v) + ndot(du, full_u.v), dgate, dupper
-    )
-    even.step()
-    uneven.step()
+    du2_half = tp_half(ndot(jnp.concatenate([dgate, dupper], axis=1), full_gu.v))
+    chunks = grads_out(hidden, dy_low, 4) + grads_into(u2, dgate, 4) + grads_into(u2, dupper, 4)
+    totals = [None] * 12
+    totals[0::2] = reduce_chunks(chunks[0::2])
+    totals[1::2] = reduce_chunks(chunks[1::2])
 
     def fourth_at(v):
         return lax.dynamic_slice_in_dim(v, at_fourth, fourth, 0)
@@ -370,44 +345,39 @@
     da_part = fourth_at(dy) + norm_back(
         fourth_at(du2_half).astype(F32), fourth_at(n2), fourth_at(rstd2)
     )
-    (da_part,) = even.step(da_part.astype(BF))
-    da_rows = Rows(da_part)
-    uneven.step()
-    even.step()
-    uneven.step()
-    da = da_rows.finish()
-    (da,) = even.step(da)
-    uneven.step()
-    dcontext = ndot(da, full_o).astype(BF)
-    dq, dk, dv = attention_call(backward_body, lens, (qr, kr, values, dcontext), tables, 3, 2)
-    dq, dk, dv, hidden_late = even.step(dq, dk, dv, hidden)
-    uneven.step()
+    das = Rows(da_part.astype(BF)).finish()
+    grads = []
+    for i, part in enumerate(das):
+        cut = slice(i * whole, (i + 1) * whole)
+        dcontext = ndot(part, full_o).astype(BF)
+        grads.append(
+            attention_call(
+                backward_body,
+                lens[i : i + 1],
+                (qr[cut], kr[cut], values[cut], dcontext),
+                tables,
+                3,
+                2,
+            )
+        )
+    da = jnp.concatenate(das, axis=0)
+    dq, dk, dv = [jnp.concatenate(parts, axis=0) for parts in zip(*grads)]
     n1, rstd1 = layer_norm(xf)
-    pairs = grads_out(context, da, 1) + [grads_into(u1, g, 1)[0] for g in (dv, dk, dq)]
-    sent = even.step(*(p[1] for p in pairs))
-    g_attn, g_value, g_key, g_query = [
-        p[0] + swap_fsdp(s).astype(F32) for p, s in zip(pairs, sent)
-    ]
-    uneven.step()
-    du1 = tp_join(
-        tp_half(
-            lambda q, k, v: ndot(q, full_q) + ndot(k, full_k) + ndot(v, full_v),
-            my_rows(dq),
-            my_rows(dk),
-            my_rows(dv),
-        )
-    )
-    h2 = h1 + tp_join(tp_half(lambda u: dot(u, full_d.v), hidden_late))
-    even.step()
-    uneven.step()
-    even.step()
-    uneven.step()
+    made = [(grads_out, context, da)] + [(grads_into, u1, g) for g in (dv, dk, dq)]
+    summed = []
+    for maker, left, right in made:
+        ((own, other),) = maker(left, right, 1)
+        got = swap_fsdp(other)
+        summed.append(own() + got.astype(F32))
+    g_attn, g_value, g_key, g_query = summed
+    term = ndot(
+        jnp.concatenate([my_rows(dq), my_rows(dk), my_rows(dv)], axis=1), full_qkv
+    )
+    du1 = tp_join(tp_half(term))
+    h2 = h1 + tp_join(tp_half(dot(hidden, full_d.v)))
     dh1 = dy + norm_back(tp_join(du2_half), n2, rstd2)
     grad_input = restored(dh1 + norm_back(du1, n1, rstd1), F32)
     out_block = restored(h2 * keep, BF)
-    totals = [None] * 12
-    totals[0::2] = even.done
-    totals[1::2] = uneven.done
 
     def lay(parts):
         box = Box((parts[0].shape[0] * len(parts), parts[0].shape[1]), F32)
@@ -430,7 +400,7 @@
 
 def solution(mesh):
     return jax.shard_map(
-        per_device,
+        layer,
         mesh=mesh,
         in_specs=(
             P("fsdp", "ctx", None),

time: 1190 us -> 1820 us (1.53)
  waiting for transfers between devices: 571 us -> 1200 us
  starting transfers between devices: 193 us -> 232 us
  matrix products: 183 us -> 162 us
  other arithmetic: 101 us -> 80.4 us
    ppermute x36, waiting for transfers between devices: 151 us -> 599 us  [the longest x12 408 us: reduce_chunks(): got = lax.ppermute(v, 'ctx', [(1, 0), (2, 3)])]
    ppermute x24 -> x23, waiting for transfers between devices: 211 us -> 384 us  [swap_fsdp(): return lax.ppermute(v, 'fsdp', [(0, 1), (1, 0)])]
    ppermute x5 -> x4, waiting for transfers between devices: 16.4 us -> 68.8 us  [__init__(): self.down2 = lax.ppermute(piece, 'ctx', [(2, 0), (3, 1)])]
    ppermute x16, waiting for transfers between devices: 85.3 us -> 43.4 us  [tp_swap(): return lax.ppermute(v, 'tp', [(i, i ^ bit) for i in range(n)])]
    ppermute x5 -> x4, starting transfers between devices: 24.9 us -> 61.4 us  [__init__(): self.up1 = lax.ppermute(piece, 'ctx', [(0, 1), (1, 2), (2, 3)])]
    ppermute x5 -> x4, waiting for transfers between devices: 7.05 us -> 43.4 us  [__init__(): self.up2 = lax.ppermute(piece, 'ctx', [(0, 2), (1, 3)])]
    ppermute x5 -> x4, waiting for transfers between devices: 35.5 us -> 0.01 us  [__init__(): self.down1 = lax.ppermute(piece, 'ctx', [(1, 0), (2, 1), (3, 2)])]
    dot_general x9 -> x4, matrix products: 54.1 us -> 45.6 us  [dot(): return jnp.dot(left, right, preferred_element_type=F32)]
  transfers between devices with their start and end apart: 101 -> 95, of which waited for: 46 -> 48; matrix products, arithmetic and copies ran while one was open for 25% -> 12% of each run, Pallas kernels for 5% -> 3%
where the time goes in v1:
time: 1820 us
  waiting for transfers between devices  1200 us (66%)
  starting transfers between devices  232 us (13%)
  matrix products  162 us (9%)
  local copies, waits for them, and re-layouts  82.7 us (5%)
  other arithmetic  80.4 us (4%)
  Pallas kernels  58.5 us (3%)
    ppermute x12, waiting for transfers between devices, reduce_chunks(): got = lax.ppermute(v, 'ctx', [(1, 0), (2, 3)])  408 us
    ppermute x23, waiting for transfers between devices, swap_fsdp(): return lax.ppermute(v, 'fsdp', [(0, 1), (1, 0)])  384 us
    ppermute x12, waiting for transfers between devices, reduce_chunks(): got = lax.ppermute(v, 'ctx', [(0, 1), (3, 2)])  191 us
    ppermute x4, waiting for transfers between devices, __init__(): self.down2 = lax.ppermute(piece, 'ctx', [(2, 0), (3, 1)])  68.8 us
    ppermute x12, starting transfers between devices, reduce_chunks(): got = lax.ppermute(v, 'ctx', [(0, 1), (3, 2)])  65.8 us
    dot_general x32, matrix products, tdot(): lax.dot_general(left, right, (((0,), (0,)), ((), ())), preferred_element_...  63.1 us
    ppermute x4, starting transfers between devices, __init__(): self.up1 = lax.ppermute(piece, 'ctx', [(0, 1), (1, 2), (2, 3)])  61.4 us
    pallas_call x3, Pallas kernels, attention_call(): pl.pallas_call(lambda *refs: body(block, *refs), grid_spec=pltpu.Prefetch...  58.5 us
  transfers between devices with their start and end apart: 95, of which 48 were waited for; matrix products, arithmetic and copies ran while one was open for 12% of the time, Pallas kernels for 3%

profile of v1, /device:TPU:0, one launch (start us, length us, event | category | flops | bytes accessed | tf_op | source)
XLA Modules:
  0.0 1815.1 jit_solution(17485546720954346247)
XLA Ops:
  20.8 16.3 collective-permute-done.2
  74.4 25.3 %collective-permute-done.5 = bf16[4,128,2048]{2,1,0:T(8,128)(2,1)} collective-permute-done((bf16[4,128,2048]{2,1,0:T(8,128)(2,1)}, bf16[4,128,2048]{2,1,0:T(8,128)(2,1)}, u32[]{:S(2)}, u32[]{:S(2)}) %collective-permute-start.5) | collective-permute-done | bytes 2097184 | tf_op jit(solution)/shard_map/ppermute | solution.py:128
  102.9 8.1 dynamic_update_slice.142
  136.0 9.4 collective-permute-done.16
  150.6 21.7 %collective-permute-done.17 = bf16[256,2048]{1,0:T(8,128)(2,1)S(1)} collective-permute-done((bf16[256,2048]{1,0:T(8,128)(2,1)}, bf16[256,2048]{1,0:T(8,128)(2,1)S(1)}, u32[]{:S(2)}, u32[]{:S(2)}) %collective-permute-start.17) | collective-permute-done | bytes 1048608 | tf_op jit(solution)/shard_map/ppermute | solution.py:154
  180.9 9.0 collective-permute-done.22
  191.4 30.8 %collective-permute-done.23 = bf16[256,2048]{1,0:T(8,128)(2,1)S(1)} collective-permute-done((bf16[256,2048]{1,0:T(8,128)(2,1)}, bf16[256,2048]{1,0:T(8,128)(2,1)S(1)}, u32[]{:S(2)}, u32[]{:S(2)}) %collective-permute-start.23) | collective-permute-done | bytes 1048608 | tf_op jit(solution)/shard_map/ppermute | solution.py:154
  229.8 76.2 %collective-permute-done.9 = bf16[1024,512]{1,0:T(8,128)(2,1)S(1)} collective-permute-done((bf16[1024,512]{1,0:T(8,128)(2,1)S(1)}, bf16[1024,512]{1,0:T(8,128)(2,1)S(1)}, u32[]{:S(2)}, u32[]{:S(2)}) %collective-permute-start.9) | collective-permute-done | bytes 1048608 | tf_op jit(solution)/shard_map/ppermute | solution.py:123
  307.3 21.2 %collective-permute-done.8 = bf16[1024,512]{1,0:T(8,128)(2,1)S(1)} collective-permute-done((bf16[1024,512]{1,0:T(8,128)(2,1)S(1)}, bf16[1024,512]{1,0:T(8,128)(2,1)S(1)}, u32[]{:S(2)}, u32[]{:S(2)}) %collective-permute-start.8) | collective-permute-done | bytes 1048608 | tf_op jit(solution)/shard_map/ppermute | solution.py:123
  328.5 49.2 %collective-permute-start.21 = (bf16[256,2048]{1,0:T(8,128)(2,1)}, bf16[256,2048]{1,0:T(8,128)(2,1)}, u32[]{:S(2)}, u32[]{:S(2)}) collective-permute-start(bf16[256,2048]{1,0:T(8,128)(2,1)} %collective-permute-done.20), channel_id=1, source_target_pairs={{0,4},{4,8},{8,12},{1,5},{5,9},{9,13},{2,6},{6,10},{10,14},{3,7},{... | collective-permute-start | bytes 3145736 | tf_op jit(solution)/shard_map/ppermute | solution.py:151
  380.8 23.0 %fusion.refs_1_.refs_2_.refs_3_ = f32[2048,1536]{1,0:T(8,128)} fusion(bf16[1024,2048]{1,0:T(8,128)(2,1)} %collective-permute-done.6, bf16[1024,2048]{1,0:T(8,128)(2,1)} %bitcast.9, bf16[1024,512]{1,0:T(8,128)(2,1)} %copy-done.65, bf16[1024,512]{1,0:T(8,128)(2,1)} %param.15, bf16[1024,512]{1,0:T(8,128)(2,1)} %copy-done.66, bf16[1024,512]{1,0:T(8,128)(2,1)} %param.14, ...), kind=kOutput, calls=%fused_computation.5 | convolution fusion | flops 12939427840 | bytes 27262976 | tf_op jit(solution)/shard_map/dot_general | solution.py:28
  403.8 23.0 %shard_map.169 = (bf16[2048,512]{1,0:T(8,128)(2,1)}, bf16[2048,512]{1,0:T(8,128)(2,1)}, bf16[2048,512]{1,0:T(8,128)(2,1)}, bf16[2048,512]{1,0:T(8,128)(2,1)}) custom-call(s32[2]{0:T(128)} %pad_add_fusion.refs_0_, f32[2048,1536]{1,0:T(8,128)} %fusion.refs_1_.refs_2_.refs_3_, f32[2048,1536]{1,0:T(8,128)} %fusion.refs_1_.refs_2_.refs_3_, ...), custom_call_target="tpu_custom_call" | custom-call | tf_op jit(solution)/shard_map/pallas_call | solution.py:109
  437.1 6.3 collective-permute-done.24
  452.1 18.0 collective-permute-done.12
  490.3 12.4 fusion.153
  507.1 10.6 multiply_convert_fusion.1
  523.7 13.9 fusion.20
  540.0 7.3 fusion.154
  560.6 16.9 collective-permute-done.47
  579.7 20.2 %collective-permute-done.51 = bf16[256,2048]{1,0:T(8,128)(2,1)S(1)} collective-permute-done((bf16[256,2048]{1,0:T(8,128)(2,1)S(1)}, bf16[256,2048]{1,0:T(8,128)(2,1)S(1)}, u32[]{:S(2)}, u32[]{:S(2)}) %collective-permute-start.51) | collective-permute-done | bytes 1048608 | tf_op jit(solution)/shard_map/ppermute | solution.py:123
  602.2 20.2 %collective-permute-done.55 = bf16[256,2048]{1,0:T(8,128)(2,1)S(1)} collective-permute-done((bf16[256,2048]{1,0:T(8,128)(2,1)S(1)}, bf16[256,2048]{1,0:T(8,128)(2,1)S(1)}, u32[]{:S(2)}, u32[]{:S(2)}) %collective-permute-start.55) | collective-permute-done | bytes 1048608 | tf_op jit(solution)/shard_map/ppermute | solution.py:123
  624.6 20.2 %collective-permute-done.59 = bf16[256,2048]{1,0:T(8,128)(2,1)S(1)} collective-permute-done((bf16[256,2048]{1,0:T(8,128)(2,1)S(1)}, bf16[256,2048]{1,0:T(8,128)(2,1)S(1)}, u32[]{:S(2)}, u32[]{:S(2)}) %collective-permute-start.59) | collective-permute-done | bytes 1048608 | tf_op jit(solution)/shard_map/ppermute | solution.py:123
  647.1 20.2 %collective-permute-done.63 = bf16[256,2048]{1,0:T(8,128)(2,1)S(1)} collective-permute-done((bf16[256,2048]{1,0:T(8,128)(2,1)S(1)}, bf16[256,2048]{1,0:T(8,128)(2,1)S(1)}, u32[]{:S(2)}, u32[]{:S(2)}) %collective-permute-start.63) | collective-permute-done | bytes 1048608 | tf_op jit(solution)/shard_map/ppermute | solution.py:123
  669.6 20.2 %collective-permute-done.67 = bf16[256,2048]{1,0:T(8,128)(2,1)S(1)} collective-permute-done((bf16[256,2048]{1,0:T(8,128)(2,1)S(1)}, bf16[256,2048]{1,0:T(8,128)(2,1)S(1)}, u32[]{:S(2)}, u32[]{:S(2)}) %collective-permute-start.67) | collective-permute-done | bytes 1048608 | tf_op jit(solution)/shard_map/ppermute | solution.py:123
  692.1 42.7 %collective-permute-done.79 = bf16[512,1024]{1,0:T(8,128)(2,1)S(1)} collective-permute-done((bf16[512,1024]{1,0:T(8,128)(2,1)S(1)}, bf16[512,1024]{1,0:T(8,128)(2,1)S(1)}, u32[]{:S(2)}, u32[]{:S(2)}) %collective-permute-start.79) | collective-permute-done | bytes 1048608 | tf_op jit(solution)/shard_map/ppermute | solution.py:123
  737.0 20.2 %collective-permute-done.83 = bf16[512,1024]{1,0:T(8,128)(2,1)S(1)} collective-permute-done((bf16[512,1024]{1,0:T(8,128)(2,1)S(1)}, bf16[512,1024]{1,0:T(8,128)(2,1)S(1)}, u32[]{:S(2)}, u32[]{:S(2)}) %collective-permute-start.83) | collective-permute-done | bytes 1048608 | tf_op jit(solution)/shard_map/ppermute | solution.py:123
  759.5 20.2 %collective-permute-done.87 = bf16[512,1024]{1,0:T(8,128)(2,1)S(1)} collective-permute-done((bf16[512,1024]{1,0:T(8,128)(2,1)S(1)}, bf16[512,1024]{1,0:T(8,128)(2,1)S(1)}, u32[]{:S(2)}, u32[]{:S(2)}) %collective-permute-start.87) | collective-permute-done | bytes 1048608 | tf_op jit(solution)/shard_map/ppermute | solution.py:123
  782.0 16.8 collective-permute-start.48
  799.5 24.2 %collective-permute-done.91 = bf16[512,1024]{1,0:T(8,128)(2,1)S(1)} collective-permute-done((bf16[512,1024]{1,0:T(8,128)(2,1)S(1)}, bf16[512,1024]{1,0:T(8,128)(2,1)S(1)}, u32[]{:S(2)}, u32[]{:S(2)}) %collective-permute-start.91) | collective-permute-done | bytes 1048608 | tf_op jit(solution)/shard_map/ppermute | solution.py:123
  823.7 17.0 collective-permute-start.52
  850.0 14.0 collective-permute-done.52
  868.8 17.6 collective-permute-done.56
  891.3 17.6 collective-permute-done.60
  913.7 17.6 collective-permute-done.64
  936.2 17.6 collective-permute-done.68
  958.7 17.6 collective-permute-done.72
  983.2 38.0 %collective-permute-done.80 = bf16[512,1024]{1,0:T(8,128)(2,1)S(1)} collective-permute-done((bf16[512,1024]{1,0:T(8,128)(2,1)S(1)}, bf16[512,1024]{1,0:T(8,128)(2,1)S(1)}, u32[]{:S(2)}, u32[]{:S(2)}) %collective-permute-start.80) | collective-permute-done | bytes 1048608 | tf_op jit(solution)/shard_map/ppermute | solution.py:205
  1026.1 17.6 collective-permute-done.84
  1043.7 8.8 collective-permute-start.34
  1054.6 11.6 collective-permute-done.88
  1067.3 21.3 %collective-permute-done.92 = bf16[512,1024]{1,0:T(8,128)(2,1)S(1)} collective-permute-done((bf16[512,1024]{1,0:T(8,128)(2,1)S(1)}, bf16[512,1024]{1,0:T(8,128)(2,1)S(1)}, u32[]{:S(2)}, u32[]{:S(2)}) %collective-permute-start.92) | collective-permute-done | bytes 1048608 | tf_op jit(solution)/shard_map/ppermute | solution.py:205
  1089.8 19.6 %collective-permute-done.34 = bf16[128,2048]{1,0:T(8,128)(2,1)S(1)} collective-permute-done((bf16[128,2048]{1,0:T(8,128)(2,1)S(1)}, bf16[128,2048]{1,0:T(8,128)(2,1)S(1)}, u32[]{:S(2)}, u32[]{:S(2)}) %collective-permute-start.34) | collective-permute-done | bytes 524320 | tf_op jit(solution)/shard_map/ppermute | solution.py:153
  1117.6 45.7 %collective-permute-done.36 = bf16[128,2048]{1,0:T(8,128)(2,1)S(1)} collective-permute-done((bf16[128,2048]{1,0:T(8,128)(2,1)S(1)}, bf16[128,2048]{1,0:T(8,128)(2,1)S(1)}, u32[]{:S(2)}, u32[]{:S(2)}) %collective-permute-start.36) | collective-permute-done | bytes 524320 | tf_op jit(solution)/shard_map/ppermute | solution.py:159
  1182.1 183.4 %collective-permute-done.50 = bf16[256,2048]{1,0:T(8,128)(2,1)S(1)} collective-permute-done((bf16[256,2048]{1,0:T(8,128)(2,1)S(1)}, bf16[256,2048]{1,0:T(8,128)(2,1)S(1)}, u32[]{:S(2)}, u32[]{:S(2)}) %collective-permute-start.50) | collective-permute-done | bytes 1048608 | tf_op jit(solution)/shard_map/ppermute | solution.py:209
  1367.9 22.3 %collective-permute-done.54 = bf16[256,2048]{1,0:T(8,128)(2,1)S(1)} collective-permute-done((bf16[256,2048]{1,0:T(8,128)(2,1)S(1)}, bf16[256,2048]{1,0:T(8,128)(2,1)S(1)}, u32[]{:S(2)}, u32[]{:S(2)}) %collective-permute-start.54) | collective-permute-done | bytes 1048608 | tf_op jit(solution)/shard_map/ppermute | solution.py:209
  1391.9 20.8 %collective-permute-done.58 = bf16[256,2048]{1,0:T(8,128)(2,1)S(1)} collective-permute-done((bf16[256,2048]{1,0:T(8,128)(2,1)S(1)}, bf16[256,2048]{1,0:T(8,128)(2,1)S(1)}, u32[]{:S(2)}, u32[]{:S(2)}) %collective-permute-start.58) | collective-permute-done | bytes 1048608 | tf_op jit(solution)/shard_map/ppermute | solution.py:209
  1414.4 43.3 %collective-permute-done.66 = bf16[256,2048]{1,0:T(8,128)(2,1)S(1)} collective-permute-done((bf16[256,2048]{1,0:T(8,128)(2,1)S(1)}, bf16[256,2048]{1,0:T(8,128)(2,1)S(1)}, u32[]{:S(2)}, u32[]{:S(2)}) %collective-permute-start.66) | collective-permute-done | bytes 1048608 | tf_op jit(solution)/shard_map/ppermute | solution.py:209
  1460.7 19.4 %collective-permute-done.82 = bf16[512,1024]{1,0:T(8,128)(2,1)S(1)} collective-permute-done((bf16[512,1024]{1,0:T(8,128)(2,1)S(1)}, bf16[512,1024]{1,0:T(8,128)(2,1)S(1)}, u32[]{:S(2)}, u32[]{:S(2)}) %collective-permute-start.82) | collective-permute-done | bytes 1048608 | tf_op jit(solution)/shard_map/ppermute | solution.py:209
  1484.1 18.5 %collective-permute-done.86 = bf16[512,1024]{1,0:T(8,128)(2,1)S(1)} collective-permute-done((bf16[512,1024]{1,0:T(8,128)(2,1)S(1)}, bf16[512,1024]{1,0:T(8,128)(2,1)S(1)}, u32[]{:S(2)}, u32[]{:S(2)}) %collective-permute-start.86) | collective-permute-done | bytes 1048608 | tf_op jit(solution)/shard_map/ppermute | solution.py:209
  1504.5 20.6 %collective-permute-done.90 = bf16[512,1024]{1,0:T(8,128)(2,1)S(1)} collective-permute-done((bf16[512,1024]{1,0:T(8,128)(2,1)S(1)}, bf16[512,1024]{1,0:T(8,128)(2,1)S(1)}, u32[]{:S(2)}, u32[]{:S(2)}) %collective-permute-start.90) | collective-permute-done | bytes 1048608 | tf_op jit(solution)/shard_map/ppermute | solution.py:209
  1526.7 20.8 %collective-permute-done.94 = bf16[512,1024]{1,0:T(8,128)(2,1)S(1)} collective-permute-done((bf16[512,1024]{1,0:T(8,128)(2,1)S(1)}, bf16[512,1024]{1,0:T(8,128)(2,1)S(1)}, u32[]{:S(2)}, u32[]{:S(2)}) %collective-permute-start.94) | collective-permute-done | bytes 1048608 | tf_op jit(solution)/shard_map/ppermute | solution.py:209
  1552.6 17.4 collective-permute-done.70
  1570.4 22.1 %collective-permute-done.74 = bf16[256,2048]{1,0:T(8,128)(2,1)S(1)} collective-permute-done((bf16[256,2048]{1,0:T(8,128)(2,1)S(1)}, bf16[256,2048]{1,0:T(8,128)(2,1)S(1)}, u32[]{:S(2)}, u32[]{:S(2)}) %collective-permute-start.74) | collective-permute-done | bytes 1048608 | tf_op jit(solution)/shard_map/ppermute | solution.py:209
  1592.9 19.8 %collective-permute-done.78 = bf16[256,2048]{1,0:T(8,128)(2,1)S(1)} collective-permute-done((bf16[256,2048]{1,0:T(8,128)(2,1)S(1)}, bf16[256,2048]{1,0:T(8,128)(2,1)S(1)}, u32[]{:S(2)}, u32[]{:S(2)}) %collective-permute-start.78) | collective-permute-done | bytes 1048608 | tf_op jit(solution)/shard_map/ppermute | solution.py:209
  1613.0 8.6 convolution_convert_fusion.16.refs_4_
  1621.6 17.8 shard_map.170
  1649.4 17.8 shard_map.171
  1670.9 15.2 fusion.29
  1709.5 7.6 collective-permute-done.43
  1724.5 15.0 collective-permute-done.44
  1746.0 38.1 %collective-permute-done.46 = bf16[512,1024]{1,0:T(8,128)(2,1)S(1)} collective-permute-done((bf16[512,1024]{1,0:T(8,128)(2,1)S(1)}, bf16[512,1024]{1,0:T(8,128)(2,1)S(1)}, u32[]{:S(2)}, u32[]{:S(2)}) %collective-permute-start.46) | collective-permute-done | bytes 1048608 | tf_op jit(solution)/shard_map/ppermute | solution.py:123
  1784.0 6.1 convert_add_fusion.1
  1790.2 6.1 convert_add_fusion.2
  1796.3 6.7 convert_reduce_fusion
  (458 shorter events, 359.2 us)
Async XLA Ops:
  40.8 76.5 %collective-permute-start.14 = (bf16[256,2048]{1,0:T(8,128)(2,1)}, bf16[256,2048]{1,0:T(8,128)(2,1)}, u32[]{:S(2)}, u32[]{:S(2)}) collective-permute-start(bf16[256,2048]{1,0:T(8,128)(2,1)} %constant_dynamic-slice_fusion.8), channel_id=1, source_target_pairs={{0,16},{16,0},{1,17},{17,1},{2,18},{18,2},{3,19},{19,3},{4,20},{20... | collective-permute-start | bytes 3145736 | tf_op jit(solution)/shard_map/ppermute | solution.py:123
  54.7 45.0 %collective-permute-start.5 = (bf16[4,128,2048]{2,1,0:T(8,128)(2,1)}, bf16[4,128,2048]{2,1,0:T(8,128)(2,1)}, u32[]{:S(2)}, u32[]{:S(2)}) collective-permute-start(bf16[4,128,2048]{2,1,0:T(8,128)(2,1)} %bitcast_dynamic-update-slice_fusion.8), channel_id=1, source_target_pairs={{0,2},{1,3},{2,0},{3,1},{4,6},{5,7},{6,4},{7,5},{8,10},{9,11},{10,... | collective-permute-start | bytes 6291464 | tf_op jit(solution)/shard_map/ppermute | solution.py:128
  58.6 73.9 %collective-permute-start.20 = (bf16[256,2048]{1,0:T(8,128)(2,1)}, bf16[256,2048]{1,0:T(8,128)(2,1)}, u32[]{:S(2)}, u32[]{:S(2)}) collective-permute-start(bf16[256,2048]{1,0:T(8,128)(2,1)} %constant_dynamic-slice_fusion.7), channel_id=1, source_target_pairs={{0,16},{16,0},{1,17},{17,1},{2,18},{18,2},{3,19},{19,3},{4,20},{20... | collective-permute-start | bytes 3145736 | tf_op jit(solution)/shard_map/ppermute | solution.py:123
  60.1 113.7 %collective-permute-start.10 = (bf16[512,1024]{1,0:T(8,128)(2,1)}, bf16[512,1024]{1,0:T(8,128)(2,1)}, u32[]{:S(2)}, u32[]{:S(2)}) collective-permute-start(bf16[512,1024]{1,0:T(8,128)(2,1)} %param.16), channel_id=1, source_target_pairs={{0,16},{16,0},{1,17},{17,1},{2,18},{18,2},{3,19},{19,3},{4,20},{20... | collective-permute-start | bytes 3145736 | tf_op jit(solution)/shard_map/ppermute | solution.py:123
  102.9 276.1 %collective-permute-start.6 = (bf16[1024,2048]{1,0:T(8,128)(2,1)}, bf16[1024,2048]{1,0:T(8,128)(2,1)}, u32[]{:S(2)}, u32[]{:S(2)}) collective-permute-start(bf16[1024,2048]{1,0:T(8,128)(2,1)} %bitcast.9), channel_id=1, source_target_pairs={{0,1},{1,0},{2,3},{3,2},{4,5},{5,4},{6,7},{7,6},{8,9},{9,8},{10,11... | collective-permute-start | bytes 12582920 | tf_op jit(solution)/shard_map/ppermute | solution.py:128
  121.5 50.8 %collective-permute-start.17 = (bf16[256,2048]{1,0:T(8,128)(2,1)}, bf16[256,2048]{1,0:T(8,128)(2,1)S(1)}, u32[]{:S(2)}, u32[]{:S(2)}) collective-permute-start(bf16[256,2048]{1,0:T(8,128)(2,1)} %collective-permute-done.14), channel_id=1, source_target_pairs={{8,0},{12,4},{9,1},{13,5},{10,2},{14,6},{11,3},{15,7},{24,16},{28,... | collective-permute-start | bytes 3145736 | tf_op jit(solution)/shard_map/ppermute | solution.py:154
  132.5 92.3 %collective-permute-start.15 = (bf16[256,2048]{1,0:T(8,128)(2,1)}, bf16[256,2048]{1,0:T(8,128)(2,1)S(1)}, u32[]{:S(2)}, u32[]{:S(2)}) collective-permute-start(bf16[256,2048]{1,0:T(8,128)(2,1)} %collective-permute-done.14), channel_id=1, source_target_pairs={{0,4},{4,8},{8,12},{1,5},{5,9},{9,13},{2,6},{6,10},{10,14},{3,7},{... | collective-permute-start | bytes 3145736 | tf_op jit(solution)/shard_map/ppermute | solution.py:151
  172.3 49.9 %collective-permute-start.23 = (bf16[256,2048]{1,0:T(8,128)(2,1)}, bf16[256,2048]{1,0:T(8,128)(2,1)S(1)}, u32[]{:S(2)}, u32[]{:S(2)}) collective-permute-start(bf16[256,2048]{1,0:T(8,128)(2,1)} %collective-permute-done.20), channel_id=1, source_target_pairs={{8,0},{12,4},{9,1},{13,5},{10,2},{14,6},{11,3},{15,7},{24,16},{28,... | collective-permute-start | bytes 3145736 | tf_op jit(solution)/shard_map/ppermute | solution.py:154
  173.7 51.7 %collective-permute-start.18 = (bf16[256,2048]{1,0:T(8,128)(2,1)S(1)}, bf16[256,2048]{1,0:T(8,128)(2,1)S(1)}, u32[]{:S(2)}, u32[]{:S(2)}) collective-permute-start(bf16[256,2048]{1,0:T(8,128)(2,1)S(1)} %broadcast_select_fusion.4), channel_id=1, source_target_pairs={{8,12},{4,0},{9,13},{5,1},{10,14},{6,2},{11,15},{7,3},{24,28},{20,... | collective-permute-start | bytes 3145736 | tf_op jit(solution)/shard_map/ppermute | solution.py:159
  189.9 280.8 %collective-permute-start.26 = (bf16[2048,1024]{1,0:T(8,128)(2,1)}, bf16[2048,1024]{1,0:T(8,128)(2,1)}, u32[]{:S(2)}, u32[]{:S(2)}) collective-permute-start(bf16[2048,1024]{1,0:T(8,128)(2,1)} %param.19), channel_id=1, source_target_pairs={{0,16},{16,0},{1,17},{17,1},{2,18},{18,2},{3,19},{19,3},{4,20},{20... | collective-permute-start | bytes 12582920 | tf_op jit(solution)/shard_map/ppermute | solution.py:123
  222.2 83.8 %collective-permute-start.9 = (bf16[1024,512]{1,0:T(8,128)(2,1)S(1)}, bf16[1024,512]{1,0:T(8,128)(2,1)S(1)}, u32[]{:S(2)}, u32[]{:S(2)}) collective-permute-start(bf16[1024,512]{1,0:T(8,128)(2,1)S(1)} %copy-done.61), channel_id=1, source_target_pairs={{0,16},{16,0},{1,17},{17,1},{2,18},{18,2},{3,19},{19,3},{4,20},{20... | collective-permute-start | bytes 3145736 | tf_op jit(solution)/shard_map/ppermute | solution.py:123
  224.8 103.7 %collective-permute-start.8 = (bf16[1024,512]{1,0:T(8,128)(2,1)S(1)}, bf16[1024,512]{1,0:T(8,128)(2,1)S(1)}, u32[]{:S(2)}, u32[]{:S(2)}) collective-permute-start(bf16[1024,512]{1,0:T(8,128)(2,1)S(1)} %copy-done.63), channel_id=1, source_target_pairs={{0,16},{16,0},{1,17},{17,1},{2,18},{18,2},{3,19},{19,3},{4,20},{20... | collective-permute-start | bytes 3145736 | tf_op jit(solution)/shard_map/ppermute | solution.py:123
  225.4 152.3 %collective-permute-start.7 = (bf16[1024,512]{1,0:T(8,128)(2,1)S(1)}, bf16[1024,512]{1,0:T(8,128)(2,1)S(1)}, u32[]{:S(2)}, u32[]{:S(2)}) collective-permute-start(bf16[1024,512]{1,0:T(8,128)(2,1)S(1)} %copy-done.64), channel_id=1, source_target_pairs={{0,16},{16,0},{1,17},{17,1},{2,18},{18,2},{3,19},{19,3},{4,20},{20... | collective-permute-start | bytes 3145736 | tf_op jit(solution)/shard_map/ppermute | solution.py:123
  306.0 124.9 %collective-permute-start.19 = (bf16[256,2048]{1,0:T(8,128)(2,1)}, bf16[256,2048]{1,0:T(8,128)(2,1)}, u32[]{:S(2)}, u32[]{:S(2)}) collective-permute-start(bf16[256,2048]{1,0:T(8,128)(2,1)} %collective-permute-done.14), channel_id=1, source_target_pairs={{4,0},{8,4},{12,8},{5,1},{9,5},{13,9},{6,2},{10,6},{14,10},{7,3},{... | collective-permute-start | bytes 3145736 | tf_op jit(solution)/shard_map/ppermute | solution.py:152
  328.5 108.6 %collective-permute-start.21 = (bf16[256,2048]{1,0:T(8,128)(2,1)}, bf16[256,2048]{1,0:T(8,128)(2,1)}, u32[]{:S(2)}, u32[]{:S(2)}) collective-permute-start(bf16[256,2048]{1,0:T(8,128)(2,1)} %collective-permute-done.20), channel_id=1, source_target_pairs={{0,4},{4,8},{8,12},{1,5},{5,9},{9,13},{2,6},{6,10},{10,14},{3,7},{... | collective-permute-start | bytes 3145736 | tf_op jit(solution)/shard_map/ppermute | solution.py:151
  377.7 71.8 %collective-permute-start.25 = (bf16[256,2048]{1,0:T(8,128)(2,1)}, bf16[256,2048]{1,0:T(8,128)(2,1)}, u32[]{:S(2)}, u32[]{:S(2)}) collective-permute-start(bf16[256,2048]{1,0:T(8,128)(2,1)} %collective-permute-done.20), channel_id=1, source_target_pairs={{4,0},{8,4},{12,8},{5,1},{9,5},{13,9},{6,2},{10,6},{14,10},{7,3},{... | collective-permute-start | bytes 3145736 | tf_op jit(solution)/shard_map/ppermute | solution.py:152
  379.0 64.4 %collective-permute-start.24 = (bf16[256,2048]{1,0:T(8,128)(2,1)}, bf16[256,2048]{1,0:T(8,128)(2,1)}, u32[]{:S(2)}, u32[]{:S(2)}) collective-permute-start(bf16[256,2048]{1,0:T(8,128)(2,1)} %broadcast_select_fusion.3), channel_id=1, source_target_pairs={{8,12},{4,0},{9,13},{5,1},{10,14},{6,2},{11,15},{7,3},{24,28},{20,... | collective-permute-start | bytes 3145736 | tf_op jit(solution)/shard_map/ppermute | solution.py:159
  552.9 47.0 %collective-permute-start.51 = (bf16[256,2048]{1,0:T(8,128)(2,1)S(1)}, bf16[256,2048]{1,0:T(8,128)(2,1)S(1)}, u32[]{:S(2)}, u32[]{:S(2)}) collective-permute-start(bf16[256,2048]{1,0:T(8,128)(2,1)S(1)} %copy-done.46), channel_id=1, source_target_pairs={{0,16},{16,0},{1,17},{17,1},{2,18},{18,2},{3,19},{19,3},{4,20},{20... | collective-permute-start | bytes 3145736 | tf_op jit(solution)/shard_map/ppermute | solution.py:123
  553.5 68.9 %collective-permute-start.55 = (bf16[256,2048]{1,0:T(8,128)(2,1)S(1)}, bf16[256,2048]{1,0:T(8,128)(2,1)S(1)}, u32[]{:S(2)}, u32[]{:S(2)}) collective-permute-start(bf16[256,2048]{1,0:T(8,128)(2,1)S(1)} %copy-done.45), channel_id=1, source_target_pairs={{0,16},{16,0},{1,17},{17,1},{2,18},{18,2},{3,19},{19,3},{4,20},{20... | collective-permute-start | bytes 3145736 | tf_op jit(solution)/shard_map/ppermute | solution.py:123
  557.8 87.1 %collective-permute-start.59 = (bf16[256,2048]{1,0:T(8,128)(2,1)S(1)}, bf16[256,2048]{1,0:T(8,128)(2,1)S(1)}, u32[]{:S(2)}, u32[]{:S(2)}) collective-permute-start(bf16[256,2048]{1,0:T(8,128)(2,1)S(1)} %convolution_convert_fusion.4), channel_id=1, source_target_pairs={{0,16},{16,0},{1,17},{17,1},{2,18},{18,2},{3,19},{19,3},{4,20},{20... | collective-permute-start | bytes 3145736 | tf_op jit(solution)/shard_map/ppermute | solution.py:123
  558.7 108.7 %collective-permute-start.63 = (bf16[256,2048]{1,0:T(8,128)(2,1)S(1)}, bf16[256,2048]{1,0:T(8,128)(2,1)S(1)}, u32[]{:S(2)}, u32[]{:S(2)}) collective-permute-start(bf16[256,2048]{1,0:T(8,128)(2,1)S(1)} %convolution_convert_fusion.3), channel_id=1, source_target_pairs={{0,16},{16,0},{1,17},{17,1},{2,18},{18,2},{3,19},{19,3},{4,20},{20... | collective-permute-start | bytes 3145736 | tf_op jit(solution)/shard_map/ppermute | solution.py:123
  577.5 112.4 %collective-permute-start.67 = (bf16[256,2048]{1,0:T(8,128)(2,1)S(1)}, bf16[256,2048]{1,0:T(8,128)(2,1)S(1)}, u32[]{:S(2)}, u32[]{:S(2)}) collective-permute-start(bf16[256,2048]{1,0:T(8,128)(2,1)S(1)} %convolution_convert_fusion.2), channel_id=1, source_target_pairs={{0,16},{16,0},{1,17},{17,1},{2,18},{18,2},{3,19},{19,3},{4,20},{20... | collective-permute-start | bytes 3145736 | tf_op jit(solution)/shard_map/ppermute | solution.py:123
  599.9 182.0 %collective-permute-start.71 = (bf16[256,2048]{1,0:T(8,128)(2,1)S(1)}, bf16[256,2048]{1,0:T(8,128)(2,1)S(1)}, u32[]{:S(2)}, u32[]{:S(2)}) collective-permute-start(bf16[256,2048]{1,0:T(8,128)(2,1)S(1)} %convolution_convert_fusion.1), channel_id=1, source_target_pairs={{0,16},{16,0},{1,17},{17,1},{2,18},{18,2},{3,19},{19,3},{4,20},{20... | collective-permute-start | bytes 3145736 | tf_op jit(solution)/shard_map/ppermute | solution.py:123
  622.4 112.4 %collective-permute-start.79 = (bf16[512,1024]{1,0:T(8,128)(2,1)S(1)}, bf16[512,1024]{1,0:T(8,128)(2,1)S(1)}, u32[]{:S(2)}, u32[]{:S(2)}) collective-permute-start(bf16[512,1024]{1,0:T(8,128)(2,1)S(1)} %convolution_convert_fusion.11), channel_id=1, source_target_pairs={{0,16},{16,0},{1,17},{17,1},{2,18},{18,2},{3,19},{19,3},{4,20},{20... | collective-permute-start | bytes 3145736 | tf_op jit(solution)/shard_map/ppermute | solution.py:123
  644.9 112.4 %collective-permute-start.83 = (bf16[512,1024]{1,0:T(8,128)(2,1)S(1)}, bf16[512,1024]{1,0:T(8,128)(2,1)S(1)}, u32[]{:S(2)}, u32[]{:S(2)}) collective-permute-start(bf16[512,1024]{1,0:T(8,128)(2,1)S(1)} %convolution_convert_fusion.10), channel_id=1, source_target_pairs={{0,16},{16,0},{1,17},{17,1},{2,18},{18,2},{3,19},{19,3},{4,20},{20... | collective-permute-start | bytes 3145736 | tf_op jit(solution)/shard_map/ppermute | solution.py:123
  667.4 112.4 %collective-permute-start.87 = (bf16[512,1024]{1,0:T(8,128)(2,1)S(1)}, bf16[512,1024]{1,0:T(8,128)(2,1)S(1)}, u32[]{:S(2)}, u32[]{:S(2)}) collective-permute-start(bf16[512,1024]{1,0:T(8,128)(2,1)S(1)} %convolution_convert_fusion.9), channel_id=1, source_target_pairs={{0,16},{16,0},{1,17},{17,1},{2,18},{18,2},{3,19},{19,3},{4,20},{20... | collective-permute-start | bytes 3145736 | tf_op jit(solution)/shard_map/ppermute | solution.py:123
  689.8 151.6 %collective-permute-start.75 = (bf16[256,2048]{1,0:T(8,128)(2,1)S(1)}, bf16[256,2048]{1,0:T(8,128)(2,1)S(1)}, u32[]{:S(2)}, u32[]{:S(2)}) collective-permute-start(bf16[256,2048]{1,0:T(8,128)(2,1)S(1)} %convolution_convert_fusion), channel_id=1, source_target_pairs={{0,16},{16,0},{1,17},{17,1},{2,18},{18,2},{3,19},{19,3},{4,20},{20... | collective-permute-start | bytes 3145736 | tf_op jit(solution)/shard_map/ppermute | solution.py:123
  734.8 88.9 %collective-permute-start.91 = (bf16[512,1024]{1,0:T(8,128)(2,1)S(1)}, bf16[512,1024]{1,0:T(8,128)(2,1)S(1)}, u32[]{:S(2)}, u32[]{:S(2)}) collective-permute-start(bf16[512,1024]{1,0:T(8,128)(2,1)S(1)} %convolution_convert_fusion.8), channel_id=1, source_target_pairs={{0,16},{16,0},{1,17},{17,1},{2,18},{18,2},{3,19},{19,3},{4,20},{20... | collective-permute-start | bytes 3145736 | tf_op jit(solution)/shard_map/ppermute | solution.py:123
  757.2 86.3 %collective-permute-start.31 = (bf16[256,2048]{1,0:T(8,128)(2,1)S(1)}, bf16[256,2048]{1,0:T(8,128)(2,1)S(1)}, u32[]{:S(2)}, u32[]{:S(2)}) collective-permute-start(bf16[256,2048]{1,0:T(8,128)(2,1)S(1)} %fusion.26), channel_id=1, source_target_pairs={{0,2},{1,3},{2,0},{3,1},{4,6},{5,7},{6,4},{7,5},{8,10},{9,11},{10,... | collective-permute-start | bytes 3145736 | tf_op jit(solution)/shard_map/ppermute | solution.py:128
  779.7 65.7 %collective-permute-start.28 = (bf16[256,2048]{1,0:T(8,128)(2,1)S(1)}, bf16[256,2048]{1,0:T(8,128)(2,1)S(1)}, u32[]{:S(2)}, u32[]{:S(2)}) collective-permute-start(bf16[256,2048]{1,0:T(8,128)(2,1)S(1)} %fusion.27), channel_id=1, source_target_pairs={{0,2},{1,3},{2,0},{3,1},{4,6},{5,7},{6,4},{7,5},{8,10},{9,11},{10,... | collective-permute-start | bytes 3145736 | tf_op jit(solution)/shard_map/ppermute | solution.py:128
  782.0 66.2 %collective-permute-start.48 = (bf16[256,2048]{1,0:T(8,128)(2,1)S(1)}, bf16[256,2048]{1,0:T(8,128)(2,1)S(1)}, u32[]{:S(2)}, u32[]{:S(2)}) collective-permute-start(bf16[256,2048]{1,0:T(8,128)(2,1)S(1)} %add_convert_fusion.35), channel_id=1, source_target_pairs={{0,4},{12,8},{1,5},{13,9},{2,6},{14,10},{3,7},{15,11},{16,20},{28,... | collective-permute-start | bytes 3145736 | tf_op jit(solution)/shard_map/ppermute | solution.py:205
  843.6 65.3 %collective-permute-start.60 = (bf16[256,2048]{1,0:T(8,128)(2,1)S(1)}, bf16[256,2048]{1,0:T(8,128)(2,1)S(1)}, u32[]{:S(2)}, u32[]{:S(2)}) collective-permute-start(bf16[256,2048]{1,0:T(8,128)(2,1)S(1)} %add_convert_fusion.26), channel_id=1, source_target_pairs={{0,4},{12,8},{1,5},{13,9},{2,6},{14,10},{3,7},{15,11},{16,20},{28,... | collective-permute-start | bytes 3145736 | tf_op jit(solution)/shard_map/ppermute | solution.py:205
  845.4 86.0 %collective-permute-start.64 = (bf16[256,2048]{1,0:T(8,128)(2,1)S(1)}, bf16[256,2048]{1,0:T(8,128)(2,1)S(1)}, u32[]{:S(2)}, u32[]{:S(2)}) collective-permute-start(bf16[256,2048]{1,0:T(8,128)(2,1)S(1)} %add_convert_fusion.23), channel_id=1, source_target_pairs={{0,4},{12,8},{1,5},{13,9},{2,6},{14,10},{3,7},{15,11},{16,20},{28,... | collective-permute-start | bytes 3145736 | tf_op jit(solution)/shard_map/ppermute | solution.py:205
  848.2 105.6 %collective-permute-start.68 = (bf16[256,2048]{1,0:T(8,128)(2,1)S(1)}, bf16[256,2048]{1,0:T(8,128)(2,1)S(1)}, u32[]{:S(2)}, u32[]{:S(2)}) collective-permute-start(bf16[256,2048]{1,0:T(8,128)(2,1)S(1)} %add_convert_fusion.20), channel_id=1, source_target_pairs={{0,4},{12,8},{1,5},{13,9},{2,6},{14,10},{3,7},{15,11},{16,20},{28,... | collective-permute-start | bytes 3145736 | tf_op jit(solution)/shard_map/ppermute | solution.py:205
  863.9 112.4 %collective-permute-start.72 = (bf16[256,2048]{1,0:T(8,128)(2,1)S(1)}, bf16[256,2048]{1,0:T(8,128)(2,1)S(1)}, u32[]{:S(2)}, u32[]{:S(2)}) collective-permute-start(bf16[256,2048]{1,0:T(8,128)(2,1)S(1)} %add_convert_fusion.17), channel_id=1, source_target_pairs={{0,4},{12,8},{1,5},{13,9},{2,6},{14,10},{3,7},{15,11},{16,20},{28,... | collective-permute-start | bytes 3145736 | tf_op jit(solution)/shard_map/ppermute | solution.py:205
  886.4 166.5 %collective-permute-start.76 = (bf16[256,2048]{1,0:T(8,128)(2,1)S(1)}, bf16[256,2048]{1,0:T(8,128)(2,1)S(1)}, u32[]{:S(2)}, u32[]{:S(2)}) collective-permute-start(bf16[256,2048]{1,0:T(8,128)(2,1)S(1)} %add_convert_fusion.14), channel_id=1, source_target_pairs={{0,4},{12,8},{1,5},{13,9},{2,6},{14,10},{3,7},{15,11},{16,20},{28,... | collective-permute-start | bytes 3145736 | tf_op jit(solution)/shard_map/ppermute | solution.py:205
  908.9 112.4 %collective-permute-start.80 = (bf16[512,1024]{1,0:T(8,128)(2,1)S(1)}, bf16[512,1024]{1,0:T(8,128)(2,1)S(1)}, u32[]{:S(2)}, u32[]{:S(2)}) collective-permute-start(bf16[512,1024]{1,0:T(8,128)(2,1)S(1)} %add_convert_fusion.11), channel_id=1, source_target_pairs={{0,4},{12,8},{1,5},{13,9},{2,6},{14,10},{3,7},{15,11},{16,20},{28,... | collective-permute-start | bytes 3145736 | tf_op jit(solution)/shard_map/ppermute | solution.py:205
  931.3 112.4 %collective-permute-start.84 = (bf16[512,1024]{1,0:T(8,128)(2,1)S(1)}, bf16[512,1024]{1,0:T(8,128)(2,1)S(1)}, u32[]{:S(2)}, u32[]{:S(2)}) collective-permute-start(bf16[512,1024]{1,0:T(8,128)(2,1)S(1)} %add_convert_fusion.8), channel_id=1, source_target_pairs={{0,4},{12,8},{1,5},{13,9},{2,6},{14,10},{3,7},{15,11},{16,20},{28,... | collective-permute-start | bytes 3145736 | tf_op jit(solution)/shard_map/ppermute | solution.py:205
  953.8 112.4 %collective-permute-start.88 = (bf16[512,1024]{1,0:T(8,128)(2,1)S(1)}, bf16[512,1024]{1,0:T(8,128)(2,1)S(1)}, u32[]{:S(2)}, u32[]{:S(2)}) collective-permute-start(bf16[512,1024]{1,0:T(8,128)(2,1)S(1)} %add_convert_fusion.5), channel_id=1, source_target_pairs={{0,4},{12,8},{1,5},{13,9},{2,6},{14,10},{3,7},{15,11},{16,20},{28,... | collective-permute-start | bytes 3145736 | tf_op jit(solution)/shard_map/ppermute | solution.py:205
  976.3 112.4 %collective-permute-start.92 = (bf16[512,1024]{1,0:T(8,128)(2,1)S(1)}, bf16[512,1024]{1,0:T(8,128)(2,1)S(1)}, u32[]{:S(2)}, u32[]{:S(2)}) collective-permute-start(bf16[512,1024]{1,0:T(8,128)(2,1)S(1)} %add_convert_fusion.2), channel_id=1, source_target_pairs={{0,4},{12,8},{1,5},{13,9},{2,6},{14,10},{3,7},{15,11},{16,20},{28,... | collective-permute-start | bytes 3145736 | tf_op jit(solution)/shard_map/ppermute | solution.py:205
  1021.2 95.6 %collective-permute-start.33 = (bf16[128,2048]{1,0:T(8,128)(2,1)S(1)}, bf16[128,2048]{1,0:T(8,128)(2,1)S(1)}, u32[]{:S(2)}, u32[]{:S(2)}) collective-permute-start(bf16[128,2048]{1,0:T(8,128)(2,1)S(1)} %get-tuple-element.46), channel_id=1, source_target_pairs={{0,4},{4,8},{8,12},{1,5},{5,9},{9,13},{2,6},{6,10},{10,14},{3,7},{... | collective-permute-start | bytes 1572872 | tf_op jit(solution)/shard_map/ppermute | solution.py:151
  1043.7 65.7 %collective-permute-start.34 = (bf16[128,2048]{1,0:T(8,128)(2,1)S(1)}, bf16[128,2048]{1,0:T(8,128)(2,1)S(1)}, u32[]{:S(2)}, u32[]{:S(2)}) collective-permute-start(bf16[128,2048]{1,0:T(8,128)(2,1)S(1)} %get-tuple-element.46), channel_id=1, source_target_pairs={{0,8},{4,12},{1,9},{5,13},{2,10},{6,14},{3,11},{7,15},{16,24},{20,... | collective-permute-start | bytes 1572872 | tf_op jit(solution)/shard_map/ppermute | solution.py:153
  1052.9 56.5 %collective-permute-start.35 = (bf16[128,2048]{1,0:T(8,128)(2,1)S(1)}, bf16[128,2048]{1,0:T(8,128)(2,1)S(1)}, u32[]{:S(2)}, u32[]{:S(2)}) collective-permute-start(bf16[128,2048]{1,0:T(8,128)(2,1)S(1)} %get-tuple-element.46), channel_id=1, source_target_pairs={{8,0},{12,4},{9,1},{13,5},{10,2},{14,6},{11,3},{15,7},{24,16},{28,... | collective-permute-start | bytes 1572872 | tf_op jit(solution)/shard_map/ppermute | solution.py:154
  1110.2 55.3 %collective-permute-start.37 = (bf16[128,2048]{1,0:T(8,128)(2,1)S(1)}, bf16[128,2048]{1,0:T(8,128)(2,1)S(1)}, u32[]{:S(2)}, u32[]{:S(2)}) collective-permute-start(bf16[128,2048]{1,0:T(8,128)(2,1)S(1)} %get-tuple-element.46), channel_id=1, source_target_pairs={{4,0},{8,4},{12,8},{5,1},{9,5},{13,9},{6,2},{10,6},{14,10},{7,3},{... | collective-permute-start | bytes 1572872 | tf_op jit(solution)/shard_map/ppermute | solution.py:152
  1111.9 684.3 %collective-permute-start.29 = (bf16[256,2048]{1,0:T(8,128)(2,1)}, bf16[256,2048]{1,0:T(8,128)(2,1)}, u32[]{:S(2)}, u32[]{:S(2)}) collective-permute-start(bf16[256,2048]{1,0:T(8,128)(2,1)} %add_convert_fusion.38), channel_id=1, source_target_pairs={{0,1},{1,0},{2,3},{3,2},{4,5},{5,4},{6,7},{7,6},{8,9},{9,8},{10,11... | collective-permute-start | bytes 3145736 | tf_op jit(solution)/shard_map/ppermute | solution.py:128
  1112.9 51.4 %collective-permute-start.93 = (bf16[512,1024]{1,0:T(8,128)(2,1)S(1)}, bf16[512,1024]{1,0:T(8,128)(2,1)S(1)}, u32[]{:S(2)}, u32[]{:S(2)}) collective-permute-start(bf16[512,1024]{1,0:T(8,128)(2,1)S(1)} %add_convert_fusion.1), channel_id=1, source_target_pairs={{4,8},{8,4},{5,9},{9,5},{6,10},{10,6},{7,11},{11,7},{20,24},{24,20... | collective-permute-start | bytes 3145736 | tf_op jit(solution)/shard_map/ppermute | solution.py:207
  1115.1 48.1 %collective-permute-start.36 = (bf16[128,2048]{1,0:T(8,128)(2,1)S(1)}, bf16[128,2048]{1,0:T(8,128)(2,1)S(1)}, u32[]{:S(2)}, u32[]{:S(2)}) collective-permute-start(bf16[128,2048]{1,0:T(8,128)(2,1)S(1)} %broadcast_select_fusion.5), channel_id=1, source_target_pairs={{8,12},{4,0},{9,13},{5,1},{10,14},{6,2},{11,15},{7,3},{24,28},{20,... | collective-permute-start | bytes 1572872 | tf_op jit(solution)/shard_map/ppermute | solution.py:159
  1116.8 53.6 %collective-permute-start.49 = (bf16[256,2048]{1,0:T(8,128)(2,1)S(1)}, bf16[256,2048]{1,0:T(8,128)(2,1)S(1)}, u32[]{:S(2)}, u32[]{:S(2)}) collective-permute-start(bf16[256,2048]{1,0:T(8,128)(2,1)S(1)} %add_convert_fusion.34), channel_id=1, source_target_pairs={{4,8},{8,4},{5,9},{9,5},{6,10},{10,6},{7,11},{11,7},{20,24},{24,20... | collective-permute-start | bytes 3145736 | tf_op jit(solution)/shard_map/ppermute | solution.py:207
  1175.0 306.5 %collective-permute-start.38 = (bf16[4,128,2048]{2,1,0:T(8,128)(2,1)S(1)}, bf16[4,128,2048]{2,1,0:T(8,128)(2,1)S(1)}, u32[]{:S(2)}, u32[]{:S(2)}) collective-permute-start(bf16[4,128,2048]{2,1,0:T(8,128)(2,1)S(1)} %bitcast_dynamic-update-slice_fusion.4), channel_id=1, source_target_pairs={{0,2},{1,3},{2,0},{3,1},{4,6},{5,7},{6,4},{7,5},{8,10},{9,11},{10,... | collective-permute-start | bytes 6291464 | tf_op jit(solution)/shard_map/ppermute | solution.py:128
  1177.0 188.5 %collective-permute-start.50 = (bf16[256,2048]{1,0:T(8,128)(2,1)S(1)}, bf16[256,2048]{1,0:T(8,128)(2,1)S(1)}, u32[]{:S(2)}, u32[]{:S(2)}) collective-permute-start(bf16[256,2048]{1,0:T(8,128)(2,1)S(1)} %add_convert_fusion.33), channel_id=1, source_target_pairs={{4,0},{8,12},{5,1},{9,13},{6,2},{10,14},{7,3},{11,15},{20,16},{24,... | collective-permute-start | bytes 3145736 | tf_op jit(solution)/shard_map/ppermute | solution.py:209
  1178.7 211.6 %collective-permute-start.54 = (bf16[256,2048]{1,0:T(8,128)(2,1)S(1)}, bf16[256,2048]{1,0:T(8,128)(2,1)S(1)}, u32[]{:S(2)}, u32[]{:S(2)}) collective-permute-start(bf16[256,2048]{1,0:T(8,128)(2,1)S(1)} %add_convert_fusion.30), channel_id=1, source_target_pairs={{4,0},{8,12},{5,1},{9,13},{6,2},{10,14},{7,3},{11,15},{20,16},{24,... | collective-permute-start | bytes 3145736 | tf_op jit(solution)/shard_map/ppermute | solution.py:209
  1180.4 232.3 %collective-permute-start.58 = (bf16[256,2048]{1,0:T(8,128)(2,1)S(1)}, bf16[256,2048]{1,0:T(8,128)(2,1)S(1)}, u32[]{:S(2)}, u32[]{:S(2)}) collective-permute-start(bf16[256,2048]{1,0:T(8,128)(2,1)S(1)} %add_convert_fusion.27), channel_id=1, source_target_pairs={{4,0},{8,12},{5,1},{9,13},{6,2},{10,14},{7,3},{11,15},{20,16},{24,... | collective-permute-start | bytes 3145736 | tf_op jit(solution)/shard_map/ppermute | solution.py:209
  1365.5 93.6 %collective-permute-start.62 = (bf16[256,2048]{1,0:T(8,128)(2,1)S(1)}, bf16[256,2048]{1,0:T(8,128)(2,1)S(1)}, u32[]{:S(2)}, u32[]{:S(2)}) collective-permute-start(bf16[256,2048]{1,0:T(8,128)(2,1)S(1)} %add_convert_fusion.24), channel_id=1, source_target_pairs={{4,0},{8,12},{5,1},{9,13},{6,2},{10,14},{7,3},{11,15},{20,16},{24,... | collective-permute-start | bytes 3145736 | tf_op jit(solution)/shard_map/ppermute | solution.py:209
  1390.2 67.4 %collective-permute-start.66 = (bf16[256,2048]{1,0:T(8,128)(2,1)S(1)}, bf16[256,2048]{1,0:T(8,128)(2,1)S(1)}, u32[]{:S(2)}, u32[]{:S(2)}) collective-permute-start(bf16[256,2048]{1,0:T(8,128)(2,1)S(1)} %add_convert_fusion.21), channel_id=1, source_target_pairs={{4,0},{8,12},{5,1},{9,13},{6,2},{10,14},{7,3},{11,15},{20,16},{24,... | collective-permute-start | bytes 3145736 | tf_op jit(solution)/shard_map/ppermute | solution.py:209
  1412.7 67.4 %collective-permute-start.82 = (bf16[512,1024]{1,0:T(8,128)(2,1)S(1)}, bf16[512,1024]{1,0:T(8,128)(2,1)S(1)}, u32[]{:S(2)}, u32[]{:S(2)}) collective-permute-start(bf16[512,1024]{1,0:T(8,128)(2,1)S(1)} %add_convert_fusion.9), channel_id=1, source_target_pairs={{4,0},{8,12},{5,1},{9,13},{6,2},{10,14},{7,3},{11,15},{20,16},{24,... | collective-permute-start | bytes 3145736 | tf_op jit(solution)/shard_map/ppermute | solution.py:209
  1459.1 66.0 %collective-permute-start.90 = (bf16[512,1024]{1,0:T(8,128)(2,1)S(1)}, bf16[512,1024]{1,0:T(8,128)(2,1)S(1)}, u32[]{:S(2)}, u32[]{:S(2)}) collective-permute-start(bf16[512,1024]{1,0:T(8,128)(2,1)S(1)} %add_convert_fusion.3), channel_id=1, source_target_pairs={{4,0},{8,12},{5,1},{9,13},{6,2},{10,14},{7,3},{11,15},{20,16},{24,... | collective-permute-start | bytes 3145736 | tf_op jit(solution)/shard_map/ppermute | solution.py:209
  1480.1 67.4 %collective-permute-start.94 = (bf16[512,1024]{1,0:T(8,128)(2,1)S(1)}, bf16[512,1024]{1,0:T(8,128)(2,1)S(1)}, u32[]{:S(2)}, u32[]{:S(2)}) collective-permute-start(bf16[512,1024]{1,0:T(8,128)(2,1)S(1)} %add_convert_fusion), channel_id=1, source_target_pairs={{4,0},{8,12},{5,1},{9,13},{6,2},{10,14},{7,3},{11,15},{20,16},{24,... | collective-permute-start | bytes 3145736 | tf_op jit(solution)/shard_map/ppermute | solution.py:209
  1483.0 160.9 %collective-permute-start.39 = (bf16[1024,2048]{1,0:T(8,128)(2,1)}, bf16[1024,2048]{1,0:T(8,128)(2,1)}, u32[]{:S(2)}, u32[]{:S(2)}) collective-permute-start(bf16[1024,2048]{1,0:T(8,128)(2,1)} %bitcast.28), channel_id=1, source_target_pairs={{0,1},{1,0},{2,3},{3,2},{4,5},{5,4},{6,7},{7,6},{8,9},{9,8},{10,11... | collective-permute-start | bytes 12582920 | tf_op jit(solution)/shard_map/ppermute | solution.py:128
  1502.6 67.4 %collective-permute-start.70 = (bf16[256,2048]{1,0:T(8,128)(2,1)S(1)}, bf16[256,2048]{1,0:T(8,128)(2,1)S(1)}, u32[]{:S(2)}, u32[]{:S(2)}) collective-permute-start(bf16[256,2048]{1,0:T(8,128)(2,1)S(1)} %add_convert_fusion.18), channel_id=1, source_target_pairs={{4,0},{8,12},{5,1},{9,13},{6,2},{10,14},{7,3},{11,15},{20,16},{24,... | collective-permute-start | bytes 3145736 | tf_op jit(solution)/shard_map/ppermute | solution.py:209
  1525.1 67.4 %collective-permute-start.74 = (bf16[256,2048]{1,0:T(8,128)(2,1)S(1)}, bf16[256,2048]{1,0:T(8,128)(2,1)S(1)}, u32[]{:S(2)}, u32[]{:S(2)}) collective-permute-start(bf16[256,2048]{1,0:T(8,128)(2,1)S(1)} %add_convert_fusion.15), channel_id=1, source_target_pairs={{4,0},{8,12},{5,1},{9,13},{6,2},{10,14},{7,3},{11,15},{20,16},{24,... | collective-permute-start | bytes 3145736 | tf_op jit(solution)/shard_map/ppermute | solution.py:209
  1547.5 65.1 %collective-permute-start.78 = (bf16[256,2048]{1,0:T(8,128)(2,1)S(1)}, bf16[256,2048]{1,0:T(8,128)(2,1)S(1)}, u32[]{:S(2)}, u32[]{:S(2)}) collective-permute-start(bf16[256,2048]{1,0:T(8,128)(2,1)S(1)} %add_convert_fusion.12), channel_id=1, source_target_pairs={{4,0},{8,12},{5,1},{9,13},{6,2},{10,14},{7,3},{11,15},{20,16},{24,... | collective-permute-start | bytes 3145736 | tf_op jit(solution)/shard_map/ppermute | solution.py:209
  1702.4 87.8 %collective-permute-start.45 = (bf16[1024,512]{1,0:T(8,128)(2,1)S(1)}, bf16[1024,512]{1,0:T(8,128)(2,1)S(1)}, u32[]{:S(2)}, u32[]{:S(2)}) collective-permute-start(bf16[1024,512]{1,0:T(8,128)(2,1)S(1)} %convolution_convert_fusion.12), channel_id=1, source_target_pairs={{0,16},{16,0},{1,17},{17,1},{2,18},{18,2},{3,19},{19,3},{4,20},{20... | collective-permute-start | bytes 3145736 | tf_op jit(solution)/shard_map/ppermute | solution.py:123
  1708.5 75.5 %collective-permute-start.46 = (bf16[512,1024]{1,0:T(8,128)(2,1)S(1)}, bf16[512,1024]{1,0:T(8,128)(2,1)S(1)}, u32[]{:S(2)}, u32[]{:S(2)}) collective-permute-start(bf16[512,1024]{1,0:T(8,128)(2,1)S(1)} %fusion.37), channel_id=1, source_target_pairs={{0,16},{16,0},{1,17},{17,1},{2,18},{18,2},{3,19},{19,3},{4,20},{20... | collective-permute-start | bytes 3145736 | tf_op jit(solution)/shard_map/ppermute | solution.py:123
  1745.9 50.4 %collective-permute-start.42 = (bf16[256,2048]{1,0:T(8,128)(2,1)S(1)}, bf16[256,2048]{1,0:T(8,128)(2,1)S(1)}, u32[]{:S(2)}, u32[]{:S(2)}) collective-permute-start(bf16[256,2048]{1,0:T(8,128)(2,1)S(1)} %add_convert_fusion.36), channel_id=1, source_target_pairs={{0,1},{1,0},{2,3},{3,2},{4,5},{5,4},{6,7},{7,6},{8,9},{9,8},{10,11... | collective-permute-start | bytes 3145736 | tf_op jit(solution)/shard_map/ppermute | solution.py:128
  (101 other events, 2492.6 us)

commit v2 on v1

--- a/solution.py
+++ b/solution.py
@@ -52,8 +52,8 @@
     return expo / jnp.sum(expo, axis=-1, keepdims=True)
 
 
-def forward_body(block, lens, qraw, kraw, vraw, cosine, sine, qr, kr, v, ctx):
-    length = lens[pl.program_id(0)]
+def forward_body(block, start, lens, qraw, kraw, vraw, cosine, sine, qr, kr, v, ctx):
+    length = lens[start + pl.program_id(0)]
     v[...] = vraw[...].astype(BF)
     for raw, out in ((qraw, qr), (kraw, kr)):
         x = raw[...]
@@ -64,8 +64,8 @@
         ctx[first:last, :] = mm(probs, v[:last, :], ((1,), (0,))).astype(BF)
 
 
-def backward_body(block, lens, qr, kr, v, dctx, cosine, sine, dq, dk, dv, dk_sum, dv_sum):
-    length = lens[pl.program_id(0)]
+def backward_body(block, start, lens, qr, kr, v, dctx, cosine, sine, dq, dk, dv, dk_sum, dv_sum):
+    length = lens[start + pl.program_id(0)]
     factor = 1.0 / HD**0.5
     dk_sum[...] = jnp.zeros_like(dk_sum)
     dv_sum[...] = jnp.zeros_like(dv_sum)
@@ -91,31 +91,33 @@
     dv[...] = dv_sum[...].astype(BF)
 
 
-def attention_call(body, lengths, arrays, tables, outs, scratch, thirds=False):
+def attention_call(body, lengths, arrays, tables, outs, scratch, seqs, thirds=False):
     rows, width = arrays[0].shape
     if thirds:
         width //= 3
-    nseq = lengths.shape[0]
-    whole = rows // nseq
+    whole = rows // lengths.shape[0]
     heads = width // HD
-    tile = pl.BlockSpec((whole, HD), lambda s, h, lens: (s, h))
-    tiles = [tile] * len(arrays)
+    start, count = seqs
+
+    def tile(offset, column):
+        return pl.BlockSpec((whole, HD), lambda s, h, lens: (s + offset, h + column))
+
     if thirds:
-        tiles = [
-            pl.BlockSpec((whole, HD), lambda s, h, lens, i=i: (s, h + i * heads)) for i in range(3)
-        ]
+        tiles = [tile(start, i * heads) for i in range(3)]
+    else:
+        tiles = [tile(start if v.shape[0] == rows else 0, 0) for v in arrays]
     table = pl.BlockSpec((whole, HD), lambda s, h, lens: (0, 0))
     block = whole // 4
     return pl.pallas_call(
-        lambda *refs: body(block, *refs),
+        lambda *refs: body(block, start, *refs),
         grid_spec=pltpu.PrefetchScalarGridSpec(
             num_scalar_prefetch=1,
-            grid=(nseq, heads),
+            grid=(count, heads),
             in_specs=tiles + [table] * len(tables),
-            out_specs=[tile] * outs,
+            out_specs=[tile(0, 0)] * outs,
             scratch_shapes=[pltpu.VMEM((whole, HD), F32)] * scratch,
         ),
-        out_shape=[jax.ShapeDtypeStruct((rows, width), BF)] * outs,
+        out_shape=[jax.ShapeDtypeStruct((count * whole, width), BF)] * outs,
     )(lengths, *arrays, *tables)
 
 
@@ -132,13 +134,13 @@
     n = lax.axis_size("tp")
     mid = term.shape[0] // 2
     got = tp_swap(term[mid:].astype(BF), 1)
-    total = term[:mid] + got.astype(F32)
+    sent = (term[:mid] + got.astype(F32)).astype(BF)
     bit = 2
     while bit < n:
-        sent = total.astype(BF)
-        total = sent.astype(F32) + tp_swap(sent, bit).astype(F32)
+        got = tp_swap(sent, bit)
+        sent = (sent.astype(F32) + got.astype(F32)).astype(BF)
         bit *= 2
-    return total.astype(BF)
+    return sent
 
 
 def tp_join(kept):
@@ -147,20 +149,16 @@
 
 class LineGather:
     def __init__(self, piece):
-        self.piece = piece
-        self.up1 = lax.ppermute(piece, "ctx", [(0, 1), (1, 2), (2, 3)])
-        self.down1 = lax.ppermute(piece, "ctx", [(1, 0), (2, 1), (3, 2)])
-        self.up2 = lax.ppermute(piece, "ctx", [(0, 2), (1, 3)])
-        self.down2 = lax.ppermute(piece, "ctx", [(2, 0), (3, 1)])
+        n = lax.axis_size("ctx")
+        self.got = [piece]
+        for far in range(1, n):
+            pairs = [(i, (i + far) % n) for i in range(n)]
+            self.got.append(lax.ppermute(piece, "ctx", pairs))
 
     def finish(self, store):
         me = lax.axis_index("ctx")
-        relay = jnp.where(me == 2, self.up2, self.down2)
-        far = lax.ppermute(relay, "ctx", [(2, 3), (1, 0)])
-        store(me, self.piece)
-        store((me - 1) % 4, jnp.where(me >= 1, self.up1, far))
-        store((me - 2) % 4, jnp.where(me >= 2, self.up2, self.down2))
-        store((me - 3) % 4, jnp.where(me == 3, far, self.down1))
+        for far, got in enumerate(self.got):
+            store((me - far) % len(self.got), got)
 
 
 class Box:
@@ -198,16 +196,30 @@
 def reduce_chunks(chunks):
     place = lax.axis_index("ctx")
     edge = (place == 0) | (place == 3)
-    done = []
-    for own, other in chunks:
-        got = swap_fsdp(other)
-        v = (own() + got.astype(F32)).astype(BF)
-        got = lax.ppermute(v, "ctx", [(0, 1), (3, 2)])
-        v = (v.astype(F32) + got.astype(F32)).astype(BF)
-        got = lax.ppermute(v, "ctx", [(1, 2), (2, 1)])
-        v = (v.astype(F32) + got.astype(F32)).astype(BF)
-        got = lax.ppermute(v, "ctx", [(1, 0), (2, 3)])
-        done.append(jnp.where(edge, got, v))
+    n = len(chunks)
+    first, inner, crossed, done = {}, {}, {}, []
+    for tick in range(n + 3):
+        a, b, c = tick - 1, tick - 2, tick - 3
+        total = sent = None
+        pairs = [(0, 1), (1, 0), (2, 3), (3, 2)]
+        if c in crossed:
+            sent = total = (inner[c].astype(F32) + crossed[c].astype(F32)).astype(BF)
+        if a in first:
+            alone = total is None or total.shape != first[a].shape
+            sent = first[a] if alone else jnp.where(edge, first[a], total)
+        if sent is not None:
+            got = lax.ppermute(sent, "ctx", pairs)
+        if total is not None:
+            back = got if total.shape == sent.shape else lax.ppermute(total, "ctx", pairs)
+            done.append(jnp.where(edge, back, total))
+        if b in inner:
+            crossed[b] = lax.ppermute(inner[b], "ctx", [(1, 2), (2, 1)])
+        if a in first:
+            inner[a] = (first[a].astype(F32) + got.astype(F32)).astype(BF)
+        if tick < n:
+            own, other = chunks[tick]
+            got = swap_fsdp(other)
+            first[tick] = (own() + got.astype(F32)).astype(BF)
     return done
 
 
@@ -259,10 +271,10 @@
         return box.v
 
     gate_part = swap_fsdp(quarter(w_gate))
+    up_part = swap_fsdp(quarter(w_up))
     key_other = swap_fsdp(w_key)
     value_other = swap_fsdp(w_value)
     query_other = swap_fsdp(w_query)
-    up_part = swap_fsdp(quarter(w_up))
     out_other = swap_fsdp(w_attn_out)
     down_other = swap_fsdp(w_down)
     u1 = jnp.concatenate(Rows(
@@ -288,7 +300,7 @@
     full_d.put(w_down, 0)
     gate_line.finish(lambda which, got: full_gu.put(got, dh + which * part))
     qr, kr, values, context = attention_call(
-        forward_body, lens, (raw, raw, raw), tables, 4, 0, thirds=True
+        forward_body, lens, (raw, raw, raw), tables, 4, 0, (0, nseq), thirds=True
     )
 
     def my_rows(v):
@@ -308,17 +320,22 @@
     gate, upper = both[:, :ff], both[:, ff:]
     hidden = (gate * jax.nn.sigmoid(gate) * upper).astype(BF)
 
-    def grads_into(u, g, parts):
-        step = dh // parts
+    def grads_into(u, g, high, wide):
+        step, span = dh // high, g.shape[1] // wide
         return [
             (
-                lambda j=j: tdot(u[:, j * step : (j + 1) * step], g),
-                tdot(u[:, dh + j * step : dh + (j + 1) * step], g).astype(BF),
+                lambda j=j, k=k: tdot(
+                    u[:, j * step : (j + 1) * step], g[:, k * span : (k + 1) * span]
+                ),
+                tdot(
+                    u[:, dh + j * step : dh + (j + 1) * step], g[:, k * span : (k + 1) * span]
+                ).astype(BF),
             )
-            for j in range(parts)
+            for j in range(high)
+            for k in range(wide)
         ]
 
-    def grads_out(u, g, parts):
+    def grads_out(u, g, parts, wide=1):
         step = u.shape[1] // parts
         return [
             (
@@ -328,13 +345,14 @@
             for j in range(parts)
         ]
 
-    hidden, gate, upper = lax.optimization_barrier((hidden, gate, upper))
+    hidden, both = lax.optimization_barrier((hidden, both))
+    gate, upper = both[:, :ff], both[:, ff:]
     sigma = jax.nn.sigmoid(gate)
     dhidden = ndot(dy_low, full_d.v)
     dgate = (dhidden * upper * sigma * (1.0 + gate * (1.0 - sigma))).astype(BF)
     dupper = (dhidden * gate * sigma).astype(BF)
     du2_half = tp_half(ndot(jnp.concatenate([dgate, dupper], axis=1), full_gu.v))
-    chunks = grads_out(hidden, dy_low, 4) + grads_into(u2, dgate, 4) + grads_into(u2, dupper, 4)
+    chunks = grads_out(hidden, dy_low, 4) + grads_into(u2, dgate, 2, 2) + grads_into(u2, dupper, 2, 2)
     totals = [None] * 12
     totals[0::2] = reduce_chunks(chunks[0::2])
     totals[1::2] = reduce_chunks(chunks[1::2])
@@ -348,17 +366,9 @@
     das = Rows(da_part.astype(BF)).finish()
     grads = []
     for i, part in enumerate(das):
-        cut = slice(i * whole, (i + 1) * whole)
         dcontext = ndot(part, full_o).astype(BF)
         grads.append(
-            attention_call(
-                backward_body,
-                lens[i : i + 1],
-                (qr[cut], kr[cut], values[cut], dcontext),
-                tables,
-                3,
-                2,
-            )
+            attention_call(backward_body, lens, (qr, kr, values, dcontext), tables, 3, 2, (i, 1))
         )
     da = jnp.concatenate(das, axis=0)
     dq, dk, dv = [jnp.concatenate(parts, axis=0) for parts in zip(*grads)]
@@ -366,7 +376,7 @@
     made = [(grads_out, context, da)] + [(grads_into, u1, g) for g in (dv, dk, dq)]
     summed = []
     for maker, left, right in made:
-        ((own, other),) = maker(left, right, 1)
+        ((own, other),) = maker(left, right, 1, 1)
         got = swap_fsdp(other)
         summed.append(own() + got.astype(F32))
     g_attn, g_value, g_key, g_query = summed
@@ -375,14 +385,15 @@
     )
     du1 = tp_join(tp_half(term))
     h2 = h1 + tp_join(tp_half(dot(hidden, full_d.v)))
+    out_block = restored(h2 * keep, BF)
     dh1 = dy + norm_back(tp_join(du2_half), n2, rstd2)
     grad_input = restored(dh1 + norm_back(du1, n1, rstd1), F32)
-    out_block = restored(h2 * keep, BF)
-
-    def lay(parts):
-        box = Box((parts[0].shape[0] * len(parts), parts[0].shape[1]), F32)
+
+    def lay(parts, wide):
+        rows_each, span = parts[0].shape
+        box = Box((rows_each * len(parts) // wide, span * wide), F32)
         for j, p in enumerate(parts):
-            box.put(p, j * p.shape[0])
+            box.put(p, j // wide * rows_each, j % wide * span)
         return box.v
 
     return (
@@ -392,9 +403,9 @@
         g_key,
         g_value,
         g_attn,
-        lay(totals[4:8]),
-        lay(totals[8:12]),
-        lay(totals[0:4]),
+        lay(totals[4:8], 2),
+        lay(totals[8:12], 2),
+        lay(totals[0:4], 1),
     )
 
 

time: 1820 us -> 1370 us (0.75)
  waiting for transfers between devices: 1200 us -> 695 us
  starting transfers between devices: 232 us -> 268 us
    ppermute x56 -> x40, waiting for transfers between devices: 769 us -> 420 us  [the longest x16 237 us: reduce_chunks(): got = lax.ppermute(sent, 'ctx', pairs)]
    ppermute x23, waiting for transfers between devices: 384 us -> 233 us  [swap_fsdp(): return lax.ppermute(v, 'fsdp', [(0, 1), (1, 0)])]
    ppermute x56 -> x40, starting transfers between devices: 192 us -> 237 us  [the longest x16 178 us: reduce_chunks(): got = lax.ppermute(sent, 'ctx', pairs)]
    dynamic_update_slice x17 -> x29, local copies, waits for them, and re-layouts: 31.6 us -> 42.9 us  [put(): self.v = lax.dynamic_update_slice(self.v, piece.astype(self.v.dtype), at)]
  transfers between devices with their start and end apart: 95 -> 79, of which waited for: 48 -> 28; matrix products, arithmetic and copies ran while one was open for 12% -> 16% of each run, Pallas kernels for 3% -> 4%
where the time goes in v2:
time: 1370 us; the launch traced here: 1360 us
  waiting for transfers between devices  695 us (51%)
  starting transfers between devices  268 us (20%)
  matrix products  172 us (13%)
  local copies, waits for them, and re-layouts  88.7 us (6%)
  other arithmetic  74.5 us (5%)
  Pallas kernels  59.1 us (4%)
    ppermute x16, waiting for transfers between devices, reduce_chunks(): got = lax.ppermute(sent, 'ctx', pairs)  237 us
    ppermute x23, waiting for transfers between devices, swap_fsdp(): return lax.ppermute(v, 'fsdp', [(0, 1), (1, 0)])  233 us
    ppermute x12, waiting for transfers between devices, __init__(): self.got.append(lax.ppermute(piece, 'ctx', pairs))  183 us
    ppermute x16, starting transfers between devices, reduce_chunks(): got = lax.ppermute(sent, 'ctx', pairs)  178 us
    dot_general x32, matrix products, tdot(): lax.dot_general(left, right, (((0,), (0,)), ((), ())), preferred_element_...  81.1 us
    pallas_call x3, Pallas kernels, attention_call(): pl.pallas_call(lambda *refs: body(block, start, *refs), grid_spec=pltpu.P...  59.1 us
    ppermute x12, starting transfers between devices, __init__(): self.got.append(lax.ppermute(piece, 'ctx', pairs))  46.7 us
    dot_general x5, matrix products, ndot(): lax.dot_general(left, right, (((1,), (1,)), ((), ())), preferred_element_...  46.5 us
  transfers between devices with their start and end apart: 79, of which 28 were waited for; matrix products, arithmetic and copies ran while one was open for 16% of the time, Pallas kernels for 4%

profile of v2, /device:TPU:0, one launch (start us, length us, event | category | flops | bytes accessed | tf_op | source)
XLA Modules:
  0.0 1360.7 jit_solution(9816092545751380273)
XLA Ops:
  10.2 10.5 collective-permute-done
  21.8 20.5 %collective-permute-done.1 = bf16[128,2048]{1,0:T(8,128)(2,1)} collective-permute-done((bf16[128,2048]{1,0:T(8,128)(2,1)S(1)}, bf16[128,2048]{1,0:T(8,128)(2,1)}, u32[]{:S(2)}, u32[]{:S(2)}) %collective-permute-start.1) | collective-permute-done | bytes 524320 | tf_op jit(solution)/shard_map/ppermute | solution.py:156
  50.1 42.0 %collective-permute-done.3 = bf16[4,128,2048]{2,1,0:T(8,128)(2,1)} collective-permute-done((bf16[4,128,2048]{2,1,0:T(8,128)(2,1)S(1)}, bf16[4,128,2048]{2,1,0:T(8,128)(2,1)}, u32[]{:S(2)}, u32[]{:S(2)}) %collective-permute-start.3) | collective-permute-done | bytes 2097184 | tf_op jit(solution)/shard_map/ppermute | solution.py:130
  112.0 18.4 %dynamic_update_slice.142 = bf16[2048,4096]{1,0:T(8,128)(2,1)} pad(bf16[1024,2048]{1,0:T(8,128)(2,1)S(1)} %copy-done.20, bf16[]{:T(256)} %constant.111.clone.1), padding=0_1024x0_2048 | pad | bytes 20971522 | tf_op jit(solution)/shard_map/dynamic_update_slice | solution.py:171
  130.6 3.4 convert_multiply_fusion.2
  134.0 54.6 %collective-permute-done.8 = bf16[512,1024]{1,0:T(8,128)(2,1)} collective-permute-done((bf16[512,1024]{1,0:T(8,128)(2,1)S(1)}, bf16[512,1024]{1,0:T(8,128)(2,1)}, u32[]{:S(2)}, u32[]{:S(2)}) %collective-permute-start.8) | collective-permute-done | bytes 1048608 | tf_op jit(solution)/shard_map/ppermute | solution.py:125
  193.5 23.0 %fusion.refs_1_.refs_2_.refs_3_ = f32[2048,1536]{1,0:T(8,128)} fusion(bf16[1024,2048]{1,0:T(8,128)(2,1)} %collective-permute-done.4, bf16[1024,2048]{1,0:T(8,128)(2,1)} %bitcast.9, bf16[1024,512]{1,0:T(8,128)(2,1)} %collective-permute-done.7, bf16[1024,512]{1,0:T(8,128)(2,1)} %param.15, bf16[1024,512]{1,0:T(8,128)(2,1)} %collective-permute-done.6, ...), kind=kOutput, calls=%fused_computation.5 | convolution fusion | flops 12939427840 | bytes 27262976 | tf_op jit(solution)/shard_map/dot_general | solution.py:28
  216.5 23.0 %shard_map.169 = (bf16[2048,512]{1,0:T(8,128)(2,1)}, bf16[2048,512]{1,0:T(8,128)(2,1)}, bf16[2048,512]{1,0:T(8,128)(2,1)}, bf16[2048,512]{1,0:T(8,128)(2,1)}) custom-call(s32[2]{0:T(128)} %pad_add_fusion.refs_0_, f32[2048,1536]{1,0:T(8,128)} %fusion.refs_1_.refs_2_.refs_3_, f32[2048,1536]{1,0:T(8,128)} %fusion.refs_1_.refs_2_.refs_3_, ...), custom_call_target="tpu_custom_call" | custom-call | tf_op jit(solution)/shard_map/pallas_call | solution.py:111
  245.1 4.8 constant_dynamic-update-slice_fusion.3
  254.0 10.8 collective-permute-start.13
  273.3 16.9 %collective-permute-done.13 = bf16[256,2048]{1,0:T(8,128)(2,1)S(1)} collective-permute-done((bf16[256,2048]{1,0:T(8,128)(2,1)}, bf16[256,2048]{1,0:T(8,128)(2,1)S(1)}, u32[]{:S(2)}, u32[]{:S(2)}) %collective-permute-start.13) | collective-permute-done | bytes 1048608 | tf_op jit(solution)/shard_map/ppermute | solution.py:156
  292.1 43.0 %collective-permute-done.14 = bf16[256,2048]{1,0:T(8,128)(2,1)S(1)} collective-permute-done((bf16[256,2048]{1,0:T(8,128)(2,1)}, bf16[256,2048]{1,0:T(8,128)(2,1)S(1)}, u32[]{:S(2)}, u32[]{:S(2)}) %collective-permute-start.14) | collective-permute-done | bytes 1048608 | tf_op jit(solution)/shard_map/ppermute | solution.py:156
  336.3 23.6 %collective-permute-start.19 = (bf16[256,2048]{1,0:T(8,128)(2,1)S(1)}, bf16[256,2048]{1,0:T(8,128)(2,1)S(1)}, u32[]{:S(2)}, u32[]{:S(2)}) collective-permute-start(bf16[256,2048]{1,0:T(8,128)(2,1)S(1)} %collective-permute-done.16), channel_id=1, source_target_pairs={{0,12},{4,0},{8,4},{12,8},{1,13},{5,1},{9,5},{13,9},{2,14},{6,2},{... | collective-permute-start | bytes 3145736 | tf_op jit(solution)/shard_map/ppermute | solution.py:156
  363.7 61.2 %collective-permute-done.18 = bf16[256,2048]{1,0:T(8,128)(2,1)S(1)} collective-permute-done((bf16[256,2048]{1,0:T(8,128)(2,1)S(1)}, bf16[256,2048]{1,0:T(8,128)(2,1)S(1)}, u32[]{:S(2)}, u32[]{:S(2)}) %collective-permute-start.18) | collective-permute-done | bytes 1048608 | tf_op jit(solution)/shard_map/ppermute | solution.py:156
  426.0 21.2 %collective-permute-done.19 = bf16[256,2048]{1,0:T(8,128)(2,1)S(1)} collective-permute-done((bf16[256,2048]{1,0:T(8,128)(2,1)S(1)}, bf16[256,2048]{1,0:T(8,128)(2,1)S(1)}, u32[]{:S(2)}, u32[]{:S(2)}) %collective-permute-start.19) | collective-permute-done | bytes 1048608 | tf_op jit(solution)/shard_map/ppermute | solution.py:156
  451.0 3.4 copy-done.41
  459.0 3.4 fusion.162
  462.4 11.0 fusion.166
  473.4 4.8 fusion.20
  481.7 9.6 fusion.167
  491.4 14.0 %multiply_convert_fusion.1 = (bf16[512,2048]{1,0:T(8,128)(2,1)}, bf16[512,2048]{1,0:T(8,128)(2,1)}) fusion(f32[512,4096]{1,0:T(8,128)} %fusion.166, bf16[512,2048]{1,0:T(8,128)(2,1)} %get-tuple-element.50, bf16[2048,2048]{1,0:T(8,128)(2,1)} %copy-done.41), kind=kOutput, calls=%fused_computation.47 | convolution fusion | flops 4308598784 | bytes 23068672 | tf_op jit(solution)/shard_map/dot_general | solution.py:36
  516.1 15.2 %fusion.21 = f32[512,2048]{1,0:T(8,128)} fusion(bf16[2048,4096]{1,0:T(8,128)(2,1)} %constant_dynamic-update-slice_fusion.15, bf16[512,2048]{1,0:T(8,128)(2,1)} %get-tuple-element.48, bf16[512,2048]{1,0:T(8,128)(2,1)} %get-tuple-element.47), kind=kOutput, calls=%fused_computation.39 | convolution fusion | flops 8598323200 | bytes 25165824 | tf_op jit(solution)/shard_map/dot_general | solution.py:36
  549.6 13.9 %collective-permute-done.41 = bf16[512,1024]{1,0:T(8,128)(2,1)S(1)} collective-permute-done((bf16[512,1024]{1,0:T(8,128)(2,1)}, bf16[512,1024]{1,0:T(8,128)(2,1)S(1)}, u32[]{:S(2)}, u32[]{:S(2)}) %collective-permute-start.41) | collective-permute-done | bytes 1048608 | tf_op jit(solution)/shard_map/ppermute | solution.py:125
  565.8 42.7 %collective-permute-done.49 = bf16[512,1024]{1,0:T(8,128)(2,1)S(1)} collective-permute-done((bf16[512,1024]{1,0:T(8,128)(2,1)S(1)}, bf16[512,1024]{1,0:T(8,128)(2,1)S(1)}, u32[]{:S(2)}, u32[]{:S(2)}) %collective-permute-start.49) | collective-permute-done | bytes 1048608 | tf_op jit(solution)/shard_map/ppermute | solution.py:125
  609.8 21.2 %collective-permute-done.57 = bf16[512,1024]{1,0:T(8,128)(2,1)S(1)} collective-permute-done((bf16[512,1024]{1,0:T(8,128)(2,1)S(1)}, bf16[512,1024]{1,0:T(8,128)(2,1)S(1)}, u32[]{:S(2)}, u32[]{:S(2)}) %collective-permute-start.57) | collective-permute-done | bytes 1048608 | tf_op jit(solution)/shard_map/ppermute | solution.py:125
  633.2 20.2 %collective-permute-done.65 = bf16[512,1024]{1,0:T(8,128)(2,1)S(1)} collective-permute-done((bf16[512,1024]{1,0:T(8,128)(2,1)S(1)}, bf16[512,1024]{1,0:T(8,128)(2,1)S(1)}, u32[]{:S(2)}, u32[]{:S(2)}) %collective-permute-start.65) | collective-permute-done | bytes 1048608 | tf_op jit(solution)/shard_map/ppermute | solution.py:125
  658.8 20.7 %collective-permute-done.42 = bf16[512,1024]{1,0:T(8,128)(2,1)S(1)} collective-permute-done((bf16[512,1024]{1,0:T(8,128)(2,1)S(1)}, bf16[512,1024]{1,0:T(8,128)(2,1)S(1)}, u32[]{:S(2)}, u32[]{:S(2)}) %collective-permute-start.42) | collective-permute-done | bytes 1048608 | tf_op jit(solution)/shard_map/ppermute | solution.py:211
  680.4 21.5 %collective-permute-done.50 = bf16[512,1024]{1,0:T(8,128)(2,1)S(1)} collective-permute-done((bf16[512,1024]{1,0:T(8,128)(2,1)S(1)}, bf16[512,1024]{1,0:T(8,128)(2,1)S(1)}, u32[]{:S(2)}, u32[]{:S(2)}) %collective-permute-start.50) | collective-permute-done | bytes 1048608 | tf_op jit(solution)/shard_map/ppermute | solution.py:211
  705.8 24.2 %collective-permute-done.58 = bf16[512,1024]{1,0:T(8,128)(2,1)S(1)} collective-permute-done((bf16[512,1024]{1,0:T(8,128)(2,1)S(1)}, bf16[512,1024]{1,0:T(8,128)(2,1)S(1)}, u32[]{:S(2)}, u32[]{:S(2)}) %collective-permute-start.58) | collective-permute-done | bytes 1048608 | tf_op jit(solution)/shard_map/ppermute | solution.py:211
  730.9 35.8 %collective-permute-done.66 = bf16[512,1024]{1,0:T(8,128)(2,1)S(1)} collective-permute-done((bf16[512,1024]{1,0:T(8,128)(2,1)S(1)}, bf16[512,1024]{1,0:T(8,128)(2,1)S(1)}, u32[]{:S(2)}, u32[]{:S(2)}) %collective-permute-start.66) | collective-permute-done | bytes 1048608 | tf_op jit(solution)/shard_map/ppermute | solution.py:211
  768.1 9.9 collective-permute-done.29
  789.0 18.0 %collective-permute-done.56 = bf16[512,1024]{1,0:T(8,128)(2,1)S(1)} collective-permute-done((bf16[512,1024]{1,0:T(8,128)(2,1)S(1)}, bf16[512,1024]{1,0:T(8,128)(2,1)S(1)}, u32[]{:S(2)}, u32[]{:S(2)}) %collective-permute-start.56) | collective-permute-done | bytes 1048608 | tf_op jit(solution)/shard_map/ppermute | solution.py:125
  808.5 40.2 %collective-permute-start.44 = (bf16[512,1024]{1,0:T(8,128)(2,1)S(1)}, bf16[512,1024]{1,0:T(8,128)(2,1)S(1)}, u32[]{:S(2)}, u32[]{:S(2)}) collective-permute-start(bf16[512,1024]{1,0:T(8,128)(2,1)S(1)} %get-tuple-element.79), channel_id=1, source_target_pairs={{0,4},{4,0},{8,12},{12,8},{1,5},{5,1},{9,13},{13,9},{2,6},{6,2},{1... | collective-permute-start | bytes 3145736 | tf_op jit(solution)/shard_map/ppermute | solution.py:211
  850.6 18.8 %collective-permute-start.60 = (bf16[512,1024]{1,0:T(8,128)(2,1)}, bf16[512,1024]{1,0:T(8,128)(2,1)S(1)}, u32[]{:S(2)}, u32[]{:S(2)}) collective-permute-start(bf16[512,1024]{1,0:T(8,128)(2,1)} %get-tuple-element.83), channel_id=1, source_target_pairs={{0,4},{4,0},{8,12},{12,8},{1,5},{5,1},{9,13},{13,9},{2,6},{6,2},{1... | collective-permute-start | bytes 3145736 | tf_op jit(solution)/shard_map/ppermute | solution.py:211
  876.4 18.8 %collective-permute-done.52 = bf16[512,1024]{1,0:T(8,128)(2,1)S(1)} collective-permute-done((bf16[512,1024]{1,0:T(8,128)(2,1)}, bf16[512,1024]{1,0:T(8,128)(2,1)S(1)}, u32[]{:S(2)}, u32[]{:S(2)}) %collective-permute-start.52) | collective-permute-done | bytes 1048608 | tf_op jit(solution)/shard_map/ppermute | solution.py:211
  897.6 20.0 %collective-permute-done.60 = bf16[512,1024]{1,0:T(8,128)(2,1)S(1)} collective-permute-done((bf16[512,1024]{1,0:T(8,128)(2,1)}, bf16[512,1024]{1,0:T(8,128)(2,1)S(1)}, u32[]{:S(2)}, u32[]{:S(2)}) %collective-permute-start.60) | collective-permute-done | bytes 1048608 | tf_op jit(solution)/shard_map/ppermute | solution.py:211
  920.1 16.1 %collective-permute-done.68 = bf16[512,1024]{1,0:T(8,128)(2,1)S(1)} collective-permute-done((bf16[512,1024]{1,0:T(8,128)(2,1)}, bf16[512,1024]{1,0:T(8,128)(2,1)S(1)}, u32[]{:S(2)}, u32[]{:S(2)}) %collective-permute-start.68) | collective-permute-done | bytes 1048608 | tf_op jit(solution)/shard_map/ppermute | solution.py:211
  944.3 3.3 convolution_convert_fusion.16.refs_4_
  947.6 17.7 %shard_map.170 = (bf16[1024,512]{1,0:T(8,128)(2,1)}, bf16[1024,512]{1,0:T(8,128)(2,1)}, bf16[1024,512]{1,0:T(8,128)(2,1)}) custom-call(s32[2]{0:T(128)} %pad_add_fusion.refs_0_, bf16[2048,512]{1,0:T(8,128)(2,1)} %get-tuple-element.24.refs_1_, bf16[2048,512]{1,0:T(8,128)(2,1)} %get-tuple-element.25.refs_2_, bf16[2048,512]{1,0:T(8,128)(2,1)} %get-tuple-element.26.refs_3_, ...), custom_call_target="tpu_custom_call" | custom-call | tf_op jit(solution)/shard_map/pallas_call | solution.py:111
  974.3 23.6 %collective-permute-start.46 = (bf16[512,1024]{1,0:T(8,128)(2,1)S(1)}, bf16[512,1024]{1,0:T(8,128)(2,1)S(1)}, u32[]{:S(2)}, u32[]{:S(2)}) collective-permute-start(bf16[512,1024]{1,0:T(8,128)(2,1)S(1)} %get-tuple-element.93), channel_id=1, source_target_pairs={{0,4},{4,0},{8,12},{12,8},{1,5},{5,1},{9,13},{13,9},{2,6},{6,2},{1... | collective-permute-start | bytes 3145736 | tf_op jit(solution)/shard_map/ppermute | solution.py:211
  1000.9 12.1 collective-permute-start.70
  1016.1 18.1 %collective-permute-start.54 = (bf16[512,1024]{1,0:T(8,128)(2,1)S(1)}, bf16[512,1024]{1,0:T(8,128)(2,1)S(1)}, u32[]{:S(2)}, u32[]{:S(2)}) collective-permute-start(bf16[512,1024]{1,0:T(8,128)(2,1)S(1)} %get-tuple-element.91), channel_id=1, source_target_pairs={{0,4},{4,0},{8,12},{12,8},{1,5},{5,1},{9,13},{13,9},{2,6},{6,2},{1... | collective-permute-start | bytes 3145736 | tf_op jit(solution)/shard_map/ppermute | solution.py:211
  1038.9 44.7 %collective-permute-done.54 = bf16[512,1024]{1,0:T(8,128)(2,1)S(1)} collective-permute-done((bf16[512,1024]{1,0:T(8,128)(2,1)S(1)}, bf16[512,1024]{1,0:T(8,128)(2,1)S(1)}, u32[]{:S(2)}, u32[]{:S(2)}) %collective-permute-start.54) | collective-permute-done | bytes 1048608 | tf_op jit(solution)/shard_map/ppermute | solution.py:211
  1090.7 8.1 collective-permute-start.72
  1100.3 36.4 %collective-permute-start.74 = (bf16[512,1024]{1,0:T(8,128)(2,1)S(1)}, bf16[512,1024]{1,0:T(8,128)(2,1)S(1)}, u32[]{:S(2)}, u32[]{:S(2)}) collective-permute-start(bf16[512,1024]{1,0:T(8,128)(2,1)S(1)} %add_convert_fusion.4), channel_id=1, source_target_pairs={{0,4},{4,0},{8,12},{12,8},{1,5},{5,1},{9,13},{13,9},{2,6},{6,2},{1... | collective-permute-start | bytes 3145736 | tf_op jit(solution)/shard_map/ppermute | solution.py:211
  1137.1 15.2 %collective-permute-start.76 = (bf16[512,1024]{1,0:T(8,128)(2,1)S(1)}, bf16[512,1024]{1,0:T(8,128)(2,1)S(1)}, u32[]{:S(2)}, u32[]{:S(2)}) collective-permute-start(bf16[512,1024]{1,0:T(8,128)(2,1)S(1)} %add_convert_fusion.2), channel_id=1, source_target_pairs={{0,4},{4,0},{8,12},{12,8},{1,5},{5,1},{9,13},{13,9},{2,6},{6,2},{1... | collective-permute-start | bytes 3145736 | tf_op jit(solution)/shard_map/ppermute | solution.py:211
  1152.9 4.5 pad_convert_fusion.1
  1159.1 17.2 %collective-permute-done.76 = bf16[512,1024]{1,0:T(8,128)(2,1)S(1)} collective-permute-done((bf16[512,1024]{1,0:T(8,128)(2,1)S(1)}, bf16[512,1024]{1,0:T(8,128)(2,1)S(1)}, u32[]{:S(2)}, u32[]{:S(2)}) %collective-permute-start.76) | collective-permute-done | bytes 1048608 | tf_op jit(solution)/shard_map/ppermute | solution.py:211
  1178.0 16.4 %collective-permute-done.78 = bf16[512,1024]{1,0:T(8,128)(2,1)S(1)} collective-permute-done((bf16[512,1024]{1,0:T(8,128)(2,1)S(1)}, bf16[512,1024]{1,0:T(8,128)(2,1)S(1)}, u32[]{:S(2)}, u32[]{:S(2)}) %collective-permute-start.78) | collective-permute-done | bytes 1048608 | tf_op jit(solution)/shard_map/ppermute | solution.py:211
  1198.2 3.4 convolution_convert_fusion.15.refs_4_
  1201.6 18.3 %shard_map.171 = (bf16[1024,512]{1,0:T(8,128)(2,1)}, bf16[1024,512]{1,0:T(8,128)(2,1)}, bf16[1024,512]{1,0:T(8,128)(2,1)}) custom-call(s32[2]{0:T(128)} %pad_add_fusion.refs_0_, bf16[2048,512]{1,0:T(8,128)(2,1)} %get-tuple-element.24.refs_1_, bf16[2048,512]{1,0:T(8,128)(2,1)} %get-tuple-element.25.refs_2_, bf16[2048,512]{1,0:T(8,128)(2,1)} %get-tuple-element.26.refs_3_, ...), custom_call_target="tpu_custom_call" | custom-call | tf_op jit(solution)/shard_map/pallas_call | solution.py:111
  1223.5 10.6 fusion.30
  1234.3 4.6 convolution_convert_fusion.14
  1239.5 4.6 convolution_convert_fusion.13
  1245.7 5.3 convolution_convert_fusion.12
  1255.9 9.1 collective-permute-done.35
  1266.5 5.9 convert_add_fusion.4
  1272.4 15.0 %collective-permute-done.36 = bf16[1024,512]{1,0:T(8,128)(2,1)S(1)} collective-permute-done((bf16[1024,512]{1,0:T(8,128)(2,1)S(1)}, bf16[1024,512]{1,0:T(8,128)(2,1)S(1)}, u32[]{:S(2)}, u32[]{:S(2)}) %collective-permute-start.36) | collective-permute-done | bytes 1048608 | tf_op jit(solution)/shard_map/ppermute | solution.py:125
  1287.5 5.9 convert_add_fusion.3
  1293.9 38.1 %collective-permute-done.38 = bf16[512,1024]{1,0:T(8,128)(2,1)S(1)} collective-permute-done((bf16[512,1024]{1,0:T(8,128)(2,1)S(1)}, bf16[512,1024]{1,0:T(8,128)(2,1)S(1)}, u32[]{:S(2)}, u32[]{:S(2)}) %collective-permute-start.38) | collective-permute-done | bytes 1048608 | tf_op jit(solution)/shard_map/ppermute | solution.py:125
  1331.9 3.8 convert_add_fusion.1
  1335.8 6.1 convert_add_fusion.2
  1341.9 6.7 convert_reduce_fusion
  1352.3 5.1 fusion.6
  (409 shorter events, 217.9 us)
Async XLA Ops:
  5.6 36.7 %collective-permute-start.1 = (bf16[128,2048]{1,0:T(8,128)(2,1)S(1)}, bf16[128,2048]{1,0:T(8,128)(2,1)}, u32[]{:S(2)}, u32[]{:S(2)}) collective-permute-start(bf16[128,2048]{1,0:T(8,128)(2,1)S(1)} %fusion.45), channel_id=1, source_target_pairs={{0,8},{4,12},{8,0},{12,4},{1,9},{5,13},{9,1},{13,5},{2,10},{6,14},... | collective-permute-start | bytes 1572872 | tf_op jit(solution)/shard_map/ppermute | solution.py:156
  8.2 35.2 %collective-permute-start.2 = (bf16[128,2048]{1,0:T(8,128)(2,1)S(1)}, bf16[128,2048]{1,0:T(8,128)(2,1)}, u32[]{:S(2)}, u32[]{:S(2)}) collective-permute-start(bf16[128,2048]{1,0:T(8,128)(2,1)S(1)} %fusion.45), channel_id=1, source_target_pairs={{0,12},{4,0},{8,4},{12,8},{1,13},{5,1},{9,5},{13,9},{2,14},{6,2},{... | collective-permute-start | bytes 1572872 | tf_op jit(solution)/shard_map/ppermute | solution.py:156
  44.5 47.6 %collective-permute-start.3 = (bf16[4,128,2048]{2,1,0:T(8,128)(2,1)S(1)}, bf16[4,128,2048]{2,1,0:T(8,128)(2,1)}, u32[]{:S(2)}, u32[]{:S(2)}) collective-permute-start(bf16[4,128,2048]{2,1,0:T(8,128)(2,1)S(1)} %bitcast_dynamic-update-slice_fusion.8), channel_id=1, source_target_pairs={{0,2},{1,3},{2,0},{3,1},{4,6},{5,7},{6,4},{7,5},{8,10},{9,11},{10,... | collective-permute-start | bytes 6291464 | tf_op jit(solution)/shard_map/ppermute | solution.py:130
  95.3 98.2 %collective-permute-start.4 = (bf16[1024,2048]{1,0:T(8,128)(2,1)}, bf16[1024,2048]{1,0:T(8,128)(2,1)}, u32[]{:S(2)}, u32[]{:S(2)}) collective-permute-start(bf16[1024,2048]{1,0:T(8,128)(2,1)} %bitcast.9), channel_id=1, source_target_pairs={{0,1},{1,0},{2,3},{3,2},{4,5},{5,4},{6,7},{7,6},{8,9},{9,8},{10,11... | collective-permute-start | bytes 12582920 | tf_op jit(solution)/shard_map/ppermute | solution.py:130
  95.3 96.1 %collective-permute-start.7 = (bf16[1024,512]{1,0:T(8,128)(2,1)}, bf16[1024,512]{1,0:T(8,128)(2,1)}, u32[]{:S(2)}, u32[]{:S(2)}) collective-permute-start(bf16[1024,512]{1,0:T(8,128)(2,1)} %param.15), channel_id=1, source_target_pairs={{0,16},{16,0},{1,17},{17,1},{2,18},{18,2},{3,19},{19,3},{4,20},{20... | collective-permute-start | bytes 3145736 | tf_op jit(solution)/shard_map/ppermute | solution.py:125
  96.8 95.2 %collective-permute-start.6 = (bf16[1024,512]{1,0:T(8,128)(2,1)}, bf16[1024,512]{1,0:T(8,128)(2,1)}, u32[]{:S(2)}, u32[]{:S(2)}) collective-permute-start(bf16[1024,512]{1,0:T(8,128)(2,1)} %param.14), channel_id=1, source_target_pairs={{0,16},{16,0},{1,17},{17,1},{2,18},{18,2},{3,19},{19,3},{4,20},{20... | collective-permute-start | bytes 3145736 | tf_op jit(solution)/shard_map/ppermute | solution.py:125
  97.3 96.2 %collective-permute-start.5 = (bf16[1024,512]{1,0:T(8,128)(2,1)}, bf16[1024,512]{1,0:T(8,128)(2,1)}, u32[]{:S(2)}, u32[]{:S(2)}) collective-permute-start(bf16[1024,512]{1,0:T(8,128)(2,1)} %param.13), channel_id=1, source_target_pairs={{0,16},{16,0},{1,17},{17,1},{2,18},{18,2},{3,19},{19,3},{4,20},{20... | collective-permute-start | bytes 3145736 | tf_op jit(solution)/shard_map/ppermute | solution.py:125
  98.8 89.8 %collective-permute-start.8 = (bf16[512,1024]{1,0:T(8,128)(2,1)S(1)}, bf16[512,1024]{1,0:T(8,128)(2,1)}, u32[]{:S(2)}, u32[]{:S(2)}) collective-permute-start(bf16[512,1024]{1,0:T(8,128)(2,1)S(1)} %copy-done.46), channel_id=1, source_target_pairs={{0,16},{16,0},{1,17},{17,1},{2,18},{18,2},{3,19},{19,3},{4,20},{20... | collective-permute-start | bytes 3145736 | tf_op jit(solution)/shard_map/ppermute | solution.py:125
  188.6 65.4 %collective-permute-start.12 = (bf16[256,2048]{1,0:T(8,128)(2,1)}, bf16[256,2048]{1,0:T(8,128)(2,1)}, u32[]{:S(2)}, u32[]{:S(2)}) collective-permute-start(bf16[256,2048]{1,0:T(8,128)(2,1)} %constant_dynamic-slice_fusion.8), channel_id=1, source_target_pairs={{0,16},{16,0},{1,17},{17,1},{2,18},{18,2},{3,19},{19,3},{4,20},{20... | collective-permute-start | bytes 3145736 | tf_op jit(solution)/shard_map/ppermute | solution.py:125
  191.4 77.9 %collective-permute-start.16 = (bf16[256,2048]{1,0:T(8,128)(2,1)}, bf16[256,2048]{1,0:T(8,128)(2,1)S(1)}, u32[]{:S(2)}, u32[]{:S(2)}) collective-permute-start(bf16[256,2048]{1,0:T(8,128)(2,1)} %constant_dynamic-slice_fusion.7), channel_id=1, source_target_pairs={{0,16},{16,0},{1,17},{17,1},{2,18},{18,2},{3,19},{19,3},{4,20},{20... | collective-permute-start | bytes 3145736 | tf_op jit(solution)/shard_map/ppermute | solution.py:125
  192.0 256.4 %collective-permute-start.20 = (bf16[2048,1024]{1,0:T(8,128)(2,1)}, bf16[2048,1024]{1,0:T(8,128)(2,1)}, u32[]{:S(2)}, u32[]{:S(2)}) collective-permute-start(bf16[2048,1024]{1,0:T(8,128)(2,1)} %param.19), channel_id=1, source_target_pairs={{0,16},{16,0},{1,17},{17,1},{2,18},{18,2},{3,19},{19,3},{4,20},{20... | collective-permute-start | bytes 12582920 | tf_op jit(solution)/shard_map/ppermute | solution.py:125
  254.0 36.2 %collective-permute-start.13 = (bf16[256,2048]{1,0:T(8,128)(2,1)}, bf16[256,2048]{1,0:T(8,128)(2,1)S(1)}, u32[]{:S(2)}, u32[]{:S(2)}) collective-permute-start(bf16[256,2048]{1,0:T(8,128)(2,1)} %collective-permute-done.12), channel_id=1, source_target_pairs={{0,4},{4,8},{8,12},{12,0},{1,5},{5,9},{9,13},{13,1},{2,6},{6,10},{... | collective-permute-start | bytes 3145736 | tf_op jit(solution)/shard_map/ppermute | solution.py:156
  265.0 70.2 %collective-permute-start.14 = (bf16[256,2048]{1,0:T(8,128)(2,1)}, bf16[256,2048]{1,0:T(8,128)(2,1)S(1)}, u32[]{:S(2)}, u32[]{:S(2)}) collective-permute-start(bf16[256,2048]{1,0:T(8,128)(2,1)} %collective-permute-done.12), channel_id=1, source_target_pairs={{0,8},{4,12},{8,0},{12,4},{1,9},{5,13},{9,1},{13,5},{2,10},{6,14},... | collective-permute-start | bytes 3145736 | tf_op jit(solution)/shard_map/ppermute | solution.py:156
  266.7 69.6 %collective-permute-start.15 = (bf16[256,2048]{1,0:T(8,128)(2,1)}, bf16[256,2048]{1,0:T(8,128)(2,1)S(1)}, u32[]{:S(2)}, u32[]{:S(2)}) collective-permute-start(bf16[256,2048]{1,0:T(8,128)(2,1)} %collective-permute-done.12), channel_id=1, source_target_pairs={{0,12},{4,0},{8,4},{12,8},{1,13},{5,1},{9,5},{13,9},{2,14},{6,2},{... | collective-permute-start | bytes 3145736 | tf_op jit(solution)/shard_map/ppermute | solution.py:156
  269.3 92.8 %collective-permute-start.10 = (bf16[256,2048]{1,0:T(8,128)(2,1)S(1)}, bf16[256,2048]{1,0:T(8,128)(2,1)S(1)}, u32[]{:S(2)}, u32[]{:S(2)}) collective-permute-start(bf16[256,2048]{1,0:T(8,128)(2,1)S(1)} %fusion.29), channel_id=1, source_target_pairs={{0,2},{1,3},{2,0},{3,1},{4,6},{5,7},{6,4},{7,5},{8,10},{9,11},{10,... | collective-permute-start | bytes 3145736 | tf_op jit(solution)/shard_map/ppermute | solution.py:130
  290.2 72.4 %collective-permute-start.17 = (bf16[256,2048]{1,0:T(8,128)(2,1)S(1)}, bf16[256,2048]{1,0:T(8,128)(2,1)S(1)}, u32[]{:S(2)}, u32[]{:S(2)}) collective-permute-start(bf16[256,2048]{1,0:T(8,128)(2,1)S(1)} %collective-permute-done.16), channel_id=1, source_target_pairs={{0,4},{4,8},{8,12},{12,0},{1,5},{5,9},{9,13},{13,1},{2,6},{6,10},{... | collective-permute-start | bytes 3145736 | tf_op jit(solution)/shard_map/ppermute | solution.py:156
  335.1 89.7 %collective-permute-start.18 = (bf16[256,2048]{1,0:T(8,128)(2,1)S(1)}, bf16[256,2048]{1,0:T(8,128)(2,1)S(1)}, u32[]{:S(2)}, u32[]{:S(2)}) collective-permute-start(bf16[256,2048]{1,0:T(8,128)(2,1)S(1)} %collective-permute-done.16), channel_id=1, source_target_pairs={{0,8},{4,12},{8,0},{12,4},{1,9},{5,13},{9,1},{13,5},{2,10},{6,14},... | collective-permute-start | bytes 3145736 | tf_op jit(solution)/shard_map/ppermute | solution.py:156
  336.3 111.0 %collective-permute-start.19 = (bf16[256,2048]{1,0:T(8,128)(2,1)S(1)}, bf16[256,2048]{1,0:T(8,128)(2,1)S(1)}, u32[]{:S(2)}, u32[]{:S(2)}) collective-permute-start(bf16[256,2048]{1,0:T(8,128)(2,1)S(1)} %collective-permute-done.16), channel_id=1, source_target_pairs={{0,12},{4,0},{8,4},{12,8},{1,13},{5,1},{9,5},{13,9},{2,14},{6,2},{... | collective-permute-start | bytes 3145736 | tf_op jit(solution)/shard_map/ppermute | solution.py:156
  362.5 88.5 %collective-permute-start.11 = (bf16[256,2048]{1,0:T(8,128)(2,1)S(1)}, bf16[256,2048]{1,0:T(8,128)(2,1)S(1)}, u32[]{:S(2)}, u32[]{:S(2)}) collective-permute-start(bf16[256,2048]{1,0:T(8,128)(2,1)S(1)} %add_convert_fusion.39), channel_id=1, source_target_pairs={{0,1},{1,0},{2,3},{3,2},{4,5},{5,4},{6,7},{7,6},{8,9},{9,8},{10,11... | collective-permute-start | bytes 3145736 | tf_op jit(solution)/shard_map/ppermute | solution.py:130
  537.3 26.2 %collective-permute-start.41 = (bf16[512,1024]{1,0:T(8,128)(2,1)}, bf16[512,1024]{1,0:T(8,128)(2,1)S(1)}, u32[]{:S(2)}, u32[]{:S(2)}) collective-permute-start(bf16[512,1024]{1,0:T(8,128)(2,1)} %convolution_convert_fusion.9), channel_id=1, source_target_pairs={{0,16},{16,0},{1,17},{17,1},{2,18},{18,2},{3,19},{19,3},{4,20},{20... | collective-permute-start | bytes 3145736 | tf_op jit(solution)/shard_map/ppermute | solution.py:125
  537.8 244.7 %collective-permute-start.40 = (bf16[512,1024]{1,0:T(8,128)(2,1)}, bf16[512,1024]{1,0:T(8,128)(2,1)S(1)}, u32[]{:S(2)}, u32[]{:S(2)}) collective-permute-start(bf16[512,1024]{1,0:T(8,128)(2,1)} %convolution_convert_fusion.10), channel_id=1, source_target_pairs={{0,16},{16,0},{1,17},{17,1},{2,18},{18,2},{3,19},{19,3},{4,20},{20... | collective-permute-start | bytes 3145736 | tf_op jit(solution)/shard_map/ppermute | solution.py:125
  539.3 69.2 %collective-permute-start.49 = (bf16[512,1024]{1,0:T(8,128)(2,1)S(1)}, bf16[512,1024]{1,0:T(8,128)(2,1)S(1)}, u32[]{:S(2)}, u32[]{:S(2)}) collective-permute-start(bf16[512,1024]{1,0:T(8,128)(2,1)S(1)} %copy-done.65), channel_id=1, source_target_pairs={{0,16},{16,0},{1,17},{17,1},{2,18},{18,2},{3,19},{19,3},{4,20},{20... | collective-permute-start | bytes 3145736 | tf_op jit(solution)/shard_map/ppermute | solution.py:125
  546.9 84.1 %collective-permute-start.57 = (bf16[512,1024]{1,0:T(8,128)(2,1)S(1)}, bf16[512,1024]{1,0:T(8,128)(2,1)S(1)}, u32[]{:S(2)}, u32[]{:S(2)}) collective-permute-start(bf16[512,1024]{1,0:T(8,128)(2,1)S(1)} %copy-done.64), channel_id=1, source_target_pairs={{0,16},{16,0},{1,17},{17,1},{2,18},{18,2},{3,19},{19,3},{4,20},{20... | collective-permute-start | bytes 3145736 | tf_op jit(solution)/shard_map/ppermute | solution.py:125
  548.7 104.7 %collective-permute-start.65 = (bf16[512,1024]{1,0:T(8,128)(2,1)S(1)}, bf16[512,1024]{1,0:T(8,128)(2,1)S(1)}, u32[]{:S(2)}, u32[]{:S(2)}) collective-permute-start(bf16[512,1024]{1,0:T(8,128)(2,1)S(1)} %convolution_convert_fusion), channel_id=1, source_target_pairs={{0,16},{16,0},{1,17},{17,1},{2,18},{18,2},{3,19},{19,3},{4,20},{20... | collective-permute-start | bytes 3145736 | tf_op jit(solution)/shard_map/ppermute | solution.py:125
  563.5 91.2 %collective-permute-start.25 = (bf16[256,2048]{1,0:T(8,128)(2,1)S(1)}, bf16[256,2048]{1,0:T(8,128)(2,1)S(1)}, u32[]{:S(2)}, u32[]{:S(2)}) collective-permute-start(bf16[256,2048]{1,0:T(8,128)(2,1)S(1)} %fusion.27), channel_id=1, source_target_pairs={{0,2},{1,3},{2,0},{3,1},{4,6},{5,7},{6,4},{7,5},{8,10},{9,11},{10,... | collective-permute-start | bytes 3145736 | tf_op jit(solution)/shard_map/ppermute | solution.py:130
  608.5 177.3 %collective-permute-start.48 = (bf16[512,1024]{1,0:T(8,128)(2,1)}, bf16[512,1024]{1,0:T(8,128)(2,1)S(1)}, u32[]{:S(2)}, u32[]{:S(2)}) collective-permute-start(bf16[512,1024]{1,0:T(8,128)(2,1)} %convolution_convert_fusion.7), channel_id=1, source_target_pairs={{0,16},{16,0},{1,17},{17,1},{2,18},{18,2},{3,19},{19,3},{4,20},{20... | collective-permute-start | bytes 3145736 | tf_op jit(solution)/shard_map/ppermute | solution.py:125
  631.0 72.0 %collective-permute-start.22 = (bf16[256,2048]{1,0:T(8,128)(2,1)S(1)}, bf16[256,2048]{1,0:T(8,128)(2,1)S(1)}, u32[]{:S(2)}, u32[]{:S(2)}) collective-permute-start(bf16[256,2048]{1,0:T(8,128)(2,1)S(1)} %fusion.28), channel_id=1, source_target_pairs={{0,2},{1,3},{2,0},{3,1},{4,6},{5,7},{6,4},{7,5},{8,10},{9,11},{10,... | collective-permute-start | bytes 3145736 | tf_op jit(solution)/shard_map/ppermute | solution.py:130
  654.8 47.2 %collective-permute-start.50 = (bf16[512,1024]{1,0:T(8,128)(2,1)S(1)}, bf16[512,1024]{1,0:T(8,128)(2,1)S(1)}, u32[]{:S(2)}, u32[]{:S(2)}) collective-permute-start(bf16[512,1024]{1,0:T(8,128)(2,1)S(1)} %add_convert_fusion.26), channel_id=1, source_target_pairs={{0,4},{4,0},{8,12},{12,8},{1,5},{5,1},{9,13},{13,9},{2,6},{6,2},{1... | collective-permute-start | bytes 3145736 | tf_op jit(solution)/shard_map/ppermute | solution.py:211
  679.5 50.6 %collective-permute-start.58 = (bf16[512,1024]{1,0:T(8,128)(2,1)S(1)}, bf16[512,1024]{1,0:T(8,128)(2,1)S(1)}, u32[]{:S(2)}, u32[]{:S(2)}) collective-permute-start(bf16[512,1024]{1,0:T(8,128)(2,1)S(1)} %add_convert_fusion.19), channel_id=1, source_target_pairs={{0,4},{4,0},{8,12},{12,8},{1,5},{5,1},{9,13},{13,9},{2,6},{6,2},{1... | collective-permute-start | bytes 3145736 | tf_op jit(solution)/shard_map/ppermute | solution.py:211
  701.9 64.8 %collective-permute-start.66 = (bf16[512,1024]{1,0:T(8,128)(2,1)S(1)}, bf16[512,1024]{1,0:T(8,128)(2,1)S(1)}, u32[]{:S(2)}, u32[]{:S(2)}) collective-permute-start(bf16[512,1024]{1,0:T(8,128)(2,1)S(1)} %add_convert_fusion.12), channel_id=1, source_target_pairs={{0,4},{4,0},{8,12},{12,8},{1,5},{5,1},{9,13},{13,9},{2,6},{6,2},{1... | collective-permute-start | bytes 3145736 | tf_op jit(solution)/shard_map/ppermute | solution.py:211
  702.9 64.2 %collective-permute-start.27 = (bf16[128,2048]{1,0:T(8,128)(2,1)S(1)}, bf16[128,2048]{1,0:T(8,128)(2,1)S(1)}, u32[]{:S(2)}, u32[]{:S(2)}) collective-permute-start(bf16[128,2048]{1,0:T(8,128)(2,1)S(1)} %get-tuple-element.44), channel_id=1, source_target_pairs={{0,4},{4,8},{8,12},{12,0},{1,5},{5,9},{9,13},{13,1},{2,6},{6,10},{... | collective-permute-start | bytes 1572872 | tf_op jit(solution)/shard_map/ppermute | solution.py:156
  730.0 37.3 %collective-permute-start.28 = (bf16[128,2048]{1,0:T(8,128)(2,1)S(1)}, bf16[128,2048]{1,0:T(8,128)(2,1)S(1)}, u32[]{:S(2)}, u32[]{:S(2)}) collective-permute-start(bf16[128,2048]{1,0:T(8,128)(2,1)S(1)} %get-tuple-element.44), channel_id=1, source_target_pairs={{0,8},{4,12},{8,0},{12,4},{1,9},{5,13},{9,1},{13,5},{2,10},{6,14},... | collective-permute-start | bytes 1572872 | tf_op jit(solution)/shard_map/ppermute | solution.py:156
  782.5 68.0 %collective-permute-start.64 = (bf16[512,1024]{1,0:T(8,128)(2,1)S(1)}, bf16[512,1024]{1,0:T(8,128)(2,1)S(1)}, u32[]{:S(2)}, u32[]{:S(2)}) collective-permute-start(bf16[512,1024]{1,0:T(8,128)(2,1)S(1)} %copy-done.62), channel_id=1, source_target_pairs={{0,16},{16,0},{1,17},{17,1},{2,18},{18,2},{3,19},{19,3},{4,20},{20... | collective-permute-start | bytes 3145736 | tf_op jit(solution)/shard_map/ppermute | solution.py:125
  785.8 64.8 %collective-permute-start.67 = (bf16[512,1024]{1,0:T(8,128)(2,1)S(1)}, bf16[512,1024]{1,0:T(8,128)(2,1)S(1)}, u32[]{:S(2)}, u32[]{:S(2)}) collective-permute-start(bf16[512,1024]{1,0:T(8,128)(2,1)S(1)} %add_convert_fusion.11), channel_id=1, source_target_pairs={{4,8},{8,4},{5,9},{9,5},{6,10},{10,6},{7,11},{11,7},{20,24},{24,20... | collective-permute-start | bytes 3145736 | tf_op jit(solution)/shard_map/ppermute | solution.py:216
  786.5 178.8 %collective-permute-start.63 = (bf16[512,1024]{1,0:T(8,128)(2,1)}, bf16[512,1024]{1,0:T(8,128)(2,1)}, u32[]{:S(2)}, u32[]{:S(2)}) collective-permute-start(bf16[512,1024]{1,0:T(8,128)(2,1)} %convolution_convert_fusion.2), channel_id=1, source_target_pairs={{0,16},{16,0},{1,17},{17,1},{2,18},{18,2},{3,19},{19,3},{4,20},{20... | collective-permute-start | bytes 3145736 | tf_op jit(solution)/shard_map/ppermute | solution.py:125
  807.0 135.1 %collective-permute-start.30 = (bf16[4,128,2048]{2,1,0:T(8,128)(2,1)S(1)}, bf16[4,128,2048]{2,1,0:T(8,128)(2,1)S(1)}, u32[]{:S(2)}, u32[]{:S(2)}) collective-permute-start(bf16[4,128,2048]{2,1,0:T(8,128)(2,1)S(1)} %bitcast_dynamic-update-slice_fusion.4), channel_id=1, source_target_pairs={{0,2},{1,3},{2,0},{3,1},{4,6},{5,7},{6,4},{7,5},{8,10},{9,11},{10,... | collective-permute-start | bytes 6291464 | tf_op jit(solution)/shard_map/ppermute | solution.py:130
  808.5 64.2 %collective-permute-start.44 = (bf16[512,1024]{1,0:T(8,128)(2,1)S(1)}, bf16[512,1024]{1,0:T(8,128)(2,1)S(1)}, u32[]{:S(2)}, u32[]{:S(2)}) collective-permute-start(bf16[512,1024]{1,0:T(8,128)(2,1)S(1)} %get-tuple-element.79), channel_id=1, source_target_pairs={{0,4},{4,0},{8,12},{12,8},{1,5},{5,1},{9,13},{13,9},{2,6},{6,2},{1... | collective-permute-start | bytes 3145736 | tf_op jit(solution)/shard_map/ppermute | solution.py:211
  850.6 44.6 %collective-permute-start.52 = (bf16[512,1024]{1,0:T(8,128)(2,1)}, bf16[512,1024]{1,0:T(8,128)(2,1)S(1)}, u32[]{:S(2)}, u32[]{:S(2)}) collective-permute-start(bf16[512,1024]{1,0:T(8,128)(2,1)} %get-tuple-element.81), channel_id=1, source_target_pairs={{0,4},{4,0},{8,12},{12,8},{1,5},{5,1},{9,13},{13,9},{2,6},{6,2},{1... | collective-permute-start | bytes 3145736 | tf_op jit(solution)/shard_map/ppermute | solution.py:211
  850.6 67.0 %collective-permute-start.60 = (bf16[512,1024]{1,0:T(8,128)(2,1)}, bf16[512,1024]{1,0:T(8,128)(2,1)S(1)}, u32[]{:S(2)}, u32[]{:S(2)}) collective-permute-start(bf16[512,1024]{1,0:T(8,128)(2,1)} %get-tuple-element.83), channel_id=1, source_target_pairs={{0,4},{4,0},{8,12},{12,8},{1,5},{5,1},{9,13},{13,9},{2,6},{6,2},{1... | collective-permute-start | bytes 3145736 | tf_op jit(solution)/shard_map/ppermute | solution.py:211
  872.7 63.5 %collective-permute-start.68 = (bf16[512,1024]{1,0:T(8,128)(2,1)}, bf16[512,1024]{1,0:T(8,128)(2,1)S(1)}, u32[]{:S(2)}, u32[]{:S(2)}) collective-permute-start(bf16[512,1024]{1,0:T(8,128)(2,1)} %get-tuple-element.85), channel_id=1, source_target_pairs={{0,4},{4,0},{8,12},{12,8},{1,5},{5,1},{9,13},{13,9},{2,6},{6,2},{1... | collective-permute-start | bytes 3145736 | tf_op jit(solution)/shard_map/ppermute | solution.py:211
  895.2 105.6 %collective-permute-start.55 = (bf16[512,1024]{1,0:T(8,128)(2,1)}, bf16[512,1024]{1,0:T(8,128)(2,1)}, u32[]{:S(2)}, u32[]{:S(2)}) collective-permute-start(bf16[512,1024]{1,0:T(8,128)(2,1)} %convolution_convert_fusion.5), channel_id=1, source_target_pairs={{0,16},{16,0},{1,17},{17,1},{2,18},{18,2},{3,19},{19,3},{4,20},{20... | collective-permute-start | bytes 3145736 | tf_op jit(solution)/shard_map/ppermute | solution.py:125
  917.6 52.1 %collective-permute-start.39 = (bf16[512,1024]{1,0:T(8,128)(2,1)}, bf16[512,1024]{1,0:T(8,128)(2,1)}, u32[]{:S(2)}, u32[]{:S(2)}) collective-permute-start(bf16[512,1024]{1,0:T(8,128)(2,1)} %convolution_convert_fusion.11), channel_id=1, source_target_pairs={{0,16},{16,0},{1,17},{17,1},{2,18},{18,2},{3,19},{19,3},{4,20},{20... | collective-permute-start | bytes 3145736 | tf_op jit(solution)/shard_map/ppermute | solution.py:125
  938.1 36.2 %collective-permute-start.69 = (bf16[512,1024]{1,0:T(8,128)(2,1)}, bf16[512,1024]{1,0:T(8,128)(2,1)}, u32[]{:S(2)}, u32[]{:S(2)}) collective-permute-start(bf16[512,1024]{1,0:T(8,128)(2,1)} %get-tuple-element.63), channel_id=1, source_target_pairs={{4,8},{8,4},{5,9},{9,5},{6,10},{10,6},{7,11},{11,7},{20,24},{24,20... | collective-permute-start | bytes 3145736 | tf_op jit(solution)/shard_map/ppermute | solution.py:216
  942.1 28.1 %collective-permute-start.45 = (bf16[512,1024]{1,0:T(8,128)(2,1)}, bf16[512,1024]{1,0:T(8,128)(2,1)}, u32[]{:S(2)}, u32[]{:S(2)}) collective-permute-start(bf16[512,1024]{1,0:T(8,128)(2,1)} %add_convert_fusion.30), channel_id=1, source_target_pairs={{4,8},{8,4},{5,9},{9,5},{6,10},{10,6},{7,11},{11,7},{20,24},{24,20... | collective-permute-start | bytes 3145736 | tf_op jit(solution)/shard_map/ppermute | solution.py:216
  965.3 35.5 %collective-permute-start.61 = (bf16[512,1024]{1,0:T(8,128)(2,1)}, bf16[512,1024]{1,0:T(8,128)(2,1)S(1)}, u32[]{:S(2)}, u32[]{:S(2)}) collective-permute-start(bf16[512,1024]{1,0:T(8,128)(2,1)} %get-tuple-element.65), channel_id=1, source_target_pairs={{4,8},{8,4},{5,9},{9,5},{6,10},{10,6},{7,11},{11,7},{20,24},{24,20... | collective-permute-start | bytes 3145736 | tf_op jit(solution)/shard_map/ppermute | solution.py:216
  969.7 45.4 %collective-permute-start.47 = (bf16[512,1024]{1,0:T(8,128)(2,1)}, bf16[512,1024]{1,0:T(8,128)(2,1)S(1)}, u32[]{:S(2)}, u32[]{:S(2)}) collective-permute-start(bf16[512,1024]{1,0:T(8,128)(2,1)} %convolution_convert_fusion.8), channel_id=1, source_target_pairs={{0,16},{16,0},{1,17},{17,1},{2,18},{18,2},{3,19},{19,3},{4,20},{20... | collective-permute-start | bytes 3145736 | tf_op jit(solution)/shard_map/ppermute | solution.py:125
  970.3 45.0 %collective-permute-start.53 = (bf16[512,1024]{1,0:T(8,128)(2,1)S(1)}, bf16[512,1024]{1,0:T(8,128)(2,1)S(1)}, u32[]{:S(2)}, u32[]{:S(2)}) collective-permute-start(bf16[512,1024]{1,0:T(8,128)(2,1)S(1)} %copy-done.28), channel_id=1, source_target_pairs={{4,8},{8,4},{5,9},{9,5},{6,10},{10,6},{7,11},{11,7},{20,24},{24,20... | collective-permute-start | bytes 3145736 | tf_op jit(solution)/shard_map/ppermute | solution.py:216
  974.3 60.0 %collective-permute-start.46 = (bf16[512,1024]{1,0:T(8,128)(2,1)S(1)}, bf16[512,1024]{1,0:T(8,128)(2,1)S(1)}, u32[]{:S(2)}, u32[]{:S(2)}) collective-permute-start(bf16[512,1024]{1,0:T(8,128)(2,1)S(1)} %get-tuple-element.93), channel_id=1, source_target_pairs={{0,4},{4,0},{8,12},{12,8},{1,5},{5,1},{9,13},{13,9},{2,6},{6,2},{1... | collective-permute-start | bytes 3145736 | tf_op jit(solution)/shard_map/ppermute | solution.py:211
  1000.8 195.3 %collective-permute-start.31 = (bf16[1024,2048]{1,0:T(8,128)(2,1)S(1)}, bf16[1024,2048]{1,0:T(8,128)(2,1)S(1)}, u32[]{:S(2)}, u32[]{:S(2)}) collective-permute-start(bf16[1024,2048]{1,0:T(8,128)(2,1)S(1)} %bitcast.114), channel_id=1, source_target_pairs={{0,1},{1,0},{2,3},{3,2},{4,5},{5,4},{6,7},{7,6},{8,9},{9,8},{10,11... | collective-permute-start | bytes 12582920 | tf_op jit(solution)/shard_map/ppermute | solution.py:130
  1000.9 86.0 %collective-permute-start.70 = (bf16[512,1024]{1,0:T(8,128)(2,1)S(1)}, bf16[512,1024]{1,0:T(8,128)(2,1)S(1)}, u32[]{:S(2)}, u32[]{:S(2)}) collective-permute-start(bf16[512,1024]{1,0:T(8,128)(2,1)S(1)} %get-tuple-element.87), channel_id=1, source_target_pairs={{0,4},{4,0},{8,12},{12,8},{1,5},{5,1},{9,13},{13,9},{2,6},{6,2},{1... | collective-permute-start | bytes 3145736 | tf_op jit(solution)/shard_map/ppermute | solution.py:211
  1015.1 70.1 %collective-permute-start.62 = (bf16[512,1024]{1,0:T(8,128)(2,1)S(1)}, bf16[512,1024]{1,0:T(8,128)(2,1)S(1)}, u32[]{:S(2)}, u32[]{:S(2)}) collective-permute-start(bf16[512,1024]{1,0:T(8,128)(2,1)S(1)} %get-tuple-element.89), channel_id=1, source_target_pairs={{0,4},{4,0},{8,12},{12,8},{1,5},{5,1},{9,13},{13,9},{2,6},{6,2},{1... | collective-permute-start | bytes 3145736 | tf_op jit(solution)/shard_map/ppermute | solution.py:211
  1016.1 67.5 %collective-permute-start.54 = (bf16[512,1024]{1,0:T(8,128)(2,1)S(1)}, bf16[512,1024]{1,0:T(8,128)(2,1)S(1)}, u32[]{:S(2)}, u32[]{:S(2)}) collective-permute-start(bf16[512,1024]{1,0:T(8,128)(2,1)S(1)} %get-tuple-element.91), channel_id=1, source_target_pairs={{0,4},{4,0},{8,12},{12,8},{1,5},{5,1},{9,13},{13,9},{2,6},{6,2},{1... | collective-permute-start | bytes 3145736 | tf_op jit(solution)/shard_map/ppermute | solution.py:211
  1034.7 55.6 %collective-permute-start.71 = (bf16[512,1024]{1,0:T(8,128)(2,1)S(1)}, bf16[512,1024]{1,0:T(8,128)(2,1)S(1)}, u32[]{:S(2)}, u32[]{:S(2)}) collective-permute-start(bf16[512,1024]{1,0:T(8,128)(2,1)S(1)} %add_convert_fusion.7), channel_id=1, source_target_pairs={{4,8},{8,4},{5,9},{9,5},{6,10},{10,6},{7,11},{11,7},{20,24},{24,20... | collective-permute-start | bytes 3145736 | tf_op jit(solution)/shard_map/ppermute | solution.py:216
  1089.4 47.6 %collective-permute-start.77 = (bf16[512,1024]{1,0:T(8,128)(2,1)S(1)}, bf16[512,1024]{1,0:T(8,128)(2,1)S(1)}, u32[]{:S(2)}, u32[]{:S(2)}) collective-permute-start(bf16[512,1024]{1,0:T(8,128)(2,1)S(1)} %get-tuple-element.68), channel_id=1, source_target_pairs={{4,8},{8,4},{5,9},{9,5},{6,10},{10,6},{7,11},{11,7},{20,24},{24,20... | collective-permute-start | bytes 3145736 | tf_op jit(solution)/shard_map/ppermute | solution.py:216
  1090.7 62.0 %collective-permute-start.72 = (bf16[512,1024]{1,0:T(8,128)(2,1)S(1)}, bf16[512,1024]{1,0:T(8,128)(2,1)S(1)}, u32[]{:S(2)}, u32[]{:S(2)}) collective-permute-start(bf16[512,1024]{1,0:T(8,128)(2,1)S(1)} %add_convert_fusion.6), channel_id=1, source_target_pairs={{0,4},{4,0},{8,12},{12,8},{1,5},{5,1},{9,13},{13,9},{2,6},{6,2},{1... | collective-permute-start | bytes 3145736 | tf_op jit(solution)/shard_map/ppermute | solution.py:211
  1099.9 242.0 %collective-permute-start.23 = (bf16[256,2048]{1,0:T(8,128)(2,1)}, bf16[256,2048]{1,0:T(8,128)(2,1)}, u32[]{:S(2)}, u32[]{:S(2)}) collective-permute-start(bf16[256,2048]{1,0:T(8,128)(2,1)} %add_convert_fusion.38), channel_id=1, source_target_pairs={{0,1},{1,0},{2,3},{3,2},{4,5},{5,4},{6,7},{7,6},{8,9},{9,8},{10,11... | collective-permute-start | bytes 3145736 | tf_op jit(solution)/shard_map/ppermute | solution.py:130
  1100.3 57.1 %collective-permute-start.74 = (bf16[512,1024]{1,0:T(8,128)(2,1)S(1)}, bf16[512,1024]{1,0:T(8,128)(2,1)S(1)}, u32[]{:S(2)}, u32[]{:S(2)}) collective-permute-start(bf16[512,1024]{1,0:T(8,128)(2,1)S(1)} %add_convert_fusion.4), channel_id=1, source_target_pairs={{0,4},{4,0},{8,12},{12,8},{1,5},{5,1},{9,13},{13,9},{2,6},{6,2},{1... | collective-permute-start | bytes 3145736 | tf_op jit(solution)/shard_map/ppermute | solution.py:211
  1137.1 39.2 %collective-permute-start.76 = (bf16[512,1024]{1,0:T(8,128)(2,1)S(1)}, bf16[512,1024]{1,0:T(8,128)(2,1)S(1)}, u32[]{:S(2)}, u32[]{:S(2)}) collective-permute-start(bf16[512,1024]{1,0:T(8,128)(2,1)S(1)} %add_convert_fusion.2), channel_id=1, source_target_pairs={{0,4},{4,0},{8,12},{12,8},{1,5},{5,1},{9,13},{13,9},{2,6},{6,2},{1... | collective-permute-start | bytes 3145736 | tf_op jit(solution)/shard_map/ppermute | solution.py:211
  1152.7 41.7 %collective-permute-start.78 = (bf16[512,1024]{1,0:T(8,128)(2,1)S(1)}, bf16[512,1024]{1,0:T(8,128)(2,1)S(1)}, u32[]{:S(2)}, u32[]{:S(2)}) collective-permute-start(bf16[512,1024]{1,0:T(8,128)(2,1)S(1)} %add_convert_fusion), channel_id=1, source_target_pairs={{0,4},{4,0},{8,12},{12,8},{1,5},{5,1},{9,13},{13,9},{2,6},{6,2},{1... | collective-permute-start | bytes 3145736 | tf_op jit(solution)/shard_map/ppermute | solution.py:211
  1244.2 43.3 %collective-permute-start.36 = (bf16[1024,512]{1,0:T(8,128)(2,1)S(1)}, bf16[1024,512]{1,0:T(8,128)(2,1)S(1)}, u32[]{:S(2)}, u32[]{:S(2)}) collective-permute-start(bf16[1024,512]{1,0:T(8,128)(2,1)S(1)} %convolution_convert_fusion.13), channel_id=1, source_target_pairs={{0,16},{16,0},{1,17},{17,1},{2,18},{18,2},{3,19},{19,3},{4,20},{20... | collective-permute-start | bytes 3145736 | tf_op jit(solution)/shard_map/ppermute | solution.py:125
  1251.0 84.8 %collective-permute-start.37 = (bf16[1024,512]{1,0:T(8,128)(2,1)S(1)}, bf16[1024,512]{1,0:T(8,128)(2,1)S(1)}, u32[]{:S(2)}, u32[]{:S(2)}) collective-permute-start(bf16[1024,512]{1,0:T(8,128)(2,1)S(1)} %convolution_convert_fusion.12), channel_id=1, source_target_pairs={{0,16},{16,0},{1,17},{17,1},{2,18},{18,2},{3,19},{19,3},{4,20},{20... | collective-permute-start | bytes 3145736 | tf_op jit(solution)/shard_map/ppermute | solution.py:125
  1253.6 78.3 %collective-permute-start.38 = (bf16[512,1024]{1,0:T(8,128)(2,1)S(1)}, bf16[512,1024]{1,0:T(8,128)(2,1)S(1)}, u32[]{:S(2)}, u32[]{:S(2)}) collective-permute-start(bf16[512,1024]{1,0:T(8,128)(2,1)S(1)} %fusion.38), channel_id=1, source_target_pairs={{0,16},{16,0},{1,17},{17,1},{2,18},{18,2},{3,19},{19,3},{4,20},{20... | collective-permute-start | bytes 3145736 | tf_op jit(solution)/shard_map/ppermute | solution.py:125
  1265.0 28.4 %collective-permute-start.33 = (bf16[256,2048]{1,0:T(8,128)(2,1)S(1)}, bf16[256,2048]{1,0:T(8,128)(2,1)S(1)}, u32[]{:S(2)}, u32[]{:S(2)}) collective-permute-start(bf16[256,2048]{1,0:T(8,128)(2,1)S(1)} %fusion.26), channel_id=1, source_target_pairs={{0,2},{1,3},{2,0},{3,1},{4,6},{5,7},{6,4},{7,5},{8,10},{9,11},{10,... | collective-permute-start | bytes 3145736 | tf_op jit(solution)/shard_map/ppermute | solution.py:130
  1293.8 48.0 %collective-permute-start.34 = (bf16[256,2048]{1,0:T(8,128)(2,1)S(1)}, bf16[256,2048]{1,0:T(8,128)(2,1)S(1)}, u32[]{:S(2)}, u32[]{:S(2)}) collective-permute-start(bf16[256,2048]{1,0:T(8,128)(2,1)S(1)} %add_convert_fusion.36), channel_id=1, source_target_pairs={{0,1},{1,0},{2,3},{3,2},{4,5},{5,4},{6,7},{7,6},{8,9},{9,8},{10,11... | collective-permute-start | bytes 3145736 | tf_op jit(solution)/shard_map/ppermute | solution.py:130
  (87 other events, 1959.0 us)
